TPU v7x, 32 devices: a whole 2x2x4 slice. The times are simulated.
32 devices in a mesh: groups: 2 (over y), expert: 4 (over z), section: 4 (over x, core).
Axes of the slice: x: 2, y: 2, z: 4, core: 2. Of those that a mesh axis runs over, the one named last changes fastest.
Arguments:
- layer_inputs: bfloat16 [4, 2, 512, 1024], P('section', None, ('groups', 'expert')), parts along dimension 2, may hold values from -6 to 6
- out_cotangent: bfloat16 [2, 512, 1024], P(None, ('groups', 'expert')), parts along dimension 1, may hold values from -0.59765625 to 0.59765625
- expert_routes: int32 [4, 2, 512, 2], P('section', None, 'groups'), parts along dimension 2, may hold values from 0 to 3, all different within a row; in each aligned block of 64 rows (0 to 63, 64 to 127, ..., all dimensions but the last counted through in order) at most 40 rows name the same one
- norm_gain: float32 [4, 1024], P('section'), may hold values from 0.5 to 1.5
- router_weight: float32 [4, 4, 1024], P('section'), may hold values from -0.1875 to 0.1875
- up_weight: bfloat16 [4, 1024, 16384], P('section', None, 'expert'), may hold values from -0.1875 to 0.1875
- down_weight: bfloat16 [4, 16384, 1024], P('section', 'expert'), may hold values from -0.09375 to 0.09375
Outputs:
- up_grad: bfloat16 [4, 2048, 16384], P('section', 'groups', 'expert'), parts along dimension 1
- down_grad: bfloat16 [4, 16384, 2048], P('section', 'expert', 'groups'), parts along dimension 2
- router_grad: float32 [4, 8, 1024], P('section', 'groups'), parts along dimension 1
- gain_grad: float32 [4, 2048], P('section', 'groups'), parts along dimension 1
There are 2 independent parts, one for each index of `groups`. A program takes and returns all parts, laid end to end along the dimension named above; an argument that names none is the same for every part. Nothing has to cross between parts.
Inputs may be any that keep to these rules, and one draw needn't show every extreme that they name: `expert_routes`: in every aligned block of 64 tokens (the tokens of one index of expert, for one sublayer and micro-batch), each expert is listed by at most 40 tokens; the two experts of a token differ.
All inputs are finite; a program needn't handle non-finite values.
Results may differ from a plain program's by a relative error of at most 0.025.
Values may be sent and summed in bfloat16 or wider, within the bound.
No kernel may reach another device: no remote copies, remote signals or barrier semaphores. Data moves between devices by JAX's collectives and lax.ppermute only.
A program may use at most 192 MiB of HBM per device.

v0:
```python
import jax
import jax.numpy as jnp
from jax import lax
from jax.sharding import PartitionSpec as P

norm_eps = 1e-06
gelu_coef = 0.7978845608028654
cubic_coef = 0.044715
highest = lax.Precision.HIGHEST


def passed_along(value, axis, steps):
    count = lax.axis_size(axis)
    initial, last = (max(0, -steps), min(count, count - steps))
    return lax.ppermute(value, axis, [(source, source + steps) for source in range(initial, last)])


def gelu_parts(pre_act):
    inner_arg = gelu_coef * (pre_act + cubic_coef * pre_act * pre_act * pre_act)
    tanh_val = jnp.tanh(inner_arg)
    values = 0.5 * pre_act * (1.0 + tanh_val)
    slopes = 0.5 * (1.0 + tanh_val) + 0.5 * pre_act * (1.0 - tanh_val * tanh_val) * gelu_coef * (
        1.0 + 3.0 * cubic_coef * pre_act * pre_act
    )
    return (values, slopes)


def norm_rows(row_vals, gain_vec):
    values = row_vals.astype(jnp.float32)
    mean_sq = jnp.mean(values * values, axis=-1, keepdims=True)
    inverse = lax.rsqrt(mean_sq + norm_eps)
    normed = values * inverse
    return ((normed * gain_vec).astype(jnp.bfloat16), normed, inverse)


def route_weights(normed_low, router, chosen):
    logits = jnp.einsum("...d,ed->...e", normed_low.astype(jnp.float32), router, precision=highest)
    scores = jax.nn.sigmoid(logits)
    expert_ids = lax.broadcasted_iota(jnp.int32, scores.shape, scores.ndim - 1)
    first_hot = (chosen[..., 0:1] == expert_ids).astype(jnp.float32)
    second_hot = (chosen[..., 1:2] == expert_ids).astype(jnp.float32)
    totals = jnp.sum(scores * (first_hot + second_hot), axis=-1, keepdims=True)
    weights = scores * (first_hot + second_hot) / totals
    return (scores, first_hot, second_hot, totals, weights)


def owner_back(
    grad_in, expert_grad, combine_grad, route_parts, normed_low, normed, inverse, gain_vec, router
):
    scores, first_hot, second_hot, totals, weights = route_parts
    first_grad = jnp.sum(combine_grad * first_hot, axis=-1, keepdims=True)
    second_grad = jnp.sum(combine_grad * second_hot, axis=-1, keepdims=True)
    first_wt = jnp.sum(weights * first_hot, axis=-1, keepdims=True)
    second_wt = jnp.sum(weights * second_hot, axis=-1, keepdims=True)
    mean_grad = first_wt * first_grad + second_wt * second_grad
    sig_slope = scores * (1.0 - scores)
    logit_grad = (
        (first_hot * (first_grad - mean_grad) + second_hot * (second_grad - mean_grad))
        / totals
        * sig_slope
    )
    full_grad = expert_grad + jnp.dot(logit_grad, router, precision=highest)
    scaled_grad = full_grad * gain_vec
    center = jnp.mean(scaled_grad * normed, axis=-1, keepdims=True)
    input_grad = (grad_in.astype(jnp.float32) + inverse * (scaled_grad - normed * center)).astype(
        jnp.bfloat16
    )
    router_term = jnp.dot(logit_grad.T, normed_low.astype(jnp.float32), precision=highest)
    gain_term = jnp.sum(full_grad * normed, axis=0)
    return (input_grad, router_term, gain_term)


def expert_terms(normed_low, cot_rows, weight_col, hit_col, up_local, down_local):
    pre_act = jnp.dot(normed_low, up_local, preferred_element_type=jnp.float32)
    act_vals, slopes = gelu_parts(pre_act)
    act_low = act_vals.astype(jnp.bfloat16)
    back_hidden = lax.dot_general(
        cot_rows, down_local, (((1,), (1,)), ((), ())), preferred_element_type=jnp.float32
    )
    combine_col = jnp.sum(act_low.astype(jnp.float32) * back_hidden, axis=-1) * hit_col
    hidden_grad = (weight_col[:, None] * back_hidden * slopes).astype(jnp.bfloat16)
    expert_grad = lax.dot_general(
        hidden_grad, up_local, (((1,), (1,)), ((), ())), preferred_element_type=jnp.float32
    )
    return (expert_grad, combine_col, act_low, hidden_grad)


def weight_terms(normed_low, cot_rows, weight_col, act_low, hidden_grad):
    scaled = (weight_col[:, None] * cot_rows.astype(jnp.float32)).astype(jnp.bfloat16)
    up_term = lax.dot_general(
        normed_low, hidden_grad, (((0,), (0,)), ((), ())), preferred_element_type=jnp.float32
    )
    down_term = lax.dot_general(
        act_low, scaled, (((0,), (0,)), ((), ())), preferred_element_type=jnp.float32
    )
    return (up_term, down_term)


def body(
    layer_inputs, out_cotangent, expert_routes, norm_gain, router_weight, up_weight, down_weight
):
    sections = lax.axis_size("section")
    section_id = lax.axis_index("section")
    shards = lax.axis_size("expert")
    shard_id = lax.axis_index("expert")
    inputs = layer_inputs[0]
    micro_count, row_count, feat_dim = inputs.shape
    chosen_all = expert_routes[0]
    gain_vec = norm_gain[0]
    router = router_weight[0]
    up_local = up_weight[0]
    down_local = down_weight[0]
    experts = router.shape[0]
    hidden_len = up_local.shape[1]
    slices = shards // experts
    my_expert = shard_id // slices
    expert_hot = (lax.broadcasted_iota(jnp.int32, (experts,), 0) == my_expert).astype(jnp.float32)
    normed_own, values_own, inverse_own = norm_rows(inputs, gain_vec)
    chosen_own = lax.dynamic_slice_in_dim(chosen_all, shard_id * row_count, row_count, 1)
    route_own = route_weights(normed_own, router, chosen_own)
    normed_all = lax.all_gather(normed_own, "expert", axis=1, tiled=True)
    route_all = route_weights(normed_all, router, chosen_all)
    picked_weight = jnp.sum(route_all[4] * expert_hot, axis=-1)
    picked_hit = jnp.sum((route_all[1] + route_all[2]) * expert_hot, axis=-1)
    picked_count = normed_all.shape[1]
    last_section = sections - 1

    def local_all(operands):
        rows_now, cot_rows, weight_col, hit_col = operands
        expert_grad, combine_col, act_low, hidden_grad = expert_terms(
            rows_now, cot_rows, weight_col, hit_col, up_local, down_local
        )
        up_term, down_term = weight_terms(rows_now, cot_rows, weight_col, act_low, hidden_grad)
        return (expert_grad, combine_col, up_term, down_term)

    def local_none(operands):
        return (
            jnp.zeros((picked_count, feat_dim), jnp.float32),
            jnp.zeros((picked_count,), jnp.float32),
            jnp.zeros((feat_dim, hidden_len), jnp.float32),
            jnp.zeros((hidden_len, feat_dim), jnp.float32),
        )

    def step_fn(step_no, loop_state):
        incoming, acc_up, acc_down, acc_router, acc_gain = loop_state
        micro_no = step_no - (last_section - section_id)
        active = jnp.logical_and(micro_no >= 0, micro_no < micro_count)
        micro_id = jnp.clip(micro_no, 0, micro_count - 1)
        own_cot = lax.dynamic_index_in_dim(out_cotangent, micro_id, 0, keepdims=False)
        grad_in = jnp.where(section_id == last_section, own_cot, incoming)
        rows_now = lax.dynamic_index_in_dim(normed_all, micro_id, 0, keepdims=False)
        weight_col = lax.dynamic_index_in_dim(picked_weight, micro_id, 0, keepdims=False)
        hit_col = lax.dynamic_index_in_dim(picked_hit, micro_id, 0, keepdims=False)
        cot_rows = lax.all_gather(grad_in, "expert", axis=0, tiled=True)
        expert_grad, combine_col, up_term, down_term = lax.cond(
            active, local_all, local_none, (rows_now, cot_rows, weight_col, hit_col)
        )
        summed_grad, summed_comb = (
            lax.psum_scatter(
                expert_grad.astype(jnp.bfloat16), "expert", scatter_dimension=0, tiled=True
            ).astype(jnp.float32),
            lax.psum_scatter(
                (combine_col[:, None] * expert_hot[None, :]).astype(jnp.bfloat16),
                "expert",
                scatter_dimension=0,
                tiled=True,
            ).astype(jnp.float32),
        )
        route_now = jax.tree.map(
            lambda part_arr: lax.dynamic_index_in_dim(part_arr, micro_id, 0, keepdims=False),
            route_own,
        )
        normed_now = lax.dynamic_index_in_dim(normed_own, micro_id, 0, keepdims=False)
        values_now = lax.dynamic_index_in_dim(values_own, micro_id, 0, keepdims=False)
        inverse_now = lax.dynamic_index_in_dim(inverse_own, micro_id, 0, keepdims=False)
        input_grad, router_term, gain_term = owner_back(
            grad_in,
            summed_grad,
            summed_comb,
            route_now,
            normed_now,
            values_now,
            inverse_now,
            gain_vec,
            router,
        )
        next_in = passed_along(input_grad, "section", -1)
        acc_up = acc_up + up_term
        acc_down = acc_down + down_term
        acc_router = acc_router + jnp.where(active, router_term, 0.0)
        acc_gain = acc_gain + jnp.where(active, gain_term, 0.0)
        return (next_in, acc_up, acc_down, acc_router, acc_gain)

    init_state = (
        jnp.zeros((row_count, feat_dim), jnp.bfloat16),
        jnp.zeros((feat_dim, hidden_len), jnp.float32),
        jnp.zeros((hidden_len, feat_dim), jnp.float32),
        jnp.zeros((experts, feat_dim), jnp.float32),
        jnp.zeros((feat_dim,), jnp.float32),
    )
    final_state = lax.fori_loop(0, sections + micro_count - 1, step_fn, init_state)
    router_sum, gain_sum = lax.psum((final_state[3], final_state[4]), "expert")
    return (
        final_state[1].astype(jnp.bfloat16)[None],
        final_state[2].astype(jnp.bfloat16)[None],
        router_sum[None],
        gain_sum[None],
    )


def solution(mesh):
    in_specs = (
        P("section", None, ("groups", "expert"), None),
        P(None, ("groups", "expert"), None),
        P("section", None, "groups", None),
        P("section", None),
        P("section", None, None),
        P("section", None, "expert"),
        P("section", "expert", None),
    )
    out_specs = (
        P("section", "groups", "expert"),
        P("section", "expert", "groups"),
        P("section", "groups", None),
        P("section", "groups"),
    )
    return jax.shard_map(body, mesh=mesh, in_specs=in_specs, out_specs=out_specs, check_vma=False)
```

profile of v0, /device:TPU:0, one launch (start us, length us, event | category | flops | bytes accessed | tf_op | source)
XLA Modules:
  0.0 550.2 jit_solution(5353691147404148820)
XLA Ops:
  8.3 1.8 fusion.64
  11.8 1.5 fusion.77
  13.9 27.1 %all-gather.2.cloned.1.call-done = bf16[2,256,1024]{2,1,0:T(8,128)(2,1)} async-done(((bf16[2,64,1024]{2,1,0:T(8,128)(2,1)}), bf16[2,256,1024]{2,1,0:T(8,128)(2,1)}) %all-gather.2.cloned.1.call-update) | async-done | bytes 1048592 | tf_op jit(solution)/shard_map/all_gather | solution.py:121
  41.0 2.2 fusion.60
  43.3 466.4 %while.24 = (s32[]{:T(128)}, bf16[64,1024]{1,0:T(8,128)(2,1)S(1)}, f32[1024,4096]{1,0:T(8,128)}, f32[4096,1024]{1,0:T(8,128)}, f32[4,1024]{1,0:T(4,128)S(1)}, /*...) while((s32[]{:T(128)}, bf16[64,1024]{1,0:T(8,128)(2,1)S(1)}, ...), condition=%wide.region_17.18_spmd.clone, body=%wide.region_5.17_spmd.clone.sunk | while | flops 10797930496 | bytes 252352112 | solution.py:201
  44.3 15.3 %all_gather.15 = bf16[256,1024]{1,0:T(8,128)(2,1)S(1)} all-gather(bf16[64,1024]{1,0:T(8,128)(2,1)S(1)} %bitcast_select_fusion.2), channel_id=1, replica_groups=mesh['groups'=2,'expert'=4,'section'=4] {'expert'}, dimensions={0}, use_global_device_ids=true | all-gather | bytes 655360 | tf_op jit(solution)/shard_map/while/body/eval_jaxpr/all_gather | solution.py:154
  59.6 15.7 %conditional.3 = (bf16[256,1024]{1,0:T(8,128)(2,1)S(1)}, f32[256]{0:T(256)S(1)}, f32[1024,4096]{1,0:T(8,128)}, f32[4096,1024]{1,0:T(8,128)}) conditional(s32[]{:T(128)} %convert_element_type.245, () %tuple.86, (f32[2,256]{1,0:T(2,128)S(1)}, s32[]{:T(128)}, bf16[256,1024]{1,0:T(8,128)(2,1)S(1)}, bf16[4096,1024]{1,0:T(8,128)(2,1)}, ...), branch_computations={%region_6.6_spmd, %region_7.8_spmd} | conditional | flops 10773856256 | bytes 143141520 | solution.py:155
  59.6 7.8 %broadcast.122 = f32[1024,4096]{1,0:T(8,128)} broadcast(f32[]{:T(128)} %constant.155.clone), dimensions={} | broadcast | bytes 16777220 | tf_op jit(solution)/shard_map/broadcast.11
  67.4 7.8 %broadcast.123 = f32[4096,1024]{1,0:T(8,128)} broadcast(f32[]{:T(128)} %constant.155.clone), dimensions={} | broadcast | bytes 16777220 | tf_op jit(solution)/shard_map/broadcast.10
  76.9 12.2 %select_add_fusion.6 = f32[1024,4096]{1,0:T(8,128)} fusion(f32[1024,4096]{1,0:T(8,128)} %get-tuple-element.1030, f32[1024,4096]{1,0:T(8,128)} %get-tuple-element.1071, pred[]{:T(512)S(6)} %compare.4), kind=kLoop, calls=%fused_computation.26.clone.1 | loop fusion | flops 8388608 | bytes 50331648 | tf_op jit(solution)/shard_map/while/body/eval_jaxpr/add | solution.py:188
  89.1 13.6 %select_add_fusion.7 = f32[4096,1024]{1,0:T(8,128)} fusion(f32[4096,1024]{1,0:T(8,128)} %get-tuple-element.1031, f32[4096,1024]{1,0:T(8,128)} %get-tuple-element.1072, pred[]{:T(512)S(6)} %compare.4), kind=kLoop, calls=%fused_computation.25.clone.1 | loop fusion | flops 8388608 | bytes 50331648 | tf_op jit(solution)/shard_map/while/body/eval_jaxpr/add | solution.py:189
  102.7 4.1 reduce-scatter.7.cloned.1.call-done
  107.9 21.8 %reduce-scatter.9.cloned.1.call-done = bf16[64,1024]{1,0:T(8,128)(2,1)} async-done(((bf16[256,1024]{1,0:T(8,128)(2,1)}), bf16[64,1024]{1,0:T(8,128)(2,1)}) %reduce-scatter.9.cloned.1.call-update) | async-done | bytes 131088 | tf_op jit(solution)/shard_map/while/body/eval_jaxpr/reduce_scatter | solution.py:159
  129.7 1.5 fusion.106
  131.4 1.3 collective-permute-start
  132.7 1.9 collective-permute-done
  135.5 15.2 %all_gather.15 = bf16[256,1024]{1,0:T(8,128)(2,1)S(1)} all-gather(bf16[64,1024]{1,0:T(8,128)(2,1)S(1)} %bitcast_select_fusion.2), channel_id=1, replica_groups=mesh['groups'=2,'expert'=4,'section'=4] {'expert'}, dimensions={0}, use_global_device_ids=true | all-gather | bytes 655360 | tf_op jit(solution)/shard_map/while/body/eval_jaxpr/all_gather | solution.py:154
  150.8 15.7 %conditional.3 = (bf16[256,1024]{1,0:T(8,128)(2,1)S(1)}, f32[256]{0:T(256)S(1)}, f32[1024,4096]{1,0:T(8,128)}, f32[4096,1024]{1,0:T(8,128)}) conditional(s32[]{:T(128)} %convert_element_type.245, () %tuple.86, (f32[2,256]{1,0:T(2,128)S(1)}, s32[]{:T(128)}, bf16[256,1024]{1,0:T(8,128)(2,1)S(1)}, bf16[4096,1024]{1,0:T(8,128)(2,1)}, ...), branch_computations={%region_6.6_spmd, %region_7.8_spmd} | conditional | flops 10773856256 | bytes 143141520 | solution.py:155
  150.8 7.8 %broadcast.122 = f32[1024,4096]{1,0:T(8,128)} broadcast(f32[]{:T(128)} %constant.155.clone), dimensions={} | broadcast | bytes 16777220 | tf_op jit(solution)/shard_map/broadcast.11
  158.6 7.8 %broadcast.123 = f32[4096,1024]{1,0:T(8,128)} broadcast(f32[]{:T(128)} %constant.155.clone), dimensions={} | broadcast | bytes 16777220 | tf_op jit(solution)/shard_map/broadcast.10
  167.9 17.8 %select_add_fusion.6 = f32[1024,4096]{1,0:T(8,128)} fusion(f32[1024,4096]{1,0:T(8,128)} %get-tuple-element.1030, f32[1024,4096]{1,0:T(8,128)} %get-tuple-element.1071, pred[]{:T(512)S(6)} %compare.4), kind=kLoop, calls=%fused_computation.26.clone.1 | loop fusion | flops 8388608 | bytes 50331648 | tf_op jit(solution)/shard_map/while/body/eval_jaxpr/add | solution.py:188
  185.8 17.3 %select_add_fusion.7 = f32[4096,1024]{1,0:T(8,128)} fusion(f32[4096,1024]{1,0:T(8,128)} %get-tuple-element.1031, f32[4096,1024]{1,0:T(8,128)} %get-tuple-element.1072, pred[]{:T(512)S(6)} %compare.4), kind=kLoop, calls=%fused_computation.25.clone.1 | loop fusion | flops 8388608 | bytes 50331648 | tf_op jit(solution)/shard_map/while/body/eval_jaxpr/add | solution.py:189
  204.1 20.0 %reduce-scatter.9.cloned.1.call-done = bf16[64,1024]{1,0:T(8,128)(2,1)} async-done(((bf16[256,1024]{1,0:T(8,128)(2,1)}), bf16[64,1024]{1,0:T(8,128)(2,1)}) %reduce-scatter.9.cloned.1.call-update) | async-done | bytes 131088 | tf_op jit(solution)/shard_map/while/body/eval_jaxpr/reduce_scatter | solution.py:159
  224.2 1.5 fusion.106
  225.8 1.3 collective-permute-start
  227.1 1.9 collective-permute-done
  230.0 15.2 %all_gather.15 = bf16[256,1024]{1,0:T(8,128)(2,1)S(1)} all-gather(bf16[64,1024]{1,0:T(8,128)(2,1)S(1)} %bitcast_select_fusion.2), channel_id=1, replica_groups=mesh['groups'=2,'expert'=4,'section'=4] {'expert'}, dimensions={0}, use_global_device_ids=true | all-gather | bytes 655360 | tf_op jit(solution)/shard_map/while/body/eval_jaxpr/all_gather | solution.py:154
  245.2 15.7 %conditional.3 = (bf16[256,1024]{1,0:T(8,128)(2,1)S(1)}, f32[256]{0:T(256)S(1)}, f32[1024,4096]{1,0:T(8,128)}, f32[4096,1024]{1,0:T(8,128)}) conditional(s32[]{:T(128)} %convert_element_type.245, () %tuple.86, (f32[2,256]{1,0:T(2,128)S(1)}, s32[]{:T(128)}, bf16[256,1024]{1,0:T(8,128)(2,1)S(1)}, bf16[4096,1024]{1,0:T(8,128)(2,1)}, ...), branch_computations={%region_6.6_spmd, %region_7.8_spmd} | conditional | flops 10773856256 | bytes 143141520 | solution.py:155
  245.2 7.8 %broadcast.122 = f32[1024,4096]{1,0:T(8,128)} broadcast(f32[]{:T(128)} %constant.155.clone), dimensions={} | broadcast | bytes 16777220 | tf_op jit(solution)/shard_map/broadcast.11
  253.0 7.8 %broadcast.123 = f32[4096,1024]{1,0:T(8,128)} broadcast(f32[]{:T(128)} %constant.155.clone), dimensions={} | broadcast | bytes 16777220 | tf_op jit(solution)/shard_map/broadcast.10
  262.5 17.8 %select_add_fusion.6 = f32[1024,4096]{1,0:T(8,128)} fusion(f32[1024,4096]{1,0:T(8,128)} %get-tuple-element.1030, f32[1024,4096]{1,0:T(8,128)} %get-tuple-element.1071, pred[]{:T(512)S(6)} %compare.4), kind=kLoop, calls=%fused_computation.26.clone.1 | loop fusion | flops 8388608 | bytes 50331648 | tf_op jit(solution)/shard_map/while/body/eval_jaxpr/add | solution.py:188
  280.3 17.3 %select_add_fusion.7 = f32[4096,1024]{1,0:T(8,128)} fusion(f32[4096,1024]{1,0:T(8,128)} %get-tuple-element.1031, f32[4096,1024]{1,0:T(8,128)} %get-tuple-element.1072, pred[]{:T(512)S(6)} %compare.4), kind=kLoop, calls=%fused_computation.25.clone.1 | loop fusion | flops 8388608 | bytes 50331648 | tf_op jit(solution)/shard_map/while/body/eval_jaxpr/add | solution.py:189
  298.7 20.0 %reduce-scatter.9.cloned.1.call-done = bf16[64,1024]{1,0:T(8,128)(2,1)} async-done(((bf16[256,1024]{1,0:T(8,128)(2,1)}), bf16[64,1024]{1,0:T(8,128)(2,1)}) %reduce-scatter.9.cloned.1.call-update) | async-done | bytes 131088 | tf_op jit(solution)/shard_map/while/body/eval_jaxpr/reduce_scatter | solution.py:159
  318.7 1.5 fusion.106
  320.3 1.3 collective-permute-start
  321.6 1.9 collective-permute-done
  324.5 15.2 %all_gather.15 = bf16[256,1024]{1,0:T(8,128)(2,1)S(1)} all-gather(bf16[64,1024]{1,0:T(8,128)(2,1)S(1)} %bitcast_select_fusion.2), channel_id=1, replica_groups=mesh['groups'=2,'expert'=4,'section'=4] {'expert'}, dimensions={0}, use_global_device_ids=true | all-gather | bytes 655360 | tf_op jit(solution)/shard_map/while/body/eval_jaxpr/all_gather | solution.py:154
  339.7 30.6 %conditional.3 = (bf16[256,1024]{1,0:T(8,128)(2,1)S(1)}, f32[256]{0:T(256)S(1)}, f32[1024,4096]{1,0:T(8,128)}, f32[4096,1024]{1,0:T(8,128)}) conditional(s32[]{:T(128)} %convert_element_type.245, () %tuple.86, (f32[2,256]{1,0:T(2,128)S(1)}, s32[]{:T(128)}, bf16[256,1024]{1,0:T(8,128)(2,1)S(1)}, bf16[4096,1024]{1,0:T(8,128)(2,1)}, ...), branch_computations={%region_6.6_spmd, %region_7.8_spmd} | conditional | flops 10773856256 | bytes 143141520 | solution.py:155
  339.7 6.0 %fusion.12 = f32[256,4096]{1,0:T(8,128)S(1)} fusion(bf16[1024,4096]{1,0:T(8,128)(2,1)} %get-tuple-element.569, bf16[2,256,1024]{2,1,0:T(8,128)(2,1)} %get-tuple-element.568, s32[]{:T(128)} %get-tuple-element.565), kind=kOutput, calls=%fused_computation.16 | convolution fusion | flops 2147483648 | bytes 13107712 | tf_op jit(solution)/shard_map/while/body/eval_jaxpr/cond/branch_1_fun/dot_general | solution.py:74
  345.8 5.4 multiply_reduce_fusion
  351.2 8.1 %fusion.10 = f32[1024,4096]{1,0:T(8,128)} fusion(bf16[256,4096]{1,0:T(8,128)(2,1)S(1)} %get-tuple-element.832, bf16[2,256,1024]{2,1,0:T(8,128)(2,1)S(1)} %copy-done.2, s32[]{:T(128)} %get-tuple-element.565), kind=kOutput, calls=%fused_computation.14 | convolution fusion | flops 2147483648 | bytes 19398660 | tf_op jit(solution)/shard_map/while/body/eval_jaxpr/cond/branch_1_fun/dot_general | solution.py:90
  359.4 2.4 fusion.81
  361.7 8.6 %fusion.9 = f32[4096,1024]{1,0:T(8,128)} fusion(bf16[256,1024]{1,0:T(8,128)(2,1)S(1)} %get-tuple-element.566, f32[256]{0:T(256)S(1)} %bitcast.165, f32[256,4096]{1,0:T(8,128)S(1)} %fusion.12), kind=kOutput, calls=%fused_computation.13 | convolution fusion | flops 2157707264 | bytes 21496832 | tf_op jit(solution)/shard_map/while/body/eval_jaxpr/cond/branch_1_fun/dot_general | solution.py:93
  372.0 18.0 %select_add_fusion.6 = f32[1024,4096]{1,0:T(8,128)} fusion(f32[1024,4096]{1,0:T(8,128)} %get-tuple-element.1030, f32[1024,4096]{1,0:T(8,128)} %get-tuple-element.1071, pred[]{:T(512)S(6)} %compare.4), kind=kLoop, calls=%fused_computation.26.clone.1 | loop fusion | flops 8388608 | bytes 50331648 | tf_op jit(solution)/shard_map/while/body/eval_jaxpr/add | solution.py:188
  390.0 17.3 %select_add_fusion.7 = f32[4096,1024]{1,0:T(8,128)} fusion(f32[4096,1024]{1,0:T(8,128)} %get-tuple-element.1031, f32[4096,1024]{1,0:T(8,128)} %get-tuple-element.1072, pred[]{:T(512)S(6)} %compare.4), kind=kLoop, calls=%fused_computation.25.clone.1 | loop fusion | flops 8388608 | bytes 50331648 | tf_op jit(solution)/shard_map/while/body/eval_jaxpr/add | solution.py:189
  408.4 3.4 reduce-scatter.9.cloned.1.call-done
  411.8 1.5 fusion.106
  414.7 1.9 collective-permute-done
  417.6 15.2 %all_gather.15 = bf16[256,1024]{1,0:T(8,128)(2,1)S(1)} all-gather(bf16[64,1024]{1,0:T(8,128)(2,1)S(1)} %bitcast_select_fusion.2), channel_id=1, replica_groups=mesh['groups'=2,'expert'=4,'section'=4] {'expert'}, dimensions={0}, use_global_device_ids=true | all-gather | bytes 655360 | tf_op jit(solution)/shard_map/while/body/eval_jaxpr/all_gather | solution.py:154
  432.8 30.6 %conditional.3 = (bf16[256,1024]{1,0:T(8,128)(2,1)S(1)}, f32[256]{0:T(256)S(1)}, f32[1024,4096]{1,0:T(8,128)}, f32[4096,1024]{1,0:T(8,128)}) conditional(s32[]{:T(128)} %convert_element_type.245, () %tuple.86, (f32[2,256]{1,0:T(2,128)S(1)}, s32[]{:T(128)}, bf16[256,1024]{1,0:T(8,128)(2,1)S(1)}, bf16[4096,1024]{1,0:T(8,128)(2,1)}, ...), branch_computations={%region_6.6_spmd, %region_7.8_spmd} | conditional | flops 10773856256 | bytes 143141520 | solution.py:155
  432.8 6.0 %fusion.12 = f32[256,4096]{1,0:T(8,128)S(1)} fusion(bf16[1024,4096]{1,0:T(8,128)(2,1)} %get-tuple-element.569, bf16[2,256,1024]{2,1,0:T(8,128)(2,1)} %get-tuple-element.568, s32[]{:T(128)} %get-tuple-element.565), kind=kOutput, calls=%fused_computation.16 | convolution fusion | flops 2147483648 | bytes 13107712 | tf_op jit(solution)/shard_map/while/body/eval_jaxpr/cond/branch_1_fun/dot_general | solution.py:74
  438.9 5.4 multiply_reduce_fusion
  444.3 8.1 %fusion.10 = f32[1024,4096]{1,0:T(8,128)} fusion(bf16[256,4096]{1,0:T(8,128)(2,1)S(1)} %get-tuple-element.832, bf16[2,256,1024]{2,1,0:T(8,128)(2,1)S(1)} %copy-done.2, s32[]{:T(128)} %get-tuple-element.565), kind=kOutput, calls=%fused_computation.14 | convolution fusion | flops 2147483648 | bytes 19398660 | tf_op jit(solution)/shard_map/while/body/eval_jaxpr/cond/branch_1_fun/dot_general | solution.py:90
  452.4 2.4 fusion.81
  454.8 8.6 %fusion.9 = f32[4096,1024]{1,0:T(8,128)} fusion(bf16[256,1024]{1,0:T(8,128)(2,1)S(1)} %get-tuple-element.566, f32[256]{0:T(256)S(1)} %bitcast.165, f32[256,4096]{1,0:T(8,128)S(1)} %fusion.12), kind=kOutput, calls=%fused_computation.13 | convolution fusion | flops 2157707264 | bytes 21496832 | tf_op jit(solution)/shard_map/while/body/eval_jaxpr/cond/branch_1_fun/dot_general | solution.py:93
  465.0 17.9 %select_add_fusion.6 = f32[1024,4096]{1,0:T(8,128)} fusion(f32[1024,4096]{1,0:T(8,128)} %get-tuple-element.1030, f32[1024,4096]{1,0:T(8,128)} %get-tuple-element.1071, pred[]{:T(512)S(6)} %compare.4), kind=kLoop, calls=%fused_computation.26.clone.1 | loop fusion | flops 8388608 | bytes 50331648 | tf_op jit(solution)/shard_map/while/body/eval_jaxpr/add | solution.py:188
  482.9 17.2 %select_add_fusion.7 = f32[4096,1024]{1,0:T(8,128)} fusion(f32[4096,1024]{1,0:T(8,128)} %get-tuple-element.1031, f32[4096,1024]{1,0:T(8,128)} %get-tuple-element.1072, pred[]{:T(512)S(6)} %compare.4), kind=kLoop, calls=%fused_computation.25.clone.1 | loop fusion | flops 8388608 | bytes 50331648 | tf_op jit(solution)/shard_map/while/body/eval_jaxpr/add | solution.py:189
  501.3 3.5 reduce-scatter.9.cloned.1.call-done
  504.8 1.5 fusion.106
  507.7 1.9 collective-permute-done
  509.7 9.2 %convert_bitcast_fusion = bf16[1,4096,1024]{2,1,0:T(8,128)(2,1)} fusion(f32[4096,1024]{1,0:T(8,128)} %get-tuple-element.610), kind=kLoop, calls=%fused_computation.89 | loop fusion | flops 4194304 | bytes 25165824 | tf_op jit(solution)/shard_map/broadcast_in_dim | solution.py:205
  518.9 4.4 copy-done
  523.3 3.9 convert_bitcast_fusion.1
  527.2 16.5 %all-reduce = (f32[1,4,1024]{2,1,0:T(4,128)}, f32[1,1024]{1,0:T(1,128)}) all-reduce(f32[1,4,1024]{2,1,0:T(4,128)S(1)} %bitcast.158, f32[1,1024]{1,0:T(1,128)S(1)} %bitcast.163), channel_id=1, replica_groups=mesh['groups'=2,'expert'=4,'section'=4] {'expert'}, use_global_device_ids=true, to_apply=%region_18.19 | all-reduce | flops 5120 | bytes 40960 | tf_op jit(solution)/shard_map/psum | solution.py:202
  (209 shorter events, 24.7 us)
Async XLA Ops:
  7.2 33.8 %all-gather.2.cloned.1.call-start = ((), (), s32[]{:S(2)}) async-start(), calls=%async_computation.2 | async-start | bytes 1310720 | tf_op jit(solution)/shard_map/all_gather | solution.py:121
  8.3 34.9 %copy-start.8 = (f32[2,64]{1,0:T(2,128)}, f32[2,64]{1,0:T(2,128)S(1)}, u32[]{:S(2)}) copy-start(f32[2,64]{1,0:T(2,128)S(1)} %add_rsqrt_fusion) | copy-start | bytes 1540
  13.3 0.6 copy-start.6
  13.3 29.9 %copy-start.10 = (f32[2,64]{1,0:T(2,128)}, f32[2,64]{1,0:T(2,128)S(1)}, u32[]{:S(2)}) copy-start(f32[2,64]{1,0:T(2,128)S(1)} %get-tuple-element.846) | copy-start | bytes 1540
  43.3 63.6 %reduce-scatter.7.cloned.1.call-start = ((), (), s32[]{:S(2)}) async-start(), calls=%async_computation.3 | async-start | bytes 81920 | tf_op jit(solution)/shard_map/while
  75.3 0.9 copy-start.1
  76.2 53.6 %reduce-scatter.9.cloned.1.call-start = ((), (), s32[]{:S(2)}) async-start(), calls=%async_computation.4 | async-start | bytes 655360 | tf_op jit(solution)/shard_map/while/body/eval_jaxpr/reduce_scatter | solution.py:159
  89.1 13.6 %copy-start.9 = (f32[2,64,1]{1,2,0:T(1,128)S(1)}, f32[2,64,1]{1,2,0:T(1,128)}, u32[]{:S(2)}) copy-start(f32[2,64,1]{1,2,0:T(1,128)} %get-tuple-element.1106) | copy-start | bytes 1540 | tf_op jit(solution)/shard_map/while
  89.1 13.6 %copy-start.11 = (f32[2,64,1]{1,2,0:T(1,128)S(1)}, f32[2,64,1]{1,2,0:T(1,128)}, u32[]{:S(2)}) copy-start(f32[2,64,1]{1,2,0:T(1,128)} %get-tuple-element.1115) | copy-start | bytes 1540 | tf_op jit(solution)/shard_map/while
  89.1 18.6 %copy-start.3 = (bf16[2,64,1024]{2,1,0:T(8,128)(2,1)S(1)}, bf16[2,64,1024]{2,1,0:T(8,128)(2,1)}, u32[]{:S(2)}) copy-start(bf16[2,64,1024]{2,1,0:T(8,128)(2,1)} %get-tuple-element.1120) | copy-start | bytes 786436 | tf_op jit(solution)/shard_map/while
  89.1 18.6 %copy-start.7 = (f32[2,64,4]{1,2,0:T(4,128)S(1)}, f32[2,64,4]{1,2,0:T(4,128)}, u32[]{:S(2)}) copy-start(f32[2,64,4]{1,2,0:T(4,128)} %get-tuple-element.1116) | copy-start | bytes 6148 | tf_op jit(solution)/shard_map/while
  89.1 40.6 %copy-start.4 = (f32[4,1024]{1,0:T(4,128)S(1)}, f32[4,1024]{1,0:T(4,128)}, u32[]{:S(2)}) copy-start(f32[4,1024]{1,0:T(4,128)} %get-tuple-element.1117) | copy-start | bytes 49156 | tf_op jit(solution)/shard_map/while
  89.1 40.6 %copy-start.5 = (f32[1,1024]{1,0:T(1,128)S(1)}, f32[1,1024]{1,0:T(1,128)}, u32[]{:S(2)}) copy-start(f32[1,1024]{1,0:T(1,128)} %get-tuple-element.1118) | copy-start | bytes 12292 | tf_op jit(solution)/shard_map/while
  131.4 3.2 collective-permute-start
  134.6 68.4 %reduce-scatter.7.cloned.1.call-start = ((), (), s32[]{:S(2)}) async-start(), calls=%async_computation.3 | async-start | bytes 81920 | tf_op jit(solution)/shard_map/while
  166.5 0.9 copy-start.1
  167.3 56.8 %reduce-scatter.9.cloned.1.call-start = ((), (), s32[]{:S(2)}) async-start(), calls=%async_computation.4 | async-start | bytes 655360 | tf_op jit(solution)/shard_map/while/body/eval_jaxpr/reduce_scatter | solution.py:159
  185.7 17.3 %copy-start.9 = (f32[2,64,1]{1,2,0:T(1,128)S(1)}, f32[2,64,1]{1,2,0:T(1,128)}, u32[]{:S(2)}) copy-start(f32[2,64,1]{1,2,0:T(1,128)} %get-tuple-element.1106) | copy-start | bytes 1540 | tf_op jit(solution)/shard_map/while
  185.7 17.3 %copy-start.11 = (f32[2,64,1]{1,2,0:T(1,128)S(1)}, f32[2,64,1]{1,2,0:T(1,128)}, u32[]{:S(2)}) copy-start(f32[2,64,1]{1,2,0:T(1,128)} %get-tuple-element.1115) | copy-start | bytes 1540 | tf_op jit(solution)/shard_map/while
  185.7 18.2 %copy-start.3 = (bf16[2,64,1024]{2,1,0:T(8,128)(2,1)S(1)}, bf16[2,64,1024]{2,1,0:T(8,128)(2,1)}, u32[]{:S(2)}) copy-start(bf16[2,64,1024]{2,1,0:T(8,128)(2,1)} %get-tuple-element.1120) | copy-start | bytes 786436 | tf_op jit(solution)/shard_map/while
  185.7 18.2 %copy-start.7 = (f32[2,64,4]{1,2,0:T(4,128)S(1)}, f32[2,64,4]{1,2,0:T(4,128)}, u32[]{:S(2)}) copy-start(f32[2,64,4]{1,2,0:T(4,128)} %get-tuple-element.1116) | copy-start | bytes 6148 | tf_op jit(solution)/shard_map/while
  185.7 38.4 %copy-start.4 = (f32[4,1024]{1,0:T(4,128)S(1)}, f32[4,1024]{1,0:T(4,128)}, u32[]{:S(2)}) copy-start(f32[4,1024]{1,0:T(4,128)} %get-tuple-element.1117) | copy-start | bytes 49156 | tf_op jit(solution)/shard_map/while
  185.7 38.4 %copy-start.5 = (f32[1,1024]{1,0:T(1,128)S(1)}, f32[1,1024]{1,0:T(1,128)}, u32[]{:S(2)}) copy-start(f32[1,1024]{1,0:T(1,128)} %get-tuple-element.1118) | copy-start | bytes 12292 | tf_op jit(solution)/shard_map/while
  225.8 3.2 collective-permute-start
  229.0 68.6 %reduce-scatter.7.cloned.1.call-start = ((), (), s32[]{:S(2)}) async-start(), calls=%async_computation.3 | async-start | bytes 81920 | tf_op jit(solution)/shard_map/while
  260.9 0.9 copy-start.1
  261.8 56.9 %reduce-scatter.9.cloned.1.call-start = ((), (), s32[]{:S(2)}) async-start(), calls=%async_computation.4 | async-start | bytes 655360 | tf_op jit(solution)/shard_map/while/body/eval_jaxpr/reduce_scatter | solution.py:159
  280.3 17.3 %copy-start.9 = (f32[2,64,1]{1,2,0:T(1,128)S(1)}, f32[2,64,1]{1,2,0:T(1,128)}, u32[]{:S(2)}) copy-start(f32[2,64,1]{1,2,0:T(1,128)} %get-tuple-element.1106) | copy-start | bytes 1540 | tf_op jit(solution)/shard_map/while
  280.3 17.3 %copy-start.11 = (f32[2,64,1]{1,2,0:T(1,128)S(1)}, f32[2,64,1]{1,2,0:T(1,128)}, u32[]{:S(2)}) copy-start(f32[2,64,1]{1,2,0:T(1,128)} %get-tuple-element.1115) | copy-start | bytes 1540 | tf_op jit(solution)/shard_map/while
  280.3 18.2 %copy-start.3 = (bf16[2,64,1024]{2,1,0:T(8,128)(2,1)S(1)}, bf16[2,64,1024]{2,1,0:T(8,128)(2,1)}, u32[]{:S(2)}) copy-start(bf16[2,64,1024]{2,1,0:T(8,128)(2,1)} %get-tuple-element.1120) | copy-start | bytes 786436 | tf_op jit(solution)/shard_map/while
  280.3 18.2 %copy-start.7 = (f32[2,64,4]{1,2,0:T(4,128)S(1)}, f32[2,64,4]{1,2,0:T(4,128)}, u32[]{:S(2)}) copy-start(f32[2,64,4]{1,2,0:T(4,128)} %get-tuple-element.1116) | copy-start | bytes 6148 | tf_op jit(solution)/shard_map/while
  280.3 38.4 %copy-start.4 = (f32[4,1024]{1,0:T(4,128)S(1)}, f32[4,1024]{1,0:T(4,128)}, u32[]{:S(2)}) copy-start(f32[4,1024]{1,0:T(4,128)} %get-tuple-element.1117) | copy-start | bytes 49156 | tf_op jit(solution)/shard_map/while
  280.3 38.4 %copy-start.5 = (f32[1,1024]{1,0:T(1,128)S(1)}, f32[1,1024]{1,0:T(1,128)}, u32[]{:S(2)}) copy-start(f32[1,1024]{1,0:T(1,128)} %get-tuple-element.1118) | copy-start | bytes 12292 | tf_op jit(solution)/shard_map/while
  320.3 3.2 collective-permute-start
  323.6 83.7 %reduce-scatter.7.cloned.1.call-start = ((), (), s32[]{:S(2)}) async-start(), calls=%async_computation.3 | async-start | bytes 81920 | tf_op jit(solution)/shard_map/while
  339.7 6.1 %copy-start.12 = (bf16[4096,1024]{1,0:T(8,128)(2,1)S(1)}, bf16[4096,1024]{1,0:T(8,128)(2,1)}, u32[]{:S(2)}) copy-start(bf16[4096,1024]{1,0:T(8,128)(2,1)} %get-tuple-element.567) | copy-start | bytes 25165828 | tf_op jit(solution)/shard_map/while/body/eval_jaxpr/cond
  339.7 19.6 %slice-start = ((s8[8388608]{0:T(1024)(128)(4,1)}), s8[4194304]{0:T(1024)(128)(4,1)S(1)}, s32[]{:S(2)}) async-start(s8[8388608]{0:T(1024)(128)(4,1)} %bitcast.155), calls=%async_computation.5 | async-start | bytes 8388608 | tf_op jit(solution)/shard_map/while/body/eval_jaxpr/cond
  345.8 5.4 copy-start.2
  345.8 13.6 %slice-start.1 = ((s8[8388608]{0:T(1024)(128)(4,1)}), s8[4194304]{0:T(1024)(128)(4,1)S(1)}, s32[]{:S(2)}) async-start(s8[8388608]{0:T(1024)(128)(4,1)} %bitcast.155), calls=%async_computation.6 | async-start | bytes 8388608 | tf_op jit(solution)/shard_map/while/body/eval_jaxpr/cond
  370.4 0.9 copy-start.1
  371.2 40.6 %reduce-scatter.9.cloned.1.call-start = ((), (), s32[]{:S(2)}) async-start(), calls=%async_computation.4 | async-start | bytes 655360 | tf_op jit(solution)/shard_map/while/body/eval_jaxpr/reduce_scatter | solution.py:159
  389.9 17.3 %copy-start.9 = (f32[2,64,1]{1,2,0:T(1,128)S(1)}, f32[2,64,1]{1,2,0:T(1,128)}, u32[]{:S(2)}) copy-start(f32[2,64,1]{1,2,0:T(1,128)} %get-tuple-element.1106) | copy-start | bytes 1540 | tf_op jit(solution)/shard_map/while
  389.9 17.3 %copy-start.11 = (f32[2,64,1]{1,2,0:T(1,128)S(1)}, f32[2,64,1]{1,2,0:T(1,128)}, u32[]{:S(2)}) copy-start(f32[2,64,1]{1,2,0:T(1,128)} %get-tuple-element.1115) | copy-start | bytes 1540 | tf_op jit(solution)/shard_map/while
  390.0 18.2 %copy-start.3 = (bf16[2,64,1024]{2,1,0:T(8,128)(2,1)S(1)}, bf16[2,64,1024]{2,1,0:T(8,128)(2,1)}, u32[]{:S(2)}) copy-start(bf16[2,64,1024]{2,1,0:T(8,128)(2,1)} %get-tuple-element.1120) | copy-start | bytes 786436 | tf_op jit(solution)/shard_map/while
  390.0 18.2 %copy-start.7 = (f32[2,64,4]{1,2,0:T(4,128)S(1)}, f32[2,64,4]{1,2,0:T(4,128)}, u32[]{:S(2)}) copy-start(f32[2,64,4]{1,2,0:T(4,128)} %get-tuple-element.1116) | copy-start | bytes 6148 | tf_op jit(solution)/shard_map/while
  390.0 21.8 %copy-start.4 = (f32[4,1024]{1,0:T(4,128)S(1)}, f32[4,1024]{1,0:T(4,128)}, u32[]{:S(2)}) copy-start(f32[4,1024]{1,0:T(4,128)} %get-tuple-element.1117) | copy-start | bytes 49156 | tf_op jit(solution)/shard_map/while
  390.0 21.8 %copy-start.5 = (f32[1,1024]{1,0:T(1,128)S(1)}, f32[1,1024]{1,0:T(1,128)}, u32[]{:S(2)}) copy-start(f32[1,1024]{1,0:T(1,128)} %get-tuple-element.1118) | copy-start | bytes 12292 | tf_op jit(solution)/shard_map/while
  413.4 3.2 collective-permute-start
  416.6 83.6 %reduce-scatter.7.cloned.1.call-start = ((), (), s32[]{:S(2)}) async-start(), calls=%async_computation.3 | async-start | bytes 81920 | tf_op jit(solution)/shard_map/while
  432.8 6.1 %copy-start.12 = (bf16[4096,1024]{1,0:T(8,128)(2,1)S(1)}, bf16[4096,1024]{1,0:T(8,128)(2,1)}, u32[]{:S(2)}) copy-start(bf16[4096,1024]{1,0:T(8,128)(2,1)} %get-tuple-element.567) | copy-start | bytes 25165828 | tf_op jit(solution)/shard_map/while/body/eval_jaxpr/cond
  432.8 19.6 %slice-start = ((s8[8388608]{0:T(1024)(128)(4,1)}), s8[4194304]{0:T(1024)(128)(4,1)S(1)}, s32[]{:S(2)}) async-start(s8[8388608]{0:T(1024)(128)(4,1)} %bitcast.155), calls=%async_computation.5 | async-start | bytes 8388608 | tf_op jit(solution)/shard_map/while/body/eval_jaxpr/cond
  438.8 5.4 copy-start.2
  438.9 13.6 %slice-start.1 = ((s8[8388608]{0:T(1024)(128)(4,1)}), s8[4194304]{0:T(1024)(128)(4,1)S(1)}, s32[]{:S(2)}) async-start(s8[8388608]{0:T(1024)(128)(4,1)} %bitcast.155), calls=%async_computation.6 | async-start | bytes 8388608 | tf_op jit(solution)/shard_map/while/body/eval_jaxpr/cond
  463.4 0.9 copy-start.1
  464.3 40.5 %reduce-scatter.9.cloned.1.call-start = ((), (), s32[]{:S(2)}) async-start(), calls=%async_computation.4 | async-start | bytes 655360 | tf_op jit(solution)/shard_map/while/body/eval_jaxpr/reduce_scatter | solution.py:159
  482.9 17.3 %copy-start.9 = (f32[2,64,1]{1,2,0:T(1,128)S(1)}, f32[2,64,1]{1,2,0:T(1,128)}, u32[]{:S(2)}) copy-start(f32[2,64,1]{1,2,0:T(1,128)} %get-tuple-element.1106) | copy-start | bytes 1540 | tf_op jit(solution)/shard_map/while
  482.9 17.3 %copy-start.11 = (f32[2,64,1]{1,2,0:T(1,128)S(1)}, f32[2,64,1]{1,2,0:T(1,128)}, u32[]{:S(2)}) copy-start(f32[2,64,1]{1,2,0:T(1,128)} %get-tuple-element.1115) | copy-start | bytes 1540 | tf_op jit(solution)/shard_map/while
  482.9 18.2 %copy-start.3 = (bf16[2,64,1024]{2,1,0:T(8,128)(2,1)S(1)}, bf16[2,64,1024]{2,1,0:T(8,128)(2,1)}, u32[]{:S(2)}) copy-start(bf16[2,64,1024]{2,1,0:T(8,128)(2,1)} %get-tuple-element.1120) | copy-start | bytes 786436 | tf_op jit(solution)/shard_map/while
  482.9 18.2 %copy-start.7 = (f32[2,64,4]{1,2,0:T(4,128)S(1)}, f32[2,64,4]{1,2,0:T(4,128)}, u32[]{:S(2)}) copy-start(f32[2,64,4]{1,2,0:T(4,128)} %get-tuple-element.1116) | copy-start | bytes 6148 | tf_op jit(solution)/shard_map/while
  482.9 21.9 %copy-start.4 = (f32[4,1024]{1,0:T(4,128)S(1)}, f32[4,1024]{1,0:T(4,128)}, u32[]{:S(2)}) copy-start(f32[4,1024]{1,0:T(4,128)} %get-tuple-element.1117) | copy-start | bytes 49156 | tf_op jit(solution)/shard_map/while
  482.9 21.9 %copy-start.5 = (f32[1,1024]{1,0:T(1,128)S(1)}, f32[1,1024]{1,0:T(1,128)}, u32[]{:S(2)}) copy-start(f32[1,1024]{1,0:T(1,128)} %get-tuple-element.1118) | copy-start | bytes 12292 | tf_op jit(solution)/shard_map/while
  506.4 3.2 collective-permute-start
  509.7 13.6 %copy-start = (f32[1024,4096]{1,0:T(8,128)S(1)}, f32[1024,4096]{1,0:T(8,128)}, u32[]{:S(2)}) copy-start(f32[1024,4096]{1,0:T(8,128)} %get-tuple-element.609) | copy-start | bytes 50331652
Sparse Core Ops, SparseCore 0:
  10.2 30.6 all-gather.1
  76.3 30.5 reduce-scatter.6
  109.7 19.9 reduce-scatter.8
  167.5 33.8 reduce-scatter.6
  204.1 20.0 reduce-scatter.8
  261.9 33.8 reduce-scatter.6
  298.6 20.0 reduce-scatter.8
  371.3 17.5 reduce-scatter.6
  391.8 19.9 reduce-scatter.8
  464.4 17.4 reduce-scatter.6
  484.7 20.0 reduce-scatter.8
where the time goes:
time: 551 us; the launch traced here: 550 us
  other arithmetic  188 us (34%)
  waiting for transfers between devices  113 us (21%)
  blocking collectives  92.6 us (17%)
  matrix products  73.1 us (13%)
  local copies, waits for them, and re-layouts  61.6 us (11%)
  between operations  13.8 us (3%)
  starting transfers between devices  6.77 us (1%)
    add x5, other arithmetic, step_fn(): acc_up = acc_up + up_term  83.5 us
    add x5, other arithmetic, step_fn(): acc_down = acc_down + down_term  82.6 us
    all_gather x5, blocking collectives, step_fn(): cot_rows = lax.all_gather(grad_in, 'expert', axis=0, tiled=True)  76.1 us
    reduce_scatter x5, waiting for transfers between devices, step_fn(): lax.psum_scatter(expert_grad.astype(jnp.bfloat16), 'expert', scatter_dime...  68.8 us
    another operation x12, local copies, waits for them, and re-layouts  47.1 us
    all_gather x1, waiting for transfers between devices, body(): normed_all = lax.all_gather(normed_own, 'expert', axis=1, tiled=True)  27.1 us
    dot_general x2, matrix products, weight_terms(): lax.dot_general(act_low, scaled, (((0,), (0,)), ((), ())), preferred_elem...  17.3 us
    psum x1, blocking collectives, body(): router_sum, gain_sum = lax.psum((final_state[3], final_state[4]), 'expert')  16.5 us
  transfers between devices with their start and end apart: 16, of which 12 were waited for; matrix products, arithmetic and copies ran while one was open for 32% of the time, Pallas kernels for 0%

commit v1 on v0

v1 whole, which is shorter than its diff:
```python
import functools

import jax
import jax.numpy as jnp
from jax import lax
from jax.experimental import pallas as pl
from jax.experimental.pallas import tpu as pltpu
from jax.sharding import PartitionSpec as P

norm_eps = 1e-06
gelu_coef = 0.7978845608028654
cubic_coef = 0.044715
BLOCK_ROWS = 64
BLOCK_CAP = 40
F32 = jnp.float32
BF16 = jnp.bfloat16
AUX = 8


def vmem():
    return pl.BlockSpec(memory_space=pltpu.VMEM)


def smem():
    return pl.BlockSpec(memory_space=pltpu.SMEM)


def params(mebi=24):
    return pltpu.CompilerParams(vmem_limit_bytes=mebi * 1024 * 1024)


def cost(flops, nbytes):
    return pl.CostEstimate(flops=int(flops), bytes_accessed=int(nbytes), transcendentals=0)


def dot(a, b, dims):
    return lax.dot_general(a, b, ((dims[0:1], dims[1:2]), ((), ())), preferred_element_type=F32)


def iota(shape, dim):
    return lax.broadcasted_iota(jnp.int32, shape, dim)


def row_norm(values):
    mean_sq = jnp.mean(values * values, axis=-1, keepdims=True)
    return lax.rsqrt(mean_sq + norm_eps)


def eye(size):
    return (iota((size, size), 0) == iota((size, size), 1)).astype(F32)


def prep_kernel(
    shards, slices, rows, slots, cap, place, x_far, cot_far, up_far, col_ref, row_ref, gain_ref, router_ref, *outs
):
    x_ref, cot_ref, sems = outs[-3:]
    up_ref = outs[-4]
    outs = outs[:-4]
    loads = [
        pltpu.make_async_copy(source, target, sems.at[index])
        for index, (source, target) in enumerate([(x_far, x_ref), (cot_far, cot_ref), (up_far, up_ref)])
    ]
    for load in loads:
        load.start()
    loads[0].wait()
    loads[1].wait()
    h_outs, c_outs = outs[:shards], outs[shards : 2 * shards - 1]
    gather_ref, scatter_ref, score_ref, own_ref = outs[2 * shards - 1 :]
    me = place[0]
    is_last = place[1] == place[2]
    total = x_ref.shape[0]
    experts = router_ref.shape[0]
    x = x_ref[...].astype(F32)
    h32 = (x * row_norm(x)) * gain_ref[...]
    h = h32.astype(BF16)
    logits = lax.dot_general(
        h.astype(F32), router_ref[...], (((1,), (1,)), ((), ())),
        preferred_element_type=F32, precision=lax.Precision.HIGHEST,
    )
    scores = 1.0 / (1.0 + jnp.exp(-logits))
    ids = iota((total, experts), 1)
    hits = jnp.logical_or(col_ref[:, 0:1] == ids, col_ref[:, 1:2] == ids).astype(F32)
    totals = jnp.sum(scores * hits, axis=-1, keepdims=True)
    weights = scores * hits / totals
    score_ref[0] = scores
    score_ref[1] = weights
    score_ref[2] = hits
    score_ref[3] = jnp.broadcast_to(totals, (total, experts))
    first, second = iota((total, total), 0), iota((total, total), 1)
    same = (first // rows) == (second // rows)
    before = jnp.logical_and(same, second < first).astype(BF16)
    after = jnp.logical_and(same, first < second).astype(BF16)
    base_col = (iota((total, experts), 0) // rows * cap).astype(F32)
    slot_col = jnp.where(hits > 0.0, dot(before, hits.astype(BF16), (1, 0)) + base_col, -1.0)
    ids_row = iota((experts, total), 0)
    hits_row = jnp.logical_or(row_ref[0:1, :] == ids_row, row_ref[1:2, :] == ids_row).astype(F32)
    base_row = (iota((experts, total), 1) // rows * cap).astype(F32)
    slot_row = jnp.where(hits_row > 0.0, dot(hits_row.astype(BF16), after, (1, 0)) + base_row, -1.0)
    cot = cot_ref[...]
    own_ref[...] = jnp.where(is_last, cot.astype(F32), 0.0).astype(BF16)
    slot_lane = iota((total, slots), 1).astype(F32)
    slot_sub = iota((slots, total), 0).astype(F32)
    for step in range(shards):
        expert = lax.rem(me + step, shards) // slices
        mine = (ids == expert).astype(F32)
        slot_c = jnp.sum(slot_col * mine, axis=-1, keepdims=True)
        slot_r = jnp.sum(slot_row * (ids_row == expert).astype(F32), axis=0, keepdims=True)
        scatter = (slot_c == slot_lane).astype(F32)
        gather = (slot_r == slot_sub).astype(F32).astype(BF16)
        weight_c = jnp.sum(weights * mine, axis=-1, keepdims=True)
        weight_r = jnp.sum(scatter * weight_c, axis=0, keepdims=True)
        high = weight_r.astype(BF16).astype(F32)
        low = weight_r - high
        aux_id = iota((AUX, slots), 0)
        aux = jnp.where(aux_id == 0, high, jnp.where(aux_id == 1, low, 0.0)).astype(BF16)
        picked = dot(gather, h, (1, 0)).astype(BF16)
        for target in [h_outs[step]] + ([c_outs[step - 1]] if step else []):
            target[0:slots, :] = picked
            target[slots : slots + AUX, :] = jnp.zeros((AUX, x.shape[1]), BF16)
            target[slots : slots + AUX, 0:slots] = aux
        if step:
            c_outs[step - 1][slots + AUX :, :] = dot(gather, cot, (1, 0)).astype(BF16)
        gather_ref[step] = gather
        scatter_ref[step] = scatter.astype(BF16)
    loads[2].wait()


def forward_kernel(slots, width, loads, own, others, *refs):
    refs = list(refs)[1:]
    take = lambda n: [refs.pop(0) for _ in range(n)]
    if loads:
        sem = refs.pop()
        load = pltpu.make_async_copy(take(1)[0], refs.pop(), sem)
        load.start()
    sources = [take(1) for _ in range(own)] + [take(2) for _ in range(others)]
    up_ref = take(1)[0]
    act_ref, slope_ref, rows_ref, wt_ref = refs[-4:]
    for index, source in enumerate(sources):
        span = slice(index * slots, (index + 1) * slots)
        value = source[0][0 : slots + AUX, :].astype(F32)
        for extra in source[1:]:
            value = value + extra[0 : slots + AUX, :].astype(F32)
        rows_ref[span, :] = value[0:slots, :].astype(BF16)
        weight_r = value[slots : slots + 1, 0:slots] + value[slots + 1 : slots + 2, 0:slots]
        wt_ref[span, :] = jnp.sum(eye(slots) * weight_r, axis=-1, keepdims=True)

    def block(index, carry):
        span = pl.ds(pl.multiple_of(index * width, width), width)
        u = dot(rows_ref[...], up_ref[:, span], (1, 0))
        square = u * u
        tanh_val = jnp.tanh(gelu_coef * (u + cubic_coef * square * u))
        half = 0.5 * (1.0 + tanh_val)
        act_ref[:, span] = (u * half).astype(BF16)
        slope = half + 0.5 * u * (1.0 - tanh_val * tanh_val) * (gelu_coef * (1.0 + 3.0 * cubic_coef * square))
        slope_ref[:, span] = (slope * wt_ref[...]).astype(BF16)
        return carry

    lax.fori_loop(0, up_ref.shape[1] // width, block, 0)
    if loads:
        load.wait()


def back_kernel(slots, width, base, stage, keep, has_after, has_own, has_prev, others, place, *refs):
    refs = list(refs)[1:] if has_after else list(refs)
    reached = place[1] + stage >= place[2]
    take = lambda n: [refs.pop(0) for _ in range(n)]
    own_count = (2 if has_prev else 1) if has_own else 0
    own_in = take(own_count)
    gather_ref = take(1)[0] if has_own else None
    recv_in = take(others)
    prev_in = take(others) if has_prev else None
    up_ref, down_ref, act_ref, slope_ref = take(4)
    own_out = take(1)[0] if has_own else None
    cot_ref = take(1)[0]
    q_ref = take(1)[0] if keep else None
    parts = take(others + (1 if has_own else 0))
    acc_ref = take(1)[0]
    shift = 1 if has_own else 0
    if has_own:
        own = own_in[0][...]
        if has_prev:
            own = (own.astype(F32) + own_in[1][...].astype(F32)).astype(BF16)
        own_out[...] = own
        cot_ref[0:slots, :] = dot(gather_ref[0], own, (1, 0)).astype(BF16)
    for place in range(others):
        value = recv_in[place][base : base + slots, :]
        if has_prev:
            old = prev_in[place][(place + shift) * slots : (place + shift + 1) * slots, :]
            value = (value.astype(F32) + old.astype(F32)).astype(BF16)
        cot_ref[(place + shift) * slots : (place + shift + 1) * slots, :] = value

    @pl.when(reached)
    def _():
        hidden = down_ref.shape[0]
        lanes = 128
        acc_ref[...] = jnp.zeros_like(acc_ref)

        def block(index, comb):
            span = pl.ds(pl.multiple_of(index * width, width), width)
            t = dot(cot_ref[...], down_ref[span, :], (1, 1))
            prod = act_ref[:, span].astype(F32) * t
            for start in range(0, width, lanes):
                comb = comb + prod[:, start : start + lanes]
            q = (slope_ref[:, span].astype(F32) * t).astype(BF16)
            if keep:
                q_ref[:, span] = q
            acc_ref[...] += dot(q, up_ref[:, span], (1, 1))
            return comb

        comb = lax.fori_loop(0, hidden // width, block, jnp.zeros((cot_ref.shape[0], lanes), F32))
        for place, part in enumerate(parts):
            span = slice(place * slots, (place + 1) * slots)
            part[0:slots, :] = acc_ref[span, :].astype(BF16)
            comb_c = jnp.sum(comb[span, :], axis=-1, keepdims=True)
            comb_r = jnp.sum(eye(slots) * comb_c, axis=0, keepdims=True)
            part[slots : slots + AUX, :] = jnp.zeros((AUX, part.shape[1]), BF16)
            part[slots : slots + AUX, 0:slots] = jnp.broadcast_to(comb_r, (AUX, slots)).astype(BF16)


def owner_kernel(shards, slices, slots, stage, want_next, place, *refs):
    refs = list(refs) if want_next else list(refs)[1:]
    parts = refs[:shards]
    own_ref, x_ref, gain_ref, router_ref, score_ref, scatter_ref, acc_ref = refs[shards : shards + 7]
    refs = refs[shards + 7 :]
    me = place[0]
    active = place[1] == place[2] - stage
    if want_next:
        gather_ref, acc_out, own_out = refs[0:3]
        sends = refs[3:]
    else:
        (acc_out,) = refs

    @pl.when(jnp.logical_not(active))
    def _():
        acc_out[...] = acc_ref[...]

    @pl.when(active)
    def _():
        experts = router_ref.shape[0]
        total = x_ref.shape[0]
        ids = iota((total, experts), 1)
        gh = jnp.zeros(x_ref.shape, F32)
        comb = jnp.zeros((total, experts), F32)
        for step in range(shards):
            expert = lax.rem(me + step, shards) // slices
            scatter = scatter_ref[step]
            gh = gh + dot(scatter, parts[step][0:slots, :], (1, 0))
            comb_r = parts[step][slots : slots + AUX, 0:slots].astype(F32)[0:1, :]
            comb_c = jnp.sum(scatter.astype(F32) * comb_r, axis=-1, keepdims=True)
            comb = comb + comb_c * (ids == expert).astype(F32)
        scores, weights, hits, totals = (score_ref[i] for i in range(4))
        center_comb = jnp.sum(weights * comb, axis=-1, keepdims=True)
        logit_grad = hits * (comb - center_comb) / totals * (scores * (1.0 - scores))
        for expert in range(experts):
            gh = gh + logit_grad[:, expert : expert + 1] * router_ref[expert : expert + 1, :]
        x = x_ref[...].astype(F32)
        inverse = row_norm(x)
        normed = x * inverse
        gain = gain_ref[...]
        if want_next:
            scaled = gh * gain
            center = jnp.mean(scaled * normed, axis=-1, keepdims=True)
            gx = (own_ref[...].astype(F32) + inverse * (scaled - normed * center)).astype(BF16)
            own_out[...] = gx
            for step in range(1, shards):
                sends[step - 1][...] = dot(gather_ref[step], gx, (1, 0)).astype(BF16)
        h = (normed * gain).astype(BF16).astype(F32)
        terms = [
            jnp.sum(logit_grad[:, expert : expert + 1] * h, axis=0, keepdims=True) for expert in range(experts)
        ]
        terms.append(jnp.sum(gh * normed, axis=0, keepdims=True))
        for index, term in enumerate(terms):
            acc_out[index : index + 1, :] = term
        rest = acc_out.shape[0] - len(terms)
        if rest:
            acc_out[len(terms) :, :] = jnp.zeros((rest, x.shape[1]), F32)


def up_kernel(count, *refs):
    rows, qs = refs[:count], refs[count : 2 * count]
    out_ref, mark_ref = refs[2 * count : 2 * count + 2]
    turned = refs[2 * count + 2 :]

    @pl.when(pl.program_id(0) == 0)
    def _():
        mark_ref[...] = jnp.zeros_like(mark_ref)
        for index in range(count):
            turned[index][...] = rows[index][...].astype(F32).T.astype(BF16)

    total = dot(turned[0][...], qs[0][...], (1, 0))
    for index in range(1, count):
        total = total + dot(turned[index][...], qs[index][...], (1, 0))
    out_ref[...] = total.astype(BF16)


def down_kernel(count, after, *refs):
    cots, wts, acts = (refs[i * count : (i + 1) * count] for i in range(3))
    out_ref = refs[3 * count]
    y_refs = refs[3 * count + 1 :]

    @pl.when(pl.program_id(0) == 0)
    def _():
        for index in range(count):
            y_refs[index][...] = (wts[index][...] * cots[index][...].astype(F32)).astype(BF16)

    total = dot(acts[0][...], y_refs[0][...], (0, 0))
    for index in range(1, count):
        total = total + dot(acts[index][...], y_refs[index][...], (0, 0))
    out_ref[...] = total.astype(BF16)


def finish_kernel(shards, experts, *refs):
    total = refs[0][...]
    for ref in refs[1:shards]:
        total = total + ref[...]
    refs[shards][...] = total[0:experts, :]
    refs[shards + 1][...] = total[experts : experts + 1, :]


def body(
    layer_inputs, out_cotangent, expert_routes, norm_gain, router_weight, up_weight, down_weight
):
    sections = lax.axis_size("section")
    section_id = lax.axis_index("section")
    shards = lax.axis_size("expert")
    shard_id = lax.axis_index("expert")
    micro, rows, feat = layer_inputs.shape[1:]
    router = router_weight[0]
    experts = router.shape[0]
    up = up_weight[0]
    down = down_weight[0]
    hidden = up.shape[1]
    slices = shards // experts
    total = micro * rows
    cap = rows // BLOCK_ROWS * BLOCK_CAP if rows % BLOCK_ROWS == 0 else rows
    slots = micro * cap
    sent = slots + AUX
    last = sections - 1
    x = layer_inputs[0].reshape(total, feat)
    cot = out_cotangent.reshape(total, feat)
    chosen = lax.dynamic_slice_in_dim(expert_routes[0], shard_id * rows, rows, 1).reshape(total, 2)
    gain = norm_gain
    place = jnp.stack([shard_id, section_id, jnp.int32(last)]).astype(jnp.int32)
    steps = list(range(shards))
    split = max(1, shards // 2)
    chunks = [steps[:split], steps[split:]]
    chunks = [chunk for chunk in chunks if chunk]
    width = min(1024, hidden)
    blocks = hidden // width

    def sds(shape, dtype=BF16):
        return jax.ShapeDtypeStruct(shape, dtype)

    def move(value, pairs):
        flat = [(sz * sections + ss, dz * sections + ds) for (ss, sz), (ds, dz) in pairs]
        return lax.ppermute(value, ("expert", "section"), flat)

    def spread(value, step, sources, drop):
        return move(
            value,
            [((s, z), (s - drop, (z + step) % shards)) for s in sources for z in range(shards) if s - drop >= 0],
        )

    def any_place():
        return pl.BlockSpec(memory_space=pl.ANY)

    everyone = list(range(sections))
    far = [pltpu.with_memory_space_constraint(array, pltpu.HBM) for array in (x, cot, up)]
    prep = pl.pallas_call(
        functools.partial(prep_kernel, shards, slices, rows, slots, cap),
        out_shape=[sds((sent, feat))] * shards
        + [sds((sent + slots, feat))] * (shards - 1)
        + [sds((shards, slots, total)), sds((shards, total, slots)), sds((4, total, experts), F32), sds((total, feat))]
        + [pltpu.VMEM(up.shape, BF16)],
        in_specs=[smem()] + [pl.BlockSpec(memory_space=pltpu.HBM)] * 3 + [vmem()] * 4,
        out_specs=[vmem()] * (2 * shards + 4),
        scratch_shapes=[pltpu.VMEM((total, feat), BF16)] * 2 + [pltpu.SemaphoreType.DMA((3,))],
        compiler_params=params(),
        cost_estimate=cost(1e7, 4e6),
        name="prep",
    )(place, *far, chosen, chosen.T, gain, router)
    up_near = prep[-1]
    h_send, c_send = prep[:shards], [None] + list(prep[shards : 2 * shards - 1])
    gather, scatter, score, own = prep[2 * shards - 1 : -1]
    first_recv = [None] + [spread(c_send[step], step, [last], 0) for step in steps[1:]]
    h_recv = [None] + [spread(h_send[step], step, everyone[:-1], 0) for step in steps[1:]]
    gather_next = move(gather, [((s - 1, z), (s, z)) for s in everyone[1:] for z in range(shards)])
    down_far = pltpu.with_memory_space_constraint(down, pltpu.HBM)

    def const(block):
        return pl.BlockSpec(block, lambda i: (0,) * len(block))

    def chunk_rows(chunk):
        return len(chunk) * slots

    def col_block(chunk):
        return pl.BlockSpec((chunk_rows(chunk), width), lambda i: (0, i))

    def forward(chunk, after, load):
        count = chunk_rows(chunk)
        own_part = 1 if chunk[0] == 0 else 0
        args, specs = [after], [any_place()]
        if load is not None:
            args.append(load)
            specs.append(pl.BlockSpec(memory_space=pltpu.HBM))
        args += [h_send[0]] * own_part
        for step in chunk[own_part:]:
            args += [first_recv[step], h_recv[step]]
        args += [pltpu.with_memory_space_constraint(up_near, pltpu.VMEM)]
        specs += [vmem()] * (len(args) - len(specs))
        return list(pl.pallas_call(
            functools.partial(forward_kernel, slots, width, load is not None, own_part, len(chunk) - own_part),
            out_shape=[sds((count, hidden))] * 2
            + [sds((count, feat)), sds((count, 1), F32)]
            + ([pltpu.VMEM(load.shape, BF16)] if load is not None else []),
            in_specs=specs,
            out_specs=[vmem()] * (4 if load is None else 5),
            scratch_shapes=[] if load is None else [pltpu.SemaphoreType.DMA(())],
            compiler_params=params(),
            cost_estimate=cost(2 * count * feat * hidden, 2 * feat * hidden),
            name="forward",
        )(*args))

    def back(stage, chunk, act, slope, recv, base, own_recv, own, prev, after):
        has_own = chunk[0] == 0
        has_prev = prev is not None
        keep = stage == last
        others = [step for step in chunk if step]
        args, specs = [place], [smem()]
        if after is not None:
            args.append(after)
            specs.append(any_place())
        if has_own:
            args += ([own_recv, own] if has_prev else [own]) + [gather]
        args += [recv[step] for step in others]
        if has_prev:
            args += [prev] * len(others)
        args += [pltpu.with_memory_space_constraint(array, pltpu.VMEM) for array in (up_near, down_near)]
        args += [act, slope]
        specs += [vmem()] * (len(args) - len(specs))
        count = chunk_rows(chunk)
        outs = pl.pallas_call(
            functools.partial(back_kernel, slots, width, base, stage, keep, after is not None, has_own, has_prev, len(others)),
            out_shape=([sds((total, feat))] if has_own else [])
            + [sds((count, feat))]
            + ([sds((count, hidden))] if keep else [])
            + [sds((sent, feat))] * len(chunk),
            in_specs=specs,
            out_specs=[vmem()] * (int(has_own) + 1 + int(keep) + len(chunk)),
            scratch_shapes=[pltpu.VMEM((count, feat), F32)],
            compiler_params=params(),
            cost_estimate=cost(4 * count * feat * hidden, 4 * feat * hidden),
            name="back",
        )(*args)
        outs = list(outs)
        own_now = outs.pop(0) if has_own else None
        cot_now = outs.pop(0)
        q = outs.pop(0) if keep else None
        return own_now, cot_now, q, outs

    count = len(chunks)
    kept = [None] * count
    recv, base, own_recv = first_recv, sent, None
    prev = [None] * count
    acc = jnp.zeros((-(-(experts + 1) // 8) * 8, feat), F32)
    up_spec = pl.BlockSpec((feat, width), lambda i: (0, i))
    down_spec = pl.BlockSpec((width, feat), lambda i: (i, 0))
    for stage in range(sections):
        parts, qs, cots = {}, [], []
        after = None
        for index, chunk in enumerate(chunks):
            if stage == 0:
                first = index == 0
                kept[index] = forward(chunk, gather_next if first else after, down_far if first else None)
                if first:
                    down_near = kept[index].pop()
                after = None
            own_now, cot_now, q, outs = back(
                stage, chunk, kept[index][0], kept[index][1], recv, base, own_recv, own, prev[index], after
            )
            if chunk[0] == 0:
                own = own_now
            cots.append(cot_now)
            qs.append(q)
            parts.update(zip(chunk, outs))
            after = outs[0]
        prev = cots
        section = last - stage
        partial = [parts[0]] + [spread(parts[step], -step, [section], 0) for step in steps[1:]]
        want_next = section > 0
        if want_next:
            extra, extra_specs = [], []
        else:
            up_grad, mark = pl.pallas_call(
                functools.partial(up_kernel, count),
                grid=(blocks,),
                out_shape=[sds((feat, hidden)), sds((8, 128), F32)],
                in_specs=[const((chunk_rows(c), feat)) for c in chunks] + [col_block(c) for c in chunks],
                out_specs=[up_spec, const((8, 128))],
                scratch_shapes=[pltpu.VMEM((feat, chunk_rows(c)), BF16) for c in chunks],
                compiler_params=params(),
                cost_estimate=cost(2 * shards * slots * feat * hidden, 2 * feat * hidden),
                name="up_grad",
            )(*[k[2] for k in kept], *qs)
            extra, extra_specs = [mark], [any_place()]
        outs = pl.pallas_call(
            functools.partial(owner_kernel, shards, slices, slots, stage, want_next),
            out_shape=[sds(acc.shape, F32)]
            + ([sds((total, feat))] + [sds((slots, feat))] * (shards - 1) if want_next else []),
            in_specs=[smem()] + extra_specs + [vmem()] * (shards + 7 + (1 if want_next else 0)),
            out_specs=[vmem()] * (1 + (shards if want_next else 0)),
            compiler_params=params(),
            cost_estimate=cost(1e7, 4e6),
            name="owner",
        )(place, *extra, *partial, own, x, gain, router, score, scatter, acc, *([gather_next] if want_next else []))
        acc = outs[0]
        if want_next:
            own_recv = spread(outs[1], 0, [section], 1)
            recv = [None] + [spread(outs[1 + step], step, [section], 1) for step in steps[1:]]
            base = 0
    sums = [acc] + [spread(acc, step, everyone, 0) for step in steps[1:]]
    down_grad = pl.pallas_call(
        functools.partial(down_kernel, count),
        grid=(blocks,),
        out_shape=sds((hidden, feat)),
        in_specs=[any_place()]
        + [const((chunk_rows(c), feat)) for c in chunks]
        + [const((chunk_rows(c), 1)) for c in chunks]
        + [col_block(c) for c in chunks],
        out_specs=down_spec,
        scratch_shapes=[pltpu.VMEM((chunk_rows(c), feat), BF16) for c in chunks],
        compiler_params=params(),
        cost_estimate=cost(2 * shards * slots * feat * hidden, 2 * feat * hidden),
        name="down_grad",
    )(acc, *cots, *[k[3] for k in kept], *[k[0] for k in kept])
    router_grad, gain_grad = pl.pallas_call(
        functools.partial(finish_kernel, shards, experts),
        out_shape=[sds((experts, feat), F32), sds((1, feat), F32)],
        in_specs=[vmem()] * shards,
        out_specs=[vmem()] * 2,
        compiler_params=params(),
        name="finish",
    )(*sums)
    return (up_grad[None], down_grad[None], router_grad[None], gain_grad)


def solution(mesh):
    in_specs = (
        P("section", None, ("groups", "expert"), None),
        P(None, ("groups", "expert"), None),
        P("section", None, "groups", None),
        P("section", None),
        P("section", None, None),
        P("section", None, "expert"),
        P("section", "expert", None),
    )
    out_specs = (
        P("section", "groups", "expert"),
        P("section", "expert", "groups"),
        P("section", "groups", None),
        P("section", "groups"),
    )
    return jax.shard_map(body, mesh=mesh, in_specs=in_specs, out_specs=out_specs, check_vma=False)
```

time: 551 us -> 189 us (0.34)
  other arithmetic: 188 us -> 0.08 us
  blocking collectives: 92.6 us -> 0 us
  matrix products: 73.1 us -> 0 us
  local copies, waits for them, and re-layouts: 61.6 us -> 2.39 us
  Pallas kernels: 0 us -> 47.5 us
  starting transfers between devices: 6.77 us -> 45 us
  waiting for transfers between devices: 113 us -> 91.8 us
  between operations: 13.8 us -> 1.25 us
    add x15 -> x0, other arithmetic: 166 us -> none  [the longest x5 83.5 us: step_fn(): acc_up = acc_up + up_term]
    ppermute x5 -> x34, waiting for transfers between devices: 9.64 us -> 91.8 us  [move(): return lax.ppermute(value, ('expert', 'section'), flat)]
    all_gather x5 -> x0, blocking collectives: 76.1 us -> none  [step_fn(): cot_rows = lax.all_gather(grad_in, 'expert', axis=0, tiled=True)]
    dot_general x22 -> x0, matrix products: 73.1 us -> none  [the longest x2 17.3 us: weight_terms(): lax.dot_general(act_low, scaled, (((0,), (0,)), ((), ())), preferred_elem...]
    reduce_scatter x5 -> x0, waiting for transfers between devices: 68.8 us -> none  [step_fn(): lax.psum_scatter(expert_grad.astype(jnp.bfloat16), 'expert', scatter_dime...]
    pallas_call x0 -> x18, Pallas kernels: none -> 47.5 us  [the longest x8 18.4 us: back(): pl.pallas_call(functools.partial(back_kernel, slots, width, base, stage,...]
    another operation x12 -> x0, local copies, waits for them, and re-layouts: 47.1 us -> none
    ppermute x5 -> x34, starting transfers between devices: 6.46 us -> 45 us  [move(): return lax.ppermute(value, ('expert', 'section'), flat)]
  transfers between devices with their start and end apart: 16 -> 34, of which waited for: 12 -> 3; matrix products, arithmetic and copies ran while one was open for 32% -> 0% of each run, Pallas kernels for 0% -> 20%
where the time goes in v1:
time: 189 us; the launch traced here: 188 us
  waiting for transfers between devices  91.8 us (49%)
  Pallas kernels  47.5 us (25%)
  starting transfers between devices  45 us (24%)
  local copies, waits for them, and re-layouts  2.39 us (1%)
    ppermute x34, waiting for transfers between devices, move(): return lax.ppermute(value, ('expert', 'section'), flat)  91.8 us
    ppermute x34, starting transfers between devices, move(): return lax.ppermute(value, ('expert', 'section'), flat)  45 us
    pallas_call x8, Pallas kernels, back(): pl.pallas_call(functools.partial(back_kernel, slots, width, base, stage,...  18.4 us
    pallas_call x2, Pallas kernels, forward(): pl.pallas_call(functools.partial(forward_kernel, slots, width, load is no...  7.48 us
    pallas_call x1, Pallas kernels, body(): pl.pallas_call(functools.partial(down_kernel, count), grid=(blocks,), out...  6.94 us
    pallas_call x1, Pallas kernels, body(): pl.pallas_call(functools.partial(up_kernel, count), grid=(blocks,), out_s...  6.9 us
    pallas_call x1, Pallas kernels, body(): pl.pallas_call(functools.partial(prep_kernel, shards, slices, rows, slots...  4.14 us
  transfers between devices with their start and end apart: 34, of which 3 were waited for; matrix products, arithmetic and copies ran while one was open for 0% of the time, Pallas kernels for 20%

profile of v1, /device:TPU:0, one launch (start us, length us, event | category | flops | bytes accessed | tf_op | source)
XLA Modules:
  0.0 188.0 jit_solution(3813910370977906608)
XLA Ops:
  0.6 0.0 copy-start
  0.7 0.7 copy-done
  1.3 0.1 constant_dynamic-slice_fusion
  1.4 0.1 reshape.17
  1.5 0.1 copy.12.col_ref
  1.6 0.1 pad_add_fusion.place
  1.7 0.7 copy-done.3
  2.4 0.7 copy-done.5
  3.1 4.1 %prep.1 = (bf16[88,1024]{1,0:T(8,128)(2,1)S(1)}, bf16[88,1024]{1,0:T(8,128)(2,1)S(1)}, bf16[88,1024]{1,0:T(8,128)(2,1)S(1)}, bf16[88,1024]{1,0:T(8,128)(2,1)S(1)...) custom-call(s32[3]{0:T(128)S(1)} %pad_add_fusion.place, ...), custom_call_target="tpu_custom_call" | custom-call | flops 10000000 | bytes 4000000 | tf_op jit(solution)/shard_map/prep/pallas_call | solution.py:369
  7.2 0.7 collective-permute-start.1
  7.9 5.0 %collective-permute-start.2 = (bf16[88,1024]{1,0:T(8,128)(2,1)S(1)}, bf16[88,1024]{1,0:T(8,128)(2,1)S(1)}, u32[]{:S(2)}, u32[]{:S(2)}) collective-permute-start(bf16[88,1024]{1,0:T(8,128)(2,1)S(1)} %get-tuple-element.77), channel_id=1, source_target_pairs={{0,4},{4,8},{8,12},{12,0},{1,5},{5,9},{9,13},{13,1},{2,6},{6,10},{... | collective-permute-start | bytes 540680 | tf_op jit(solution)/shard_map/ppermute | solution.py:356
  12.9 1.5 collective-permute-start
  14.4 4.5 %collective-permute-start.4 = (bf16[88,1024]{1,0:T(8,128)(2,1)S(1)}, bf16[88,1024]{1,0:T(8,128)(2,1)S(1)}, u32[]{:S(2)}, u32[]{:S(2)}) collective-permute-start(bf16[88,1024]{1,0:T(8,128)(2,1)S(1)} %get-tuple-element.86), channel_id=1, source_target_pairs={{0,8},{4,12},{8,0},{12,4},{1,9},{5,13},{9,1},{13,5},{2,10},{6,14},... | collective-permute-start | bytes 540680 | tf_op jit(solution)/shard_map/ppermute | solution.py:356
  18.9 3.3 %collective-permute-start.6 = (bf16[88,1024]{1,0:T(8,128)(2,1)S(1)}, bf16[88,1024]{1,0:T(8,128)(2,1)S(1)}, u32[]{:S(2)}, u32[]{:S(2)}) collective-permute-start(bf16[88,1024]{1,0:T(8,128)(2,1)S(1)} %get-tuple-element.88), channel_id=1, source_target_pairs={{0,12},{4,0},{8,4},{12,8},{1,13},{5,1},{9,5},{13,9},{2,14},{6,2},{... | collective-permute-start | bytes 540680 | tf_op jit(solution)/shard_map/ppermute | solution.py:356
  22.1 0.7 collective-permute-start.3
  22.8 0.7 collective-permute-start.5
  23.5 3.7 %forward.2 = (bf16[160,4096]{1,0:T(8,128)(2,1)S(1)}, bf16[160,4096]{1,0:T(8,128)(2,1)S(1)}, bf16[160,1024]{1,0:T(8,128)(2,1)S(1)}, f32[160,1]{1,0:T(8,128)S(1)}, bf16[4096,1024]{1,0:T(8,128)(2,1)S(1)}) custom-call(bf16[4,80,128]{2,1,0:T(8,128)(2,1)S(1)} %collective-permute-done.refs_0_.refs_11_, bf16[4096,1024]{1,0:T(8,128)(2,1)} %bitcast.25, ...), custom_call_target="tpu_custom_call" | custom-call | flops 1342177280 | bytes 8388608 | tf_op jit(solution)/shard_map/forward/pallas_call | solution.py:411
  27.3 0.7 back.8
  28.0 0.7 collective-permute-start.7
  28.7 1.7 collective-permute-done.6.refs_4_
  30.3 3.8 %forward.3 = (bf16[160,4096]{1,0:T(8,128)(2,1)S(1)}, bf16[160,4096]{1,0:T(8,128)(2,1)S(1)}, bf16[160,1024]{1,0:T(8,128)(2,1)S(1)}, f32[160,1]{1,0:T(8,128)S(1)}) custom-call(bf16[88,1024]{1,0:T(8,128)(2,1)S(1)} %get-tuple-element.84.refs_0_, bf16[168,1024]{1,0:T(8,128)(2,1)S(1)} %collective-permute-done.3.refs_1_.refs_0_, ...), custom_call_target="tpu_custom_call" | custom-call | flops 1342177280 | bytes 8388608 | tf_op jit(solution)/shard_map/forward/pallas_call | solution.py:411
  34.1 0.0 copy-start.2
  34.2 0.6 back.9
  34.7 0.7 collective-permute-start.8
  35.4 0.7 collective-permute-start.9
  36.2 0.6 owner.4
  36.7 0.7 collective-permute-start.10
  37.4 0.7 collective-permute-start.11
  38.1 0.7 collective-permute-start.13
  38.8 0.7 collective-permute-start.14
  39.5 0.8 back.10
  40.3 0.6 back.11
  40.9 0.7 collective-permute-start.15
  41.6 0.7 collective-permute-start.16
  42.3 0.7 collective-permute-start.12
  43.0 0.6 owner.5
  43.5 0.7 collective-permute-start.17
  44.2 0.7 collective-permute-start.18
  44.9 0.7 collective-permute-start.20
  45.6 0.9 collective-permute-start.21
  46.5 0.8 back.12
  47.2 0.6 back.13
  47.9 0.7 collective-permute-start.22
  48.6 0.7 collective-permute-start.23
  49.2 0.7 collective-permute-start.19
  49.9 0.6 owner.6
  50.5 1.3 collective-permute-start.24
  51.8 1.3 collective-permute-start.25
  53.1 1.3 collective-permute-start.26
  54.4 1.3 collective-permute-start.27
  55.7 89.3 %collective-permute-done.25.refs_3_ = bf16[80,1024]{1,0:T(8,128)(2,1)S(1)} collective-permute-done((bf16[80,1024]{1,0:T(8,128)(2,1)S(1)}, bf16[80,1024]{1,0:T(8,128)(2,1)S(1)}, u32[]{:S(2)}, u32[]{:S(2)}) %collective-permute-start.25) | collective-permute-done | bytes 163872 | tf_op jit(solution)/shard_map/ppermute | solution.py:356
  145.0 7.2 %back.14 = (bf16[128,1024]{1,0:T(8,128)(2,1)S(1)}, bf16[160,1024]{1,0:T(8,128)(2,1)S(1)}, bf16[160,4096]{1,0:T(8,128)(2,1)S(1)}, bf16[88,1024]{1,0:T(8,128)(2,1)S(1)}, bf16[88,1024]{1,0:T(8,128)(2,1)S(1)}) custom-call(s32[3]{0:T(128)S(1)} %pad_add_fusion.place, bf16[128,1024]{1,0:T(8,128)(2,1)S(1)} %collective-permute-done.24.refs_0_, ...), custom_call_target="tpu_custom_call" | custom-call | flops 2684354560 | bytes 16777216 | tf_op jit(solution)/shard_map/back/pallas_call | solution.py:442
  152.3 1.9 %collective-permute-start.28 = (bf16[88,1024]{1,0:T(8,128)(2,1)S(1)}, bf16[88,1024]{1,0:T(8,128)(2,1)S(1)}, u32[]{:S(2)}, u32[]{:S(2)}) collective-permute-start(bf16[88,1024]{1,0:T(8,128)(2,1)S(1)} %get-tuple-element.133), channel_id=1, source_target_pairs={{0,12},{4,0},{8,4},{12,8},{16,28},{20,16},{24,20},{28,24}} | collective-permute-start | bytes 540680 | tf_op jit(solution)/shard_map/ppermute | solution.py:356
  154.2 7.1 %back.15 = (bf16[160,1024]{1,0:T(8,128)(2,1)S(1)}, bf16[160,4096]{1,0:T(8,128)(2,1)S(1)}, bf16[88,1024]{1,0:T(8,128)(2,1)S(1)}, bf16[88,1024]{1,0:T(8,128)(2,1)S(1)}) custom-call(s32[3]{0:T(128)S(1)} %pad_add_fusion.place, bf16[88,1024]{1,0:T(8,128)(2,1)S(1)} %get-tuple-element.126.refs_0_.refs_1_, bf16[80,1024]{1,0:T(8,128)(2,1)S(1)} %collective-permute-done.26.refs_1_, ...), custom_call_target="tpu_custom_call" | custom-call | flops 2684354560 | bytes 16777216 | tf_op jit(solution)/shard_map/back/pallas_call | solution.py:442
  161.3 1.9 %collective-permute-start.29 = (bf16[88,1024]{1,0:T(8,128)(2,1)S(1)}, bf16[88,1024]{1,0:T(8,128)(2,1)S(1)}, u32[]{:S(2)}, u32[]{:S(2)}) collective-permute-start(bf16[88,1024]{1,0:T(8,128)(2,1)S(1)} %get-tuple-element.134), channel_id=1, source_target_pairs={{0,8},{4,12},{8,0},{12,4},{16,24},{20,28},{24,16},{28,20}} | collective-permute-start | bytes 540680 | tf_op jit(solution)/shard_map/ppermute | solution.py:356
  163.3 3.9 %collective-permute-start.30 = (bf16[88,1024]{1,0:T(8,128)(2,1)S(1)}, bf16[88,1024]{1,0:T(8,128)(2,1)S(1)}, u32[]{:S(2)}, u32[]{:S(2)}) collective-permute-start(bf16[88,1024]{1,0:T(8,128)(2,1)S(1)} %get-tuple-element.135), channel_id=1, source_target_pairs={{0,4},{4,8},{8,12},{12,0},{16,20},{20,24},{24,28},{28,16}} | collective-permute-start | bytes 540680 | tf_op jit(solution)/shard_map/ppermute | solution.py:356
  167.2 6.9 %up_grad.1 = (bf16[1024,4096]{1,0:T(8,128)(2,1)}, f32[8,128]{1,0:T(8,128)S(1)}) custom-call(bf16[160,1024]{1,0:T(8,128)(2,1)S(1)} %get-tuple-element.79.refs_0_, bf16[160,1024]{1,0:T(8,128)(2,1)S(1)} %get-tuple-element.89.refs_1_, bf16[160,4096]{1,0:T(8,128)(2,1)S(1)} %get-tuple-element.125.refs_2_, bf16[160,4096]{1,0:T(8,128)(2,1)S(1)} %get-tuple-element.130.refs_3_), custom_call_target="tpu_custom_call" | custom-call | flops 2684354560 | bytes 8388608 | tf_op jit(solution)/shard_map/up_grad/pallas_call | solution.py:494
  174.1 0.8 collective-permute-done.29.refs_3_
  174.9 1.3 owner.7.after.refs_0_
  176.2 1.6 collective-permute-start.33
  177.9 0.6 collective-permute-start.32
  178.5 1.9 %collective-permute-start.31 = (f32[8,1024]{1,0:T(8,128)S(1)}, f32[8,1024]{1,0:T(8,128)S(1)}, u32[]{:S(2)}, u32[]{:S(2)}) collective-permute-start(f32[8,1024]{1,0:T(8,128)S(1)} %owner.7.after.refs_0_), channel_id=1, source_target_pairs={{0,4},{4,8},{8,12},{12,0},{1,5},{5,9},{9,13},{13,1},{2,6},{6,10},{... | collective-permute-start | bytes 98312 | tf_op jit(solution)/shard_map/ppermute | solution.py:356
  180.4 6.9 %down_grad.1 = bf16[4096,1024]{1,0:T(8,128)(2,1)} custom-call(f32[8,1024]{1,0:T(8,128)S(1)} %owner.7.after.refs_0_, bf16[160,1024]{1,0:T(8,128)(2,1)S(1)} %get-tuple-element.138.refs_0_, bf16[160,1024]{1,0:T(8,128)(2,1)S(1)} %get-tuple-element.139.refs_1_, f32[160,1]{1,0:T(8,128)S(1)} %get-tuple-element.140.refs_2_, ...), custom_call_target="tpu_custom_call" | custom-call | flops 2684354560 | bytes 8388608 | tf_op jit(solution)/shard_map/down_grad/pallas_call | solution.py:522
  187.4 0.6 finish.1
  (42 shorter events, 0.1 us)
Async XLA Ops:
  0.6 0.7 copy-start
  1.7 0.7 copy-start.3
  2.4 0.7 copy-start.5
  7.2 16.3 %collective-permute-start.1 = (bf16[168,1024]{1,0:T(8,128)(2,1)S(1)}, bf16[168,1024]{1,0:T(8,128)(2,1)S(1)}, u32[]{:S(2)}, u32[]{:S(2)}) collective-permute-start(bf16[168,1024]{1,0:T(8,128)(2,1)S(1)} %get-tuple-element.76), channel_id=1, source_target_pairs={{3,7},{7,11},{11,15},{15,3},{19,23},{23,27},{27,31},{31,19}} | collective-permute-start | bytes 1032200 | tf_op jit(solution)/shard_map/ppermute | solution.py:356
  7.9 14.9 %collective-permute-start.2 = (bf16[88,1024]{1,0:T(8,128)(2,1)S(1)}, bf16[88,1024]{1,0:T(8,128)(2,1)S(1)}, u32[]{:S(2)}, u32[]{:S(2)}) collective-permute-start(bf16[88,1024]{1,0:T(8,128)(2,1)S(1)} %get-tuple-element.77), channel_id=1, source_target_pairs={{0,4},{4,8},{8,12},{12,0},{1,5},{5,9},{9,13},{13,1},{2,6},{6,10},{... | collective-permute-start | bytes 540680 | tf_op jit(solution)/shard_map/ppermute | solution.py:356
  12.9 9.2 %collective-permute-start = (bf16[4,80,128]{2,1,0:T(8,128)(2,1)S(1)}, bf16[4,80,128]{2,1,0:T(8,128)(2,1)S(1)}, u32[]{:S(2)}, u32[]{:S(2)}) collective-permute-start(bf16[4,80,128]{2,1,0:T(8,128)(2,1)S(1)} %get-tuple-element.74.refs_1_.refs_2_), channel_id=1, source_target_pairs={{0,1},{4,5},{8,9},{12,13},{1,2},{5,6},{9,10},{13,14},{2,3},{6,7},{... | collective-permute-start | bytes 245768 | tf_op jit(solution)/shard_map/ppermute | solution.py:356
  14.4 14.3 %collective-permute-start.4 = (bf16[88,1024]{1,0:T(8,128)(2,1)S(1)}, bf16[88,1024]{1,0:T(8,128)(2,1)S(1)}, u32[]{:S(2)}, u32[]{:S(2)}) collective-permute-start(bf16[88,1024]{1,0:T(8,128)(2,1)S(1)} %get-tuple-element.86), channel_id=1, source_target_pairs={{0,8},{4,12},{8,0},{12,4},{1,9},{5,13},{9,1},{13,5},{2,10},{6,14},... | collective-permute-start | bytes 540680 | tf_op jit(solution)/shard_map/ppermute | solution.py:356
  18.9 11.5 %collective-permute-start.6 = (bf16[88,1024]{1,0:T(8,128)(2,1)S(1)}, bf16[88,1024]{1,0:T(8,128)(2,1)S(1)}, u32[]{:S(2)}, u32[]{:S(2)}) collective-permute-start(bf16[88,1024]{1,0:T(8,128)(2,1)S(1)} %get-tuple-element.88), channel_id=1, source_target_pairs={{0,12},{4,0},{8,4},{12,8},{1,13},{5,1},{9,5},{13,9},{2,14},{6,2},{... | collective-permute-start | bytes 540680 | tf_op jit(solution)/shard_map/ppermute | solution.py:356
  22.1 8.2 %collective-permute-start.3 = (bf16[168,1024]{1,0:T(8,128)(2,1)S(1)}, bf16[168,1024]{1,0:T(8,128)(2,1)S(1)}, u32[]{:S(2)}, u32[]{:S(2)}) collective-permute-start(bf16[168,1024]{1,0:T(8,128)(2,1)S(1)} %get-tuple-element.85), channel_id=1, source_target_pairs={{3,11},{7,15},{11,3},{15,7},{19,27},{23,31},{27,19},{31,23}} | collective-permute-start | bytes 1032200 | tf_op jit(solution)/shard_map/ppermute | solution.py:356
  22.8 7.5 %collective-permute-start.5 = (bf16[168,1024]{1,0:T(8,128)(2,1)S(1)}, bf16[168,1024]{1,0:T(8,128)(2,1)S(1)}, u32[]{:S(2)}, u32[]{:S(2)}) collective-permute-start(bf16[168,1024]{1,0:T(8,128)(2,1)S(1)} %get-tuple-element.87), channel_id=1, source_target_pairs={{3,15},{7,3},{11,7},{15,11},{19,31},{23,19},{27,23},{31,27}} | collective-permute-start | bytes 1032200 | tf_op jit(solution)/shard_map/ppermute | solution.py:356
  28.0 8.1 %collective-permute-start.7 = (bf16[88,1024]{1,0:T(8,128)(2,1)S(1)}, bf16[88,1024]{1,0:T(8,128)(2,1)S(1)}, u32[]{:S(2)}, u32[]{:S(2)}) collective-permute-start(bf16[88,1024]{1,0:T(8,128)(2,1)S(1)} %get-tuple-element.90), channel_id=1, source_target_pairs={{3,15},{7,3},{11,7},{15,11},{19,31},{23,19},{27,23},{31,27}} | collective-permute-start | bytes 540680 | tf_op jit(solution)/shard_map/ppermute | solution.py:356
  34.1 2.0 %copy-start.2 = (bf16[1,2,64,1024]{3,2,1,0:T(8,128)(2,1)S(1)}, bf16[1,2,64,1024]{3,2,1,0:T(8,128)(2,1)}, u32[]{:S(2)}) copy-start(bf16[1,2,64,1024]{3,2,1,0:T(8,128)(2,1)} %param.7) | copy-start | bytes 786436
  34.1 2.0 %copy-start.4 = (f32[1,4,1024]{2,1,0:T(4,128)S(1)}, f32[1,4,1024]{2,1,0:T(4,128)}, u32[]{:S(2)}) copy-start(f32[1,4,1024]{2,1,0:T(4,128)} %param.11) | copy-start | bytes 49156
  34.2 2.0 %copy-start.6 = (f32[1,1024]{1,0:T(1,128)S(1)}, f32[1,1024]{1,0:T(1,128)}, u32[]{:S(2)}) copy-start(f32[1,1024]{1,0:T(1,128)} %refs_7_.1) | copy-start | bytes 12292
  34.7 1.4 collective-permute-start.8
  35.4 0.7 collective-permute-start.9
  36.7 2.7 %collective-permute-start.10 = (bf16[128,1024]{1,0:T(8,128)(2,1)S(1)}, bf16[128,1024]{1,0:T(8,128)(2,1)S(1)}, u32[]{:S(2)}, u32[]{:S(2)}) collective-permute-start(bf16[128,1024]{1,0:T(8,128)(2,1)S(1)} %get-tuple-element.98), channel_id=1, source_target_pairs={{3,2},{7,6},{11,10},{15,14},{19,18},{23,22},{27,26},{31,30}} | collective-permute-start | bytes 786440 | tf_op jit(solution)/shard_map/ppermute | solution.py:356
  37.4 2.0 %collective-permute-start.11 = (bf16[80,1024]{1,0:T(8,128)(2,1)S(1)}, bf16[80,1024]{1,0:T(8,128)(2,1)S(1)}, u32[]{:S(2)}, u32[]{:S(2)}) collective-permute-start(bf16[80,1024]{1,0:T(8,128)(2,1)S(1)} %get-tuple-element.99), channel_id=1, source_target_pairs={{3,6},{7,10},{11,14},{15,2},{19,22},{23,26},{27,30},{31,18}} | collective-permute-start | bytes 491528 | tf_op jit(solution)/shard_map/ppermute | solution.py:356
  38.1 2.1 %collective-permute-start.13 = (bf16[80,1024]{1,0:T(8,128)(2,1)S(1)}, bf16[80,1024]{1,0:T(8,128)(2,1)S(1)}, u32[]{:S(2)}, u32[]{:S(2)}) collective-permute-start(bf16[80,1024]{1,0:T(8,128)(2,1)S(1)} %get-tuple-element.103), channel_id=1, source_target_pairs={{3,10},{7,14},{11,2},{15,6},{19,26},{23,30},{27,18},{31,22}} | collective-permute-start | bytes 491528 | tf_op jit(solution)/shard_map/ppermute | solution.py:356
  38.8 1.5 collective-permute-start.14
  40.9 2.0 %collective-permute-start.15 = (bf16[88,1024]{1,0:T(8,128)(2,1)S(1)}, bf16[88,1024]{1,0:T(8,128)(2,1)S(1)}, u32[]{:S(2)}, u32[]{:S(2)}) collective-permute-start(bf16[88,1024]{1,0:T(8,128)(2,1)S(1)} %get-tuple-element.106), channel_id=1, source_target_pairs={{2,10},{6,14},{10,2},{14,6},{18,26},{22,30},{26,18},{30,22}} | collective-permute-start | bytes 540680 | tf_op jit(solution)/shard_map/ppermute | solution.py:356
  41.6 1.4 collective-permute-start.16
  42.3 0.7 collective-permute-start.12
  43.5 2.9 %collective-permute-start.17 = (bf16[128,1024]{1,0:T(8,128)(2,1)S(1)}, bf16[128,1024]{1,0:T(8,128)(2,1)S(1)}, u32[]{:S(2)}, u32[]{:S(2)}) collective-permute-start(bf16[128,1024]{1,0:T(8,128)(2,1)S(1)} %get-tuple-element.110), channel_id=1, source_target_pairs={{2,1},{6,5},{10,9},{14,13},{18,17},{22,21},{26,25},{30,29}} | collective-permute-start | bytes 786440 | tf_op jit(solution)/shard_map/ppermute | solution.py:356
  44.2 2.2 %collective-permute-start.18 = (bf16[80,1024]{1,0:T(8,128)(2,1)S(1)}, bf16[80,1024]{1,0:T(8,128)(2,1)S(1)}, u32[]{:S(2)}, u32[]{:S(2)}) collective-permute-start(bf16[80,1024]{1,0:T(8,128)(2,1)S(1)} %get-tuple-element.111), channel_id=1, source_target_pairs={{2,5},{6,9},{10,13},{14,1},{18,21},{22,25},{26,29},{30,17}} | collective-permute-start | bytes 491528 | tf_op jit(solution)/shard_map/ppermute | solution.py:356
  44.9 2.3 %collective-permute-start.20 = (bf16[80,1024]{1,0:T(8,128)(2,1)S(1)}, bf16[80,1024]{1,0:T(8,128)(2,1)S(1)}, u32[]{:S(2)}, u32[]{:S(2)}) collective-permute-start(bf16[80,1024]{1,0:T(8,128)(2,1)S(1)} %get-tuple-element.115), channel_id=1, source_target_pairs={{2,9},{6,13},{10,1},{14,5},{18,25},{22,29},{26,17},{30,21}} | collective-permute-start | bytes 491528 | tf_op jit(solution)/shard_map/ppermute | solution.py:356
  45.6 1.7 collective-permute-start.21
  47.9 2.0 %collective-permute-start.22 = (bf16[88,1024]{1,0:T(8,128)(2,1)S(1)}, bf16[88,1024]{1,0:T(8,128)(2,1)S(1)}, u32[]{:S(2)}, u32[]{:S(2)}) collective-permute-start(bf16[88,1024]{1,0:T(8,128)(2,1)S(1)} %get-tuple-element.118), channel_id=1, source_target_pairs={{1,9},{5,13},{9,1},{13,5},{17,25},{21,29},{25,17},{29,21}} | collective-permute-start | bytes 540680 | tf_op jit(solution)/shard_map/ppermute | solution.py:356
  48.6 1.4 collective-permute-start.23
  49.2 0.7 collective-permute-start.19
  50.5 94.5 %collective-permute-start.24 = (bf16[128,1024]{1,0:T(8,128)(2,1)S(1)}, bf16[128,1024]{1,0:T(8,128)(2,1)S(1)}, u32[]{:S(2)}, u32[]{:S(2)}) collective-permute-start(bf16[128,1024]{1,0:T(8,128)(2,1)S(1)} %get-tuple-element.122), channel_id=1, source_target_pairs={{1,0},{5,4},{9,8},{13,12},{17,16},{21,20},{25,24},{29,28}} | collective-permute-start | bytes 786440 | tf_op jit(solution)/shard_map/ppermute | solution.py:356
  51.8 93.2 %collective-permute-start.25 = (bf16[80,1024]{1,0:T(8,128)(2,1)S(1)}, bf16[80,1024]{1,0:T(8,128)(2,1)S(1)}, u32[]{:S(2)}, u32[]{:S(2)}) collective-permute-start(bf16[80,1024]{1,0:T(8,128)(2,1)S(1)} %get-tuple-element.123), channel_id=1, source_target_pairs={{1,4},{5,8},{9,12},{13,0},{17,20},{21,24},{25,28},{29,16}} | collective-permute-start | bytes 491528 | tf_op jit(solution)/shard_map/ppermute | solution.py:356
  53.1 101.1 %collective-permute-start.26 = (bf16[80,1024]{1,0:T(8,128)(2,1)S(1)}, bf16[80,1024]{1,0:T(8,128)(2,1)S(1)}, u32[]{:S(2)}, u32[]{:S(2)}) collective-permute-start(bf16[80,1024]{1,0:T(8,128)(2,1)S(1)} %get-tuple-element.127), channel_id=1, source_target_pairs={{1,8},{5,12},{9,0},{13,4},{17,24},{21,28},{25,16},{29,20}} | collective-permute-start | bytes 491528 | tf_op jit(solution)/shard_map/ppermute | solution.py:356
  54.4 99.8 %collective-permute-start.27 = (bf16[80,1024]{1,0:T(8,128)(2,1)S(1)}, bf16[80,1024]{1,0:T(8,128)(2,1)S(1)}, u32[]{:S(2)}, u32[]{:S(2)}) collective-permute-start(bf16[80,1024]{1,0:T(8,128)(2,1)S(1)} %get-tuple-element.128), channel_id=1, source_target_pairs={{1,12},{5,0},{9,4},{13,8},{17,28},{21,16},{25,20},{29,24}} | collective-permute-start | bytes 491528 | tf_op jit(solution)/shard_map/ppermute | solution.py:356
  152.3 21.9 %collective-permute-start.28 = (bf16[88,1024]{1,0:T(8,128)(2,1)S(1)}, bf16[88,1024]{1,0:T(8,128)(2,1)S(1)}, u32[]{:S(2)}, u32[]{:S(2)}) collective-permute-start(bf16[88,1024]{1,0:T(8,128)(2,1)S(1)} %get-tuple-element.133), channel_id=1, source_target_pairs={{0,12},{4,0},{8,4},{12,8},{16,28},{20,16},{24,20},{28,24}} | collective-permute-start | bytes 540680 | tf_op jit(solution)/shard_map/ppermute | solution.py:356
  161.3 13.6 %collective-permute-start.29 = (bf16[88,1024]{1,0:T(8,128)(2,1)S(1)}, bf16[88,1024]{1,0:T(8,128)(2,1)S(1)}, u32[]{:S(2)}, u32[]{:S(2)}) collective-permute-start(bf16[88,1024]{1,0:T(8,128)(2,1)S(1)} %get-tuple-element.134), channel_id=1, source_target_pairs={{0,8},{4,12},{8,0},{12,4},{16,24},{20,28},{24,16},{28,20}} | collective-permute-start | bytes 540680 | tf_op jit(solution)/shard_map/ppermute | solution.py:356
  163.3 11.6 %collective-permute-start.30 = (bf16[88,1024]{1,0:T(8,128)(2,1)S(1)}, bf16[88,1024]{1,0:T(8,128)(2,1)S(1)}, u32[]{:S(2)}, u32[]{:S(2)}) collective-permute-start(bf16[88,1024]{1,0:T(8,128)(2,1)S(1)} %get-tuple-element.135), channel_id=1, source_target_pairs={{0,4},{4,8},{8,12},{12,0},{16,20},{20,24},{24,28},{28,16}} | collective-permute-start | bytes 540680 | tf_op jit(solution)/shard_map/ppermute | solution.py:356
  167.2 20.8 %copy-start.1 = (s32[1,2,256,2]{2,3,1,0:T(2,128)S(1)}, s32[1,2,256,2]{2,3,1,0:T(2,128)}, u32[]{:S(2)}) copy-start(s32[1,2,256,2]{2,3,1,0:T(2,128)} %param.9) | copy-start | bytes 12292
  176.2 11.2 %collective-permute-start.33 = (f32[8,1024]{1,0:T(8,128)S(1)}, f32[8,1024]{1,0:T(8,128)S(1)}, u32[]{:S(2)}, u32[]{:S(2)}) collective-permute-start(f32[8,1024]{1,0:T(8,128)S(1)} %owner.7.after.refs_0_), channel_id=1, source_target_pairs={{0,12},{4,0},{8,4},{12,8},{1,13},{5,1},{9,5},{13,9},{2,14},{6,2},{... | collective-permute-start | bytes 98312 | tf_op jit(solution)/shard_map/ppermute | solution.py:356
  177.9 9.5 %collective-permute-start.32 = (f32[8,1024]{1,0:T(8,128)S(1)}, f32[8,1024]{1,0:T(8,128)S(1)}, u32[]{:S(2)}, u32[]{:S(2)}) collective-permute-start(f32[8,1024]{1,0:T(8,128)S(1)} %owner.7.after.refs_0_), channel_id=1, source_target_pairs={{0,8},{4,12},{8,0},{12,4},{1,9},{5,13},{9,1},{13,5},{2,10},{6,14},... | collective-permute-start | bytes 98312 | tf_op jit(solution)/shard_map/ppermute | solution.py:356
  178.5 8.9 %collective-permute-start.31 = (f32[8,1024]{1,0:T(8,128)S(1)}, f32[8,1024]{1,0:T(8,128)S(1)}, u32[]{:S(2)}, u32[]{:S(2)}) collective-permute-start(f32[8,1024]{1,0:T(8,128)S(1)} %owner.7.after.refs_0_), channel_id=1, source_target_pairs={{0,4},{4,8},{8,12},{12,0},{1,5},{5,9},{9,13},{13,1},{2,6},{6,10},{... | collective-permute-start | bytes 98312 | tf_op jit(solution)/shard_map/ppermute | solution.py:356

commit v2 on v1

v2 whole, which is shorter than its diff:
```python
import functools

import jax
import jax.numpy as jnp
from jax import lax
from jax.experimental import pallas as pl
from jax.experimental.pallas import tpu as pltpu
from jax.sharding import PartitionSpec as P

norm_eps = 1e-06
gelu_coef = 0.7978845608028654
cubic_coef = 0.044715
BLOCK_ROWS = 64
BLOCK_CAP = 40
F32 = jnp.float32
BF16 = jnp.bfloat16
AUX = 8
SIDES = 4
FEAT_WIDTH = 512


def vmem():
    return pl.BlockSpec(memory_space=pltpu.VMEM)


def smem():
    return pl.BlockSpec(memory_space=pltpu.SMEM)


def params(mebi=12):
    return pltpu.CompilerParams(vmem_limit_bytes=mebi * 1024 * 1024)


def cost(flops, nbytes):
    return pl.CostEstimate(flops=int(flops), bytes_accessed=int(nbytes), transcendentals=0)


def dot(a, b, dims):
    return lax.dot_general(a, b, ((dims[0:1], dims[1:2]), ((), ())), preferred_element_type=F32)


def iota(shape, dim):
    return lax.broadcasted_iota(jnp.int32, shape, dim)


def row_norm(values):
    mean_sq = jnp.mean(values * values, axis=-1, keepdims=True)
    return lax.rsqrt(mean_sq + norm_eps)


def eye(size):
    return (iota((size, size), 0) == iota((size, size), 1)).astype(F32)


def prep_kernel(
    shards, slices, rows, slots, cap, place, x_far, cot_far, gain_far, router_far, col_ref, row_ref, *outs
):
    x_ref, cot_ref, gain_ref, router_ref, sems = outs[-5:]
    outs = outs[:-5]
    loads = [
        pltpu.make_async_copy(source, target, sems.at[index])
        for index, (source, target) in enumerate([(x_far, x_ref), (cot_far, cot_ref), (gain_far, gain_ref), (router_far, router_ref)])
    ]
    for load in loads:
        load.start()
    for load in loads:
        load.wait()
    h_outs, c_outs = outs[:shards], outs[shards : 2 * shards - 1]
    gather_ref, scatter_ref, score_ref, own_ref = outs[2 * shards - 1 :]
    me = place[0]
    is_last = place[1] == place[2]
    total = x_ref.shape[0]
    experts = router_ref.shape[0]
    x = x_ref[...].astype(F32)
    h32 = (x * row_norm(x)) * gain_ref[...]
    h = h32.astype(BF16)
    logits = lax.dot_general(
        h.astype(F32), router_ref[...], (((1,), (1,)), ((), ())),
        preferred_element_type=F32, precision=lax.Precision.HIGHEST,
    )
    scores = 1.0 / (1.0 + jnp.exp(-logits))
    ids = iota((total, experts), 1)
    hits = jnp.logical_or(col_ref[:, 0:1] == ids, col_ref[:, 1:2] == ids).astype(F32)
    totals = jnp.sum(scores * hits, axis=-1, keepdims=True)
    weights = scores * hits / totals
    slopes = scores * (1.0 - scores) / totals
    score_ref[0] = scores
    score_ref[1] = weights
    score_ref[2] = hits
    score_ref[3] = jnp.broadcast_to(totals, (total, experts))
    first, second = iota((total, total), 0), iota((total, total), 1)
    same = (first // rows) == (second // rows)
    before = jnp.logical_and(same, second < first).astype(BF16)
    after = jnp.logical_and(same, first < second).astype(BF16)
    base_col = (iota((total, experts), 0) // rows * cap).astype(F32)
    slot_col = jnp.where(hits > 0.0, dot(before, hits.astype(BF16), (1, 0)) + base_col, -1.0)
    ids_row = iota((experts, total), 0)
    hits_row = jnp.logical_or(row_ref[0:1, :] == ids_row, row_ref[1:2, :] == ids_row).astype(F32)
    base_row = (iota((experts, total), 1) // rows * cap).astype(F32)
    slot_row = jnp.where(hits_row > 0.0, dot(hits_row.astype(BF16), after, (1, 0)) + base_row, -1.0)
    cot = cot_ref[...]
    own_ref[...] = jnp.where(is_last, cot.astype(F32), 0.0).astype(BF16)
    slot_lane = iota((total, slots), 1).astype(F32)
    slot_sub = iota((slots, total), 0).astype(F32)
    for step in range(shards):
        expert = lax.rem(me + step, shards) // slices
        mine = (ids == expert).astype(F32)
        slot_c = jnp.sum(slot_col * mine, axis=-1, keepdims=True)
        slot_r = jnp.sum(slot_row * (ids_row == expert).astype(F32), axis=0, keepdims=True)
        scatter = (slot_c == slot_lane).astype(F32)
        gather = (slot_r == slot_sub).astype(F32).astype(BF16)
        weight_c = jnp.sum(weights * mine, axis=-1, keepdims=True)
        rest = hits * (1.0 - mine)
        slope_c = jnp.sum(slopes * mine, axis=-1, keepdims=True)
        slope_o = jnp.sum(slopes * rest, axis=-1, keepdims=True)
        other_c = jnp.sum(ids.astype(F32) * rest, axis=-1, keepdims=True)
        sides = [weight_c, (1.0 - weight_c) * slope_c, 0.0 - weight_c * slope_o, other_c]
        aux = jnp.zeros((AUX, slots), F32)
        aux_id = iota((AUX, slots), 0)
        for index, side in enumerate(sides):
            side_r = jnp.sum(scatter * side, axis=0, keepdims=True)
            high = side_r.astype(BF16).astype(F32)
            aux = jnp.where(aux_id == 2 * index, high, jnp.where(aux_id == 2 * index + 1, side_r - high, aux))
        aux = aux.astype(BF16)
        picked = dot(gather, h, (1, 0)).astype(BF16)
        for target in [h_outs[step]] + ([c_outs[step - 1]] if step else []):
            target[0:slots, :] = picked
            target[slots : slots + AUX, :] = jnp.zeros((AUX, x.shape[1]), BF16)
            target[slots : slots + AUX, 0:slots] = aux
        if step:
            c_outs[step - 1][slots + AUX :, :] = dot(gather, cot, (1, 0)).astype(BF16)
        gather_ref[step] = gather
        scatter_ref[step] = scatter.astype(BF16)


def forward_kernel(slots, width, loads, own, others, *refs):
    refs = list(refs)[1:]
    take = lambda n: [refs.pop(0) for _ in range(n)]
    sources = [take(1) for _ in range(own)] + [take(2) for _ in range(others)]
    far = take(2 if loads else 0)
    near = take(0 if loads else 1)
    act_ref, slope_ref, rows_ref, side_ref = take(4)
    if loads:
        near = take(2)
        sems = refs[0]
    up_ref = near[0]
    blocks = up_ref.shape[1] // width

    def column_load(index):
        span = pl.ds(pl.multiple_of(index * width, width), width)
        return pltpu.make_async_copy(far[0].at[:, span], up_ref.at[:, span], sems.at[index])

    if loads:
        for index in range(blocks):
            column_load(index).start()
        down_load = pltpu.make_async_copy(far[1], near[1], sems.at[blocks])
        down_load.start()
    for index, source in enumerate(sources):
        span = slice(index * slots, (index + 1) * slots)
        value = source[0][0 : slots + AUX, :].astype(F32)
        for extra in source[1:]:
            value = value + extra[0 : slots + AUX, :].astype(F32)
        rows_ref[span, :] = value[0:slots, :].astype(BF16)
        for column in range(SIDES):
            low = slots + 2 * column
            side_r = value[low : low + 1, 0:slots] + value[low + 1 : low + 2, 0:slots]
            side_ref[span, column : column + 1] = jnp.sum(eye(slots) * side_r, axis=-1, keepdims=True)

    def block(index, carry):
        if loads:
            column_load(index).wait()
        span = pl.ds(pl.multiple_of(index * width, width), width)
        u = dot(rows_ref[...], up_ref[:, span], (1, 0))
        square = u * u
        tanh_val = jnp.tanh(gelu_coef * (u + cubic_coef * square * u))
        half = 0.5 * (1.0 + tanh_val)
        act_ref[:, span] = (u * half).astype(BF16)
        slope = half + 0.5 * u * (1.0 - tanh_val * tanh_val) * (gelu_coef * (1.0 + 3.0 * cubic_coef * square))
        slope_ref[:, span] = (slope * side_ref[:, 0:1]).astype(BF16)
        return carry

    lax.fori_loop(0, blocks, block, 0)
    if loads:
        down_load.wait()


def back_kernel(shards, slices, slots, width, base, stage, keep, has_prev, spans, place, *refs):
    refs = list(refs)
    take = lambda n: [refs.pop(0) for _ in range(n)]
    reached = place[1] + stage >= place[2]
    own_in = take(2 if has_prev else 1)
    gather_ref = take(1)[0]
    recv_in = take(shards - 1)
    prev_ref = take(1)[0] if has_prev else None
    up_ref, down_ref = take(2)
    act_refs, slope_refs = take(len(spans)), take(len(spans))
    row_refs, side_refs = (take(len(spans)), take(len(spans))) if keep else ([], [])
    gain_ref, router_ref = take(2) if keep else (None, None)
    own_out = None if keep else take(1)[0]
    cot_ref = take(1)[0]
    q_refs = take(len(spans)) if keep else []
    acc_ref = take(1)[0] if keep else None
    parts = [] if keep else take(shards)
    q_ref = refs[0]
    own = own_in[0][...]
    if has_prev:
        own = (own.astype(F32) + own_in[1][...].astype(F32)).astype(BF16)
    if not keep:
        own_out[...] = own
    cot_ref[0:slots, :] = dot(gather_ref[0], own, (1, 0)).astype(BF16)
    for place_at in range(1, shards):
        rows = slice(place_at * slots, (place_at + 1) * slots)
        value = recv_in[place_at - 1][base : base + slots, :]
        if has_prev:
            value = (value.astype(F32) + prev_ref[rows, :].astype(F32)).astype(BF16)
        cot_ref[rows, :] = value

    @pl.when(reached)
    def _():
        hidden, feat = down_ref.shape
        lanes = 128

        def block(index, combs):
            span = pl.ds(pl.multiple_of(index * width, width), width)
            t_all = dot(cot_ref[...], down_ref[span, :], (1, 1))
            out = []
            for which, (low, high) in enumerate(spans):
                t = t_all[low:high, :]
                prod = act_refs[which][:, span].astype(F32) * t
                comb = combs[which]
                for start in range(0, width, lanes):
                    comb = comb + prod[:, start : start + lanes]
                out.append(comb)
                q = (slope_refs[which][:, span].astype(F32) * t).astype(BF16)
                q_ref[low:high, span] = q
                if keep:
                    q_refs[which][:, span] = q
            return tuple(out)

        combs = lax.fori_loop(
            0, hidden // width, block, tuple(jnp.zeros((high - low, lanes), F32) for low, high in spans)
        )
        wide = min(FEAT_WIDTH, feat)
        if keep:
            experts = router_ref.shape[0]
            expert = place[0] // slices
            acc_ref[...] = jnp.zeros_like(acc_ref)
            routed = jnp.zeros((experts, feat), F32)
            for which, (low, high) in enumerate(spans):
                comb_c = jnp.sum(combs[which], axis=-1, keepdims=True)
                ids = iota((high - low, experts), 1)
                other = side_refs[which][:, 3:4]
                pull = jnp.where(ids == expert, comb_c * side_refs[which][:, 1:2], 0.0)
                pull = pull + jnp.where(ids.astype(F32) == other, comb_c * side_refs[which][:, 2:3], 0.0)
                routed = routed + lax.dot_general(
                    pull, row_refs[which][...].astype(F32), (((0,), (0,)), ((), ())),
                    preferred_element_type=F32, precision=lax.Precision.HIGHEST,
                )
            acc_ref[0:experts, :] = routed
        for start in range(0, feat, wide):
            cols = slice(start, start + wide)
            term = dot(q_ref[...], up_ref[cols, :], (1, 1))
            if keep:
                gained = jnp.sum(routed[:, cols] * router_ref[:, cols], axis=0, keepdims=True)
                for which, (low, high) in enumerate(spans):
                    rows = row_refs[which][:, cols].astype(F32)
                    gained = gained + jnp.sum(term[low:high, :] * rows, axis=0, keepdims=True)
                acc_ref[experts : experts + 1, cols] = gained / gain_ref[:, cols]
            for index, part in enumerate(parts):
                part[0:slots, cols] = term[index * slots : (index + 1) * slots, :].astype(BF16)
        for which, (low, high) in enumerate([] if keep else spans):
            comb_c = jnp.sum(combs[which], axis=-1, keepdims=True)
            for index in range(low // slots, high // slots):
                part = parts[index]
                mine = comb_c[index * slots - low : (index + 1) * slots - low, :]
                comb_r = jnp.sum(eye(slots) * mine, axis=0, keepdims=True)
                part[slots : slots + AUX, :] = jnp.zeros((AUX, feat), BF16)
                part[slots : slots + AUX, 0:slots] = jnp.broadcast_to(comb_r, (AUX, slots)).astype(BF16)


def owner_kernel(shards, slices, slots, stage, place, *refs):
    parts = refs[:shards]
    own_ref, x_ref, gain_ref, router_ref, score_ref, scatter_ref, gather_ref = refs[shards : shards + 7]
    own_out, sends = refs[shards + 7], refs[shards + 8 :]
    me = place[0]

    @pl.when(place[1] == place[2] - stage)
    def _():
        experts = router_ref.shape[0]
        total = x_ref.shape[0]
        ids = iota((total, experts), 1)
        gh = jnp.zeros(x_ref.shape, F32)
        comb = jnp.zeros((total, experts), F32)
        for step in range(shards):
            expert = lax.rem(me + step, shards) // slices
            scatter = scatter_ref[step]
            gh = gh + dot(scatter, parts[step][0:slots, :], (1, 0))
            comb_r = parts[step][slots : slots + AUX, 0:slots].astype(F32)[0:1, :]
            comb_c = jnp.sum(scatter.astype(F32) * comb_r, axis=-1, keepdims=True)
            comb = comb + comb_c * (ids == expert).astype(F32)
        scores, weights, hits, totals = (score_ref[i] for i in range(4))
        center_comb = jnp.sum(weights * comb, axis=-1, keepdims=True)
        logit_grad = hits * (comb - center_comb) / totals * (scores * (1.0 - scores))
        for expert in range(experts):
            gh = gh + logit_grad[:, expert : expert + 1] * router_ref[expert : expert + 1, :]
        x = x_ref[...].astype(F32)
        inverse = row_norm(x)
        normed = x * inverse
        scaled = gh * gain_ref[...]
        center = jnp.mean(scaled * normed, axis=-1, keepdims=True)
        gx = (own_ref[...].astype(F32) + inverse * (scaled - normed * center)).astype(BF16)
        own_out[...] = gx
        for step in range(1, shards):
            sends[step - 1][...] = dot(gather_ref[step], gx, (1, 0)).astype(BF16)


def up_kernel(count, *refs):
    rows, qs = refs[:count], refs[count : 2 * count]
    out_ref = refs[2 * count]
    turned = refs[2 * count + 1 :]

    @pl.when(pl.program_id(0) == 0)
    def _():
        for index in range(count):
            turned[index][...] = rows[index][...].astype(F32).T.astype(BF16)

    total = dot(turned[0][...], qs[0][...], (1, 0))
    for index in range(1, count):
        total = total + dot(turned[index][...], qs[index][...], (1, 0))
    out_ref[...] = total.astype(BF16)


def down_kernel(spans, cot_ref, *refs):
    count = len(spans)
    sides, acts = (refs[i * count : (i + 1) * count] for i in range(2))
    out_ref = refs[2 * count]
    y_refs = refs[2 * count + 1 :]

    @pl.when(pl.program_id(0) == 0)
    def _():
        for index in range(count):
            cots = cot_ref[spans[index][0] : spans[index][1], :].astype(F32)
            y_refs[index][...] = (sides[index][:, 0:1] * cots).astype(BF16)

    total = dot(acts[0][...], y_refs[0][...], (0, 0))
    for index in range(1, count):
        total = total + dot(acts[index][...], y_refs[index][...], (0, 0))
    out_ref[...] = total.astype(BF16)


def finish_kernel(shards, experts, *refs):
    total = refs[0][...]
    for ref in refs[1:shards]:
        total = total + ref[...]
    refs[shards][...] = total[0:experts, :]
    refs[shards + 1][...] = total[experts : experts + 1, :]


def body(
    layer_inputs, out_cotangent, expert_routes, norm_gain, router_weight, up_weight, down_weight
):
    sections = lax.axis_size("section")
    section_id = lax.axis_index("section")
    shards = lax.axis_size("expert")
    shard_id = lax.axis_index("expert")
    micro, rows, feat = layer_inputs.shape[1:]
    router = router_weight[0]
    experts = router.shape[0]
    up = up_weight[0]
    down = down_weight[0]
    hidden = up.shape[1]
    slices = shards // experts
    total = micro * rows
    cap = rows // BLOCK_ROWS * BLOCK_CAP if rows % BLOCK_ROWS == 0 else rows
    slots = micro * cap
    sent = slots + AUX
    last = sections - 1
    x = layer_inputs[0].reshape(total, feat)
    cot = out_cotangent.reshape(total, feat)
    chosen = lax.dynamic_slice_in_dim(expert_routes[0], shard_id * rows, rows, 1).reshape(total, 2)
    gain = norm_gain
    place = jnp.stack([shard_id, section_id, jnp.int32(last)]).astype(jnp.int32)
    steps = list(range(shards))
    split = max(1, shards // 2)
    chunks = [steps[:split], steps[split:]]
    chunks = [chunk for chunk in chunks if chunk]
    width = min(1024, hidden)
    blocks = hidden // width

    def sds(shape, dtype=BF16):
        return jax.ShapeDtypeStruct(shape, dtype)

    def move(value, pairs):
        flat = [(sz * sections + ss, dz * sections + ds) for (ss, sz), (ds, dz) in pairs]
        return lax.ppermute(value, ("expert", "section"), flat)

    def spread(value, step, sources, drop):
        return move(
            value,
            [((s, z), (s - drop, (z + step) % shards)) for s in sources for z in range(shards) if s - drop >= 0],
        )

    def any_place():
        return pl.BlockSpec(memory_space=pl.ANY)

    everyone = list(range(sections))
    far = [pltpu.with_memory_space_constraint(array, pltpu.HBM) for array in (x, cot, gain, router, up, down)]
    hbm = pl.BlockSpec(memory_space=pltpu.HBM)
    prep = pl.pallas_call(
        functools.partial(prep_kernel, shards, slices, rows, slots, cap),
        out_shape=[sds((sent, feat))] * shards
        + [sds((sent + slots, feat))] * (shards - 1)
        + [sds((shards, slots, total)), sds((shards, total, slots)), sds((4, total, experts), F32), sds((total, feat))],
        in_specs=[smem()] + [hbm] * 4 + [vmem()] * 2,
        out_specs=[vmem()] * (2 * shards + 3),
        scratch_shapes=[pltpu.VMEM((total, feat), BF16)] * 2
        + [pltpu.VMEM(gain.shape, F32), pltpu.VMEM(router.shape, F32), pltpu.SemaphoreType.DMA((4,))],
        compiler_params=params(),
        cost_estimate=cost(1e7, 4e6),
        name="prep",
    )(place, *far[:4], chosen, chosen.T)
    h_send, c_send = prep[:shards], [None] + list(prep[shards : 2 * shards - 1])
    gather, scatter, score, own = prep[2 * shards - 1 :]
    first_recv = [None] + [spread(c_send[step], step, [last], 0) for step in steps[1:]]
    h_recv = [None] + [spread(h_send[step], step, everyone[:-1], 0) for step in steps[1:]]
    gather_next = move(gather, [((s - 1, z), (s, z)) for s in everyone[1:] for z in range(shards)])
    def const(block):
        return pl.BlockSpec(block, lambda i: (0,) * len(block))

    def chunk_rows(chunk):
        return len(chunk) * slots

    def col_block(chunk):
        return pl.BlockSpec((chunk_rows(chunk), width), lambda i: (0, i))

    def forward(chunk, after, near):
        count = chunk_rows(chunk)
        own_part = 1 if chunk[0] == 0 else 0
        args = [after] + [h_send[0]] * own_part
        for step in chunk[own_part:]:
            args += [first_recv[step], h_recv[step]]
        specs = [any_place()] + [vmem()] * (len(args) - 1)
        args += [near[0]] if near else far[4:]
        specs += [vmem()] if near else [hbm] * 2
        return pl.pallas_call(
            functools.partial(forward_kernel, slots, width, not near, own_part, len(chunk) - own_part),
            out_shape=[sds((count, hidden))] * 2
            + [sds((count, feat)), sds((count, SIDES), F32)]
            + ([] if near else [pltpu.VMEM(up.shape, BF16), pltpu.VMEM(down.shape, BF16)]),
            in_specs=specs,
            out_specs=[vmem()] * (4 if near else 6),
            scratch_shapes=[] if near else [pltpu.SemaphoreType.DMA((blocks + 1,))],
            compiler_params=params(),
            cost_estimate=cost(2 * count * feat * hidden, 2 * feat * hidden),
            name="forward",
        )(*args)

    def back(stage, recv, base, own_recv, own, prev):
        has_prev = prev is not None
        keep = stage == last
        args = [place] + ([own_recv, own] if has_prev else [own]) + [gather]
        args += [recv[step] for step in steps[1:]]
        if has_prev:
            args += [prev]
        args += near + [k[0] for k in kept] + [k[1] for k in kept]
        if keep:
            args += [k[2] for k in kept] + [k[3] for k in kept] + [gain, router]
        every = shards * slots
        outs = pl.pallas_call(
            functools.partial(back_kernel, shards, slices, slots, width, base, stage, keep, has_prev, spans),
            out_shape=([] if keep else [sds((total, feat))])
            + [sds((every, feat))]
            + ([sds((chunk_rows(chunk), hidden)) for chunk in chunks] if keep else [])
            + ([sds((-(-(experts + 1) // 8) * 8, feat), F32)] if keep else [sds((sent, feat))] * shards),
            in_specs=[smem()] + [vmem()] * (len(args) - 1),
            out_specs=[vmem()] * (2 + len(chunks) if keep else 2 + shards),
            scratch_shapes=[pltpu.VMEM((every, hidden), BF16)],
            compiler_params=params(),
            cost_estimate=cost(4 * every * feat * hidden, 4 * feat * hidden),
            name="back",
        )(*args)
        return list(outs)

    spans = [(chunk[0] * slots, (chunk[-1] + 1) * slots) for chunk in chunks]
    count = len(chunks)
    kept, near = [], []
    after = gather_next
    for chunk in chunks:
        outs = forward(chunk, after, near)
        kept.append(outs[:4])
        after = outs[3]
        if not near:
            near = [pltpu.with_memory_space_constraint(array, pltpu.VMEM) for array in outs[4:]]
    recv, base, own_recv, prev = first_recv, sent, None, None
    for stage in range(last):
        own, prev, *parts = back(stage, recv, base, own_recv, own, prev)
        section = last - stage
        partial = [parts[0]] + [spread(parts[step], -step, [section], 0) for step in steps[1:]]
        outs = pl.pallas_call(
            functools.partial(owner_kernel, shards, slices, slots, stage),
            out_shape=[sds((total, feat))] + [sds((slots, feat))] * (shards - 1),
            in_specs=[smem()] + [vmem()] * (shards + 7),
            out_specs=[vmem()] * shards,
            compiler_params=params(),
            cost_estimate=cost(1e7, 4e6),
            name="owner",
        )(place, *partial, own, x, gain, router, score, scatter, gather_next)
        own_recv = spread(outs[0], 0, [section], 1)
        recv = [None] + [spread(outs[step], step, [section], 1) for step in steps[1:]]
        base = 0
    cots, *qs, acc = back(last, recv, base, own_recv, own, prev)
    sums = [acc] + [spread(acc, step, everyone, 0) for step in steps[1:]]
    up_grad = pl.pallas_call(
        functools.partial(up_kernel, count),
        grid=(blocks,),
        out_shape=sds((feat, hidden)),
        in_specs=[const((chunk_rows(c), feat)) for c in chunks] + [col_block(c) for c in chunks],
        out_specs=pl.BlockSpec((feat, width), lambda i: (0, i)),
        scratch_shapes=[pltpu.VMEM((feat, chunk_rows(c)), BF16) for c in chunks],
        compiler_params=params(24),
        cost_estimate=cost(2 * shards * slots * feat * hidden, 2 * feat * hidden),
        name="up_grad",
    )(*[k[2] for k in kept], *qs)
    down_grad = pl.pallas_call(
        functools.partial(down_kernel, spans),
        grid=(blocks,),
        out_shape=sds((hidden, feat)),
        in_specs=[const(cots.shape)]
        + [const((chunk_rows(c), SIDES)) for c in chunks]
        + [col_block(c) for c in chunks],
        out_specs=pl.BlockSpec((width, feat), lambda i: (i, 0)),
        scratch_shapes=[pltpu.VMEM((chunk_rows(c), feat), BF16) for c in chunks],
        compiler_params=params(24),
        cost_estimate=cost(2 * shards * slots * feat * hidden, 2 * feat * hidden),
        name="down_grad",
    )(cots, *[k[3] for k in kept], *[k[0] for k in kept])
    router_grad, gain_grad = pl.pallas_call(
        functools.partial(finish_kernel, shards, experts),
        out_shape=[sds((experts, feat), F32), sds((1, feat), F32)],
        in_specs=[vmem()] * shards,
        out_specs=[vmem()] * 2,
        compiler_params=params(),
        name="finish",
    )(*sums)
    return (up_grad[None], down_grad[None], router_grad[None], gain_grad)


def solution(mesh):
    in_specs = (
        P("section", None, ("groups", "expert"), None),
        P(None, ("groups", "expert"), None),
        P("section", None, "groups", None),
        P("section", None),
        P("section", None, None),
        P("section", None, "expert"),
        P("section", "expert", None),
    )
    out_specs = (
        P("section", "groups", "expert"),
        P("section", "expert", "groups"),
        P("section", "groups", None),
        P("section", "groups"),
    )
    return jax.shard_map(body, mesh=mesh, in_specs=in_specs, out_specs=out_specs, check_vma=False)
```

time: 189 us -> 172 us (0.910)
  starting transfers between devices: 45 us -> 36.8 us
  Pallas kernels: 47.5 us -> 39.8 us
    ppermute x34 -> x31, starting transfers between devices: 45 us -> 36.8 us  [move(): return lax.ppermute(value, ('expert', 'section'), flat)]
    pallas_call x11 -> x7, Pallas kernels: 32.8 us -> 27.7 us  [the longest x4 11 us: back(): pl.pallas_call(functools.partial(back_kernel, shards, slices, slots, widt...]
    ppermute x34 -> x31, waiting for transfers between devices: 91.8 us -> 92.9 us  [move(): return lax.ppermute(value, ('expert', 'section'), flat)]
  transfers between devices with their start and end apart: 34 -> 31, of which waited for: 3 -> 4; matrix products, arithmetic and copies ran while one was open for 0% -> 0% of each run, Pallas kernels for 20% -> 12%
where the time goes in v2:
time: 172 us
  waiting for transfers between devices  92.9 us (54%)
  Pallas kernels  39.8 us (23%)
  starting transfers between devices  36.8 us (21%)
    ppermute x31, waiting for transfers between devices, move(): return lax.ppermute(value, ('expert', 'section'), flat)  92.9 us
    ppermute x31, starting transfers between devices, move(): return lax.ppermute(value, ('expert', 'section'), flat)  36.8 us
    pallas_call x4, Pallas kernels, back(): pl.pallas_call(functools.partial(back_kernel, shards, slices, slots, widt...  11 us
    pallas_call x2, Pallas kernels, forward(): pl.pallas_call(functools.partial(forward_kernel, slots, width, not near,...  9.78 us
    pallas_call x1, Pallas kernels, body(): pl.pallas_call(functools.partial(down_kernel, spans), grid=(blocks,), out...  6.94 us
    pallas_call x1, Pallas kernels, body(): pl.pallas_call(functools.partial(up_kernel, count), grid=(blocks,), out_s...  6.89 us
  transfers between devices with their start and end apart: 31, of which 4 were waited for; matrix products, arithmetic and copies ran while one was open for 0% of the time, Pallas kernels for 12%

profile of v2, /device:TPU:0, one launch (start us, length us, event | category | flops | bytes accessed | tf_op | source)
XLA Modules:
  0.0 171.8 jit_solution(14751137376074450575)
XLA Ops:
  0.6 0.0 copy-start
  0.7 0.7 copy-done
  1.3 0.1 constant_dynamic-slice_fusion
  1.4 0.1 reshape.17
  1.5 0.1 copy.12.col_ref
  1.6 0.1 pad_add_fusion.place
  1.7 3.0 %prep.1 = (bf16[88,1024]{1,0:T(8,128)(2,1)S(1)}, bf16[88,1024]{1,0:T(8,128)(2,1)S(1)}, bf16[88,1024]{1,0:T(8,128)(2,1)S(1)}, bf16[88,1024]{1,0:T(8,128)(2,1)S(1)...) custom-call(s32[3]{0:T(128)S(1)} %pad_add_fusion.place, ...), custom_call_target="tpu_custom_call" | custom-call | flops 10000000 | bytes 4000000 | tf_op jit(solution)/shard_map/prep/pallas_call | solution.py:409
  4.7 0.7 collective-permute-start.1
  5.4 5.0 %collective-permute-start.2 = (bf16[88,1024]{1,0:T(8,128)(2,1)S(1)}, bf16[88,1024]{1,0:T(8,128)(2,1)S(1)}, u32[]{:S(2)}, u32[]{:S(2)}) collective-permute-start(bf16[88,1024]{1,0:T(8,128)(2,1)S(1)} %get-tuple-element.64), channel_id=1, source_target_pairs={{0,4},{4,8},{8,12},{12,0},{1,5},{5,9},{9,13},{13,1},{2,6},{6,10},{... | collective-permute-start | bytes 540680 | tf_op jit(solution)/shard_map/ppermute | solution.py:395
  10.3 0.7 collective-permute-start.3
  11.0 0.7 collective-permute-start.5
  11.7 1.5 collective-permute-start
  13.2 0.9 collective-permute-done.refs_0_.refs_10_
  14.1 4.5 %collective-permute-start.4 = (bf16[88,1024]{1,0:T(8,128)(2,1)S(1)}, bf16[88,1024]{1,0:T(8,128)(2,1)S(1)}, u32[]{:S(2)}, u32[]{:S(2)}) collective-permute-start(bf16[88,1024]{1,0:T(8,128)(2,1)S(1)} %get-tuple-element.68), channel_id=1, source_target_pairs={{0,8},{4,12},{8,0},{12,4},{1,9},{5,13},{9,1},{13,5},{2,10},{6,14},... | collective-permute-start | bytes 540680 | tf_op jit(solution)/shard_map/ppermute | solution.py:395
  18.6 3.3 %collective-permute-start.6 = (bf16[88,1024]{1,0:T(8,128)(2,1)S(1)}, bf16[88,1024]{1,0:T(8,128)(2,1)S(1)}, u32[]{:S(2)}, u32[]{:S(2)}) collective-permute-start(bf16[88,1024]{1,0:T(8,128)(2,1)S(1)} %get-tuple-element.70), channel_id=1, source_target_pairs={{0,12},{4,0},{8,4},{12,8},{1,13},{5,1},{9,5},{13,9},{2,14},{6,2},{... | collective-permute-start | bytes 540680 | tf_op jit(solution)/shard_map/ppermute | solution.py:395
  21.8 0.0 collective-permute-done.1.refs_2_
  21.9 6.0 %forward.2 = (bf16[160,4096]{1,0:T(8,128)(2,1)S(1)}, bf16[160,4096]{1,0:T(8,128)(2,1)S(1)}, bf16[160,1024]{1,0:T(8,128)(2,1)S(1)}, f32[160,4]{1,0:T(8,128)S(1)},...) custom-call(bf16[4,80,128]{2,1,0:T(8,128)(2,1)S(1)} %collective-permute-done.refs_0_.refs_10_, ...), custom_call_target="tpu_custom_call" | custom-call | flops 1342177280 | bytes 8388608 | tf_op jit(solution)/shard_map/forward/pallas_call | solution.py:445
  27.9 0.0 collective-permute-done.4.refs_2_
  27.9 2.0 %collective-permute-done.6.refs_4_ = bf16[88,1024]{1,0:T(8,128)(2,1)S(1)} collective-permute-done((bf16[88,1024]{1,0:T(8,128)(2,1)S(1)}, bf16[88,1024]{1,0:T(8,128)(2,1)S(1)}, u32[]{:S(2)}, u32[]{:S(2)}) %collective-permute-start.6) | collective-permute-done | bytes 180256 | tf_op jit(solution)/shard_map/ppermute | solution.py:395
  29.9 0.0 collective-permute-done.3.refs_1_.refs_3_
  29.9 0.0 collective-permute-done.5.refs_3_.refs_4_
  29.9 3.8 %forward.3 = (bf16[160,4096]{1,0:T(8,128)(2,1)S(1)}, bf16[160,4096]{1,0:T(8,128)(2,1)S(1)}, bf16[160,1024]{1,0:T(8,128)(2,1)S(1)}, f32[160,4]{1,0:T(8,128)S(1)}) custom-call(f32[160,4]{1,0:T(8,128)S(1)} %get-tuple-element.66.refs_0_.refs_15_, bf16[168,1024]{1,0:T(8,128)(2,1)S(1)} %collective-permute-done.3.refs_1_.refs_3_, ...), custom_call_target="tpu_custom_call" | custom-call | flops 1342177280 | bytes 8388608 | tf_op jit(solution)/shard_map/forward/pallas_call | solution.py:445
  33.7 0.0 copy-start.2
  33.7 0.0 copy-start.3
  33.7 0.0 copy-start.4
  33.7 0.7 back.4
  34.5 0.7 collective-permute-start.7
  35.2 0.7 collective-permute-start.8
  35.8 0.7 collective-permute-start.9
  36.5 0.0 collective-permute-done.7.refs_1_
  36.5 0.0 collective-permute-done.8.refs_2_
  36.6 0.6 owner.3
  37.1 0.7 collective-permute-start.10
  37.8 0.7 collective-permute-start.11
  38.5 0.7 collective-permute-start.12
  39.2 0.7 collective-permute-start.13
  39.9 0.0 collective-permute-done.12.refs_4_
  39.9 0.9 back.5
  40.8 0.7 collective-permute-start.14
  41.5 0.9 collective-permute-start.15
  42.3 0.7 collective-permute-start.16
  43.0 0.6 owner.4
  43.6 0.7 collective-permute-start.17
  44.3 0.7 collective-permute-start.18
  45.0 0.7 collective-permute-start.19
  45.6 0.7 collective-permute-start.20
  46.4 0.9 back.6
  47.2 0.7 collective-permute-start.21
  47.9 0.7 collective-permute-start.22
  48.6 0.7 collective-permute-start.23
  49.3 0.6 owner.5
  49.9 1.3 collective-permute-start.24
  51.2 1.3 collective-permute-start.25
  52.5 1.3 collective-permute-start.26
  53.8 1.3 collective-permute-start.27
  55.1 86.6 %collective-permute-done.25.refs_3_ = bf16[80,1024]{1,0:T(8,128)(2,1)S(1)} collective-permute-done((bf16[80,1024]{1,0:T(8,128)(2,1)S(1)}, bf16[80,1024]{1,0:T(8,128)(2,1)S(1)}, u32[]{:S(2)}, u32[]{:S(2)}) %collective-permute-start.25) | collective-permute-done | bytes 163872 | tf_op jit(solution)/shard_map/ppermute | solution.py:395
  141.6 3.3 %collective-permute-done.26.refs_4_ = bf16[80,1024]{1,0:T(8,128)(2,1)S(1)} collective-permute-done((bf16[80,1024]{1,0:T(8,128)(2,1)S(1)}, bf16[80,1024]{1,0:T(8,128)(2,1)S(1)}, u32[]{:S(2)}, u32[]{:S(2)}) %collective-permute-start.26) | collective-permute-done | bytes 163872 | tf_op jit(solution)/shard_map/ppermute | solution.py:395
  145.0 8.5 %back.7 = (bf16[320,1024]{1,0:T(8,128)(2,1)S(1)}, bf16[160,4096]{1,0:T(8,128)(2,1)S(1)}, bf16[160,4096]{1,0:T(8,128)(2,1)S(1)}, f32[8,1024]{1,0:T(8,128)S(1)}) custom-call(s32[3]{0:T(128)S(1)} %pad_add_fusion.place, bf16[128,1024]{1,0:T(8,128)(2,1)S(1)} %collective-permute-done.24.refs_0_, bf16[128,1024]{1,0:T(8,128)(2,1)S(1)} %get-tuple-element.105.refs_4_.refs_1_, ...), custom_call_target="tpu_custom_call" | custom-call | flops 5368709120 | bytes 16777216 | tf_op jit(solution)/shard_map/back/pallas_call | solution.py:469
  153.5 1.7 collective-permute-start.30
  155.2 2.1 %collective-permute-start.29 = (f32[8,1024]{1,0:T(8,128)S(1)}, f32[8,1024]{1,0:T(8,128)S(1)}, u32[]{:S(2)}, u32[]{:S(2)}) collective-permute-start(f32[8,1024]{1,0:T(8,128)S(1)} %get-tuple-element.115.refs_0_), channel_id=1, source_target_pairs={{0,8},{4,12},{8,0},{12,4},{1,9},{5,13},{9,1},{13,5},{2,10},{6,14},... | collective-permute-start | bytes 98312 | tf_op jit(solution)/shard_map/ppermute | solution.py:395
  157.3 0.0 collective-permute-start.28
  157.3 6.9 %down_grad.1 = bf16[4096,1024]{1,0:T(8,128)(2,1)} custom-call(bf16[320,1024]{1,0:T(8,128)(2,1)S(1)} %get-tuple-element.114.cot_ref, f32[160,4]{1,0:T(8,128)S(1)} %get-tuple-element.66.refs_0_.refs_15_, f32[160,4]{1,0:T(8,128)S(1)} %get-tuple-element.111.refs_16_.refs_1_, bf16[160,4096]{1,0:T(8,128)(2,1)S(1)} %get-tuple-element.75.refs_7_.refs_9_.refs_2_, ...), custom_call_target="tpu_custom_call" | custom-call | flops 2684354560 | bytes 8388608 | tf_op jit(solution)/shard_map/down_grad/pallas_call | solution.py:524
  164.3 6.9 %up_grad.1 = bf16[1024,4096]{1,0:T(8,128)(2,1)} custom-call(bf16[160,1024]{1,0:T(8,128)(2,1)S(1)} %get-tuple-element.65.refs_13_.refs_0_, bf16[160,1024]{1,0:T(8,128)(2,1)S(1)} %get-tuple-element.72.refs_14_.refs_1_, bf16[160,4096]{1,0:T(8,128)(2,1)S(1)} %get-tuple-element.112.refs_2_, bf16[160,4096]{1,0:T(8,128)(2,1)S(1)} %get-tuple-element.113.refs_3_), custom_call_target="tpu_custom_call" | custom-call | flops 2684354560 | bytes 8388608 | tf_op jit(solution)/shard_map/up_grad/pallas_call | solution.py:513
  171.2 0.6 finish.1
  (26 shorter events, 0.1 us)
Async XLA Ops:
  0.6 0.7 copy-start
  4.7 17.2 %collective-permute-start.1 = (bf16[168,1024]{1,0:T(8,128)(2,1)S(1)}, bf16[168,1024]{1,0:T(8,128)(2,1)S(1)}, u32[]{:S(2)}, u32[]{:S(2)}) collective-permute-start(bf16[168,1024]{1,0:T(8,128)(2,1)S(1)} %get-tuple-element.63), channel_id=1, source_target_pairs={{3,7},{7,11},{11,15},{15,3},{19,23},{23,27},{27,31},{31,19}} | collective-permute-start | bytes 1032200 | tf_op jit(solution)/shard_map/ppermute | solution.py:395
  5.4 13.2 %collective-permute-start.2 = (bf16[88,1024]{1,0:T(8,128)(2,1)S(1)}, bf16[88,1024]{1,0:T(8,128)(2,1)S(1)}, u32[]{:S(2)}, u32[]{:S(2)}) collective-permute-start(bf16[88,1024]{1,0:T(8,128)(2,1)S(1)} %get-tuple-element.64), channel_id=1, source_target_pairs={{0,4},{4,8},{8,12},{12,0},{1,5},{5,9},{9,13},{13,1},{2,6},{6,10},{... | collective-permute-start | bytes 540680 | tf_op jit(solution)/shard_map/ppermute | solution.py:395
  10.3 19.6 %collective-permute-start.3 = (bf16[168,1024]{1,0:T(8,128)(2,1)S(1)}, bf16[168,1024]{1,0:T(8,128)(2,1)S(1)}, u32[]{:S(2)}, u32[]{:S(2)}) collective-permute-start(bf16[168,1024]{1,0:T(8,128)(2,1)S(1)} %get-tuple-element.67), channel_id=1, source_target_pairs={{3,11},{7,15},{11,3},{15,7},{19,27},{23,31},{27,19},{31,23}} | collective-permute-start | bytes 1032200 | tf_op jit(solution)/shard_map/ppermute | solution.py:395
  11.0 18.9 %collective-permute-start.5 = (bf16[168,1024]{1,0:T(8,128)(2,1)S(1)}, bf16[168,1024]{1,0:T(8,128)(2,1)S(1)}, u32[]{:S(2)}, u32[]{:S(2)}) collective-permute-start(bf16[168,1024]{1,0:T(8,128)(2,1)S(1)} %get-tuple-element.69), channel_id=1, source_target_pairs={{3,15},{7,3},{11,7},{15,11},{19,31},{23,19},{27,23},{31,27}} | collective-permute-start | bytes 1032200 | tf_op jit(solution)/shard_map/ppermute | solution.py:395
  11.7 2.4 %collective-permute-start = (bf16[4,80,128]{2,1,0:T(8,128)(2,1)S(1)}, bf16[4,80,128]{2,1,0:T(8,128)(2,1)S(1)}, u32[]{:S(2)}, u32[]{:S(2)}) collective-permute-start(bf16[4,80,128]{2,1,0:T(8,128)(2,1)S(1)} %get-tuple-element.61.refs_1_.refs_2_), channel_id=1, source_target_pairs={{0,1},{4,5},{8,9},{12,13},{1,2},{5,6},{9,10},{13,14},{2,3},{6,7},{... | collective-permute-start | bytes 245768 | tf_op jit(solution)/shard_map/ppermute | solution.py:395
  14.1 13.8 %collective-permute-start.4 = (bf16[88,1024]{1,0:T(8,128)(2,1)S(1)}, bf16[88,1024]{1,0:T(8,128)(2,1)S(1)}, u32[]{:S(2)}, u32[]{:S(2)}) collective-permute-start(bf16[88,1024]{1,0:T(8,128)(2,1)S(1)} %get-tuple-element.68), channel_id=1, source_target_pairs={{0,8},{4,12},{8,0},{12,4},{1,9},{5,13},{9,1},{13,5},{2,10},{6,14},... | collective-permute-start | bytes 540680 | tf_op jit(solution)/shard_map/ppermute | solution.py:395
  18.6 11.3 %collective-permute-start.6 = (bf16[88,1024]{1,0:T(8,128)(2,1)S(1)}, bf16[88,1024]{1,0:T(8,128)(2,1)S(1)}, u32[]{:S(2)}, u32[]{:S(2)}) collective-permute-start(bf16[88,1024]{1,0:T(8,128)(2,1)S(1)} %get-tuple-element.70), channel_id=1, source_target_pairs={{0,12},{4,0},{8,4},{12,8},{1,13},{5,1},{9,5},{13,9},{2,14},{6,2},{... | collective-permute-start | bytes 540680 | tf_op jit(solution)/shard_map/ppermute | solution.py:395
  33.7 2.8 %copy-start.2 = (bf16[1,2,64,1024]{3,2,1,0:T(8,128)(2,1)S(1)}, bf16[1,2,64,1024]{3,2,1,0:T(8,128)(2,1)}, u32[]{:S(2)}) copy-start(bf16[1,2,64,1024]{3,2,1,0:T(8,128)(2,1)} %param.7) | copy-start | bytes 786436
  33.7 2.8 %copy-start.3 = (f32[1,4,1024]{2,1,0:T(4,128)S(1)}, f32[1,4,1024]{2,1,0:T(4,128)}, u32[]{:S(2)}) copy-start(f32[1,4,1024]{2,1,0:T(4,128)} %param.11) | copy-start | bytes 49156
  33.7 2.8 %copy-start.4 = (f32[1,1024]{1,0:T(1,128)S(1)}, f32[1,1024]{1,0:T(1,128)}, u32[]{:S(2)}) copy-start(f32[1,1024]{1,0:T(1,128)} %refs_17_.1) | copy-start | bytes 12292
  34.5 2.0 %collective-permute-start.7 = (bf16[88,1024]{1,0:T(8,128)(2,1)S(1)}, bf16[88,1024]{1,0:T(8,128)(2,1)S(1)}, u32[]{:S(2)}, u32[]{:S(2)}) collective-permute-start(bf16[88,1024]{1,0:T(8,128)(2,1)S(1)} %get-tuple-element.80), channel_id=1, source_target_pairs={{3,15},{7,3},{11,7},{15,11},{19,31},{23,19},{27,23},{31,27}} | collective-permute-start | bytes 540680 | tf_op jit(solution)/shard_map/ppermute | solution.py:395
  35.2 1.4 collective-permute-start.8
  35.8 0.7 collective-permute-start.9
  37.1 2.8 %collective-permute-start.10 = (bf16[128,1024]{1,0:T(8,128)(2,1)S(1)}, bf16[128,1024]{1,0:T(8,128)(2,1)S(1)}, u32[]{:S(2)}, u32[]{:S(2)}) collective-permute-start(bf16[128,1024]{1,0:T(8,128)(2,1)S(1)} %get-tuple-element.86), channel_id=1, source_target_pairs={{3,2},{7,6},{11,10},{15,14},{19,18},{23,22},{27,26},{31,30}} | collective-permute-start | bytes 786440 | tf_op jit(solution)/shard_map/ppermute | solution.py:395
  37.8 2.0 %collective-permute-start.11 = (bf16[80,1024]{1,0:T(8,128)(2,1)S(1)}, bf16[80,1024]{1,0:T(8,128)(2,1)S(1)}, u32[]{:S(2)}, u32[]{:S(2)}) collective-permute-start(bf16[80,1024]{1,0:T(8,128)(2,1)S(1)} %get-tuple-element.87), channel_id=1, source_target_pairs={{3,6},{7,10},{11,14},{15,2},{19,22},{23,26},{27,30},{31,18}} | collective-permute-start | bytes 491528 | tf_op jit(solution)/shard_map/ppermute | solution.py:395
  38.5 1.4 collective-permute-start.12
  39.2 0.7 collective-permute-start.13
  40.8 2.2 %collective-permute-start.14 = (bf16[88,1024]{1,0:T(8,128)(2,1)S(1)}, bf16[88,1024]{1,0:T(8,128)(2,1)S(1)}, u32[]{:S(2)}, u32[]{:S(2)}) collective-permute-start(bf16[88,1024]{1,0:T(8,128)(2,1)S(1)} %get-tuple-element.92), channel_id=1, source_target_pairs={{2,14},{6,2},{10,6},{14,10},{18,30},{22,18},{26,22},{30,26}} | collective-permute-start | bytes 540680 | tf_op jit(solution)/shard_map/ppermute | solution.py:395
  41.5 1.6 collective-permute-start.15
  42.3 0.7 collective-permute-start.16
  43.6 2.8 %collective-permute-start.17 = (bf16[128,1024]{1,0:T(8,128)(2,1)S(1)}, bf16[128,1024]{1,0:T(8,128)(2,1)S(1)}, u32[]{:S(2)}, u32[]{:S(2)}) collective-permute-start(bf16[128,1024]{1,0:T(8,128)(2,1)S(1)} %get-tuple-element.96), channel_id=1, source_target_pairs={{2,1},{6,5},{10,9},{14,13},{18,17},{22,21},{26,25},{30,29}} | collective-permute-start | bytes 786440 | tf_op jit(solution)/shard_map/ppermute | solution.py:395
  44.3 2.0 %collective-permute-start.18 = (bf16[80,1024]{1,0:T(8,128)(2,1)S(1)}, bf16[80,1024]{1,0:T(8,128)(2,1)S(1)}, u32[]{:S(2)}, u32[]{:S(2)}) collective-permute-start(bf16[80,1024]{1,0:T(8,128)(2,1)S(1)} %get-tuple-element.97), channel_id=1, source_target_pairs={{2,5},{6,9},{10,13},{14,1},{18,21},{22,25},{26,29},{30,17}} | collective-permute-start | bytes 491528 | tf_op jit(solution)/shard_map/ppermute | solution.py:395
  45.0 1.4 collective-permute-start.19
  45.6 0.7 collective-permute-start.20
  47.2 2.0 %collective-permute-start.21 = (bf16[88,1024]{1,0:T(8,128)(2,1)S(1)}, bf16[88,1024]{1,0:T(8,128)(2,1)S(1)}, u32[]{:S(2)}, u32[]{:S(2)}) collective-permute-start(bf16[88,1024]{1,0:T(8,128)(2,1)S(1)} %get-tuple-element.102), channel_id=1, source_target_pairs={{1,13},{5,1},{9,5},{13,9},{17,29},{21,17},{25,21},{29,25}} | collective-permute-start | bytes 540680 | tf_op jit(solution)/shard_map/ppermute | solution.py:395
  47.9 1.4 collective-permute-start.22
  48.6 0.7 collective-permute-start.23
  49.9 95.1 %collective-permute-start.24 = (bf16[128,1024]{1,0:T(8,128)(2,1)S(1)}, bf16[128,1024]{1,0:T(8,128)(2,1)S(1)}, u32[]{:S(2)}, u32[]{:S(2)}) collective-permute-start(bf16[128,1024]{1,0:T(8,128)(2,1)S(1)} %get-tuple-element.106), channel_id=1, source_target_pairs={{1,0},{5,4},{9,8},{13,12},{17,16},{21,20},{25,24},{29,28}} | collective-permute-start | bytes 786440 | tf_op jit(solution)/shard_map/ppermute | solution.py:395
  51.2 90.5 %collective-permute-start.25 = (bf16[80,1024]{1,0:T(8,128)(2,1)S(1)}, bf16[80,1024]{1,0:T(8,128)(2,1)S(1)}, u32[]{:S(2)}, u32[]{:S(2)}) collective-permute-start(bf16[80,1024]{1,0:T(8,128)(2,1)S(1)} %get-tuple-element.107), channel_id=1, source_target_pairs={{1,4},{5,8},{9,12},{13,0},{17,20},{21,24},{25,28},{29,16}} | collective-permute-start | bytes 491528 | tf_op jit(solution)/shard_map/ppermute | solution.py:395
  52.5 92.5 %collective-permute-start.26 = (bf16[80,1024]{1,0:T(8,128)(2,1)S(1)}, bf16[80,1024]{1,0:T(8,128)(2,1)S(1)}, u32[]{:S(2)}, u32[]{:S(2)}) collective-permute-start(bf16[80,1024]{1,0:T(8,128)(2,1)S(1)} %get-tuple-element.108), channel_id=1, source_target_pairs={{1,8},{5,12},{9,0},{13,4},{17,24},{21,28},{25,16},{29,20}} | collective-permute-start | bytes 491528 | tf_op jit(solution)/shard_map/ppermute | solution.py:395
  53.8 91.2 %collective-permute-start.27 = (bf16[80,1024]{1,0:T(8,128)(2,1)S(1)}, bf16[80,1024]{1,0:T(8,128)(2,1)S(1)}, u32[]{:S(2)}, u32[]{:S(2)}) collective-permute-start(bf16[80,1024]{1,0:T(8,128)(2,1)S(1)} %get-tuple-element.109), channel_id=1, source_target_pairs={{1,12},{5,0},{9,4},{13,8},{17,28},{21,16},{25,20},{29,24}} | collective-permute-start | bytes 491528 | tf_op jit(solution)/shard_map/ppermute | solution.py:395
  153.5 17.7 %collective-permute-start.30 = (f32[8,1024]{1,0:T(8,128)S(1)}, f32[8,1024]{1,0:T(8,128)S(1)}, u32[]{:S(2)}, u32[]{:S(2)}) collective-permute-start(f32[8,1024]{1,0:T(8,128)S(1)} %get-tuple-element.115.refs_0_), channel_id=1, source_target_pairs={{0,12},{4,0},{8,4},{12,8},{1,13},{5,1},{9,5},{13,9},{2,14},{6,2},{... | collective-permute-start | bytes 98312 | tf_op jit(solution)/shard_map/ppermute | solution.py:395
  155.2 16.0 %collective-permute-start.29 = (f32[8,1024]{1,0:T(8,128)S(1)}, f32[8,1024]{1,0:T(8,128)S(1)}, u32[]{:S(2)}, u32[]{:S(2)}) collective-permute-start(f32[8,1024]{1,0:T(8,128)S(1)} %get-tuple-element.115.refs_0_), channel_id=1, source_target_pairs={{0,8},{4,12},{8,0},{12,4},{1,9},{5,13},{9,1},{13,5},{2,10},{6,14},... | collective-permute-start | bytes 98312 | tf_op jit(solution)/shard_map/ppermute | solution.py:395
  157.3 13.8 %collective-permute-start.28 = (f32[8,1024]{1,0:T(8,128)S(1)}, f32[8,1024]{1,0:T(8,128)S(1)}, u32[]{:S(2)}, u32[]{:S(2)}) collective-permute-start(f32[8,1024]{1,0:T(8,128)S(1)} %get-tuple-element.115.refs_0_), channel_id=1, source_target_pairs={{0,4},{4,8},{8,12},{12,0},{1,5},{5,9},{9,13},{13,1},{2,6},{6,10},{... | collective-permute-start | bytes 98312 | tf_op jit(solution)/shard_map/ppermute | solution.py:395
  157.3 14.5 %copy-start.1 = (s32[1,2,256,2]{2,3,1,0:T(2,128)S(1)}, s32[1,2,256,2]{2,3,1,0:T(2,128)}, u32[]{:S(2)}) copy-start(s32[1,2,256,2]{2,3,1,0:T(2,128)} %param.9) | copy-start | bytes 12292

commit v3 on v2

v3 whole, which is shorter than its diff:
```python
import functools

import jax
import jax.numpy as jnp
from jax import lax
from jax.experimental import pallas as pl
from jax.experimental.pallas import tpu as pltpu
from jax.sharding import PartitionSpec as P


norm_eps = 1e-06
gelu_coef = 0.7978845608028654
cubic_coef = 0.044715
BLOCK_ROWS = 64
BLOCK_CAP = 40
F32 = jnp.float32
BF16 = jnp.bfloat16
AUX = 8
SIDES = 4
FEAT_WIDTH = 512
GRAD_WIDTH = 1024


def vmem():
    return pl.BlockSpec(memory_space=pltpu.VMEM)


def smem():
    return pl.BlockSpec(memory_space=pltpu.SMEM)


def params(mebi=12):
    return pltpu.CompilerParams(vmem_limit_bytes=mebi * 1024 * 1024)


def cost(flops, nbytes):
    return pl.CostEstimate(flops=int(flops), bytes_accessed=int(nbytes), transcendentals=0)


def dot(a, b, dims):
    return lax.dot_general(a, b, ((dims[0:1], dims[1:2]), ((), ())), preferred_element_type=F32)


def iota(shape, dim):
    return lax.broadcasted_iota(jnp.int32, shape, dim)


def row_norm(values):
    mean_sq = jnp.mean(values * values, axis=-1, keepdims=True)
    return lax.rsqrt(mean_sq + norm_eps)


def eye(size):
    return (iota((size, size), 0) == iota((size, size), 1)).astype(F32)


def prep_kernel(
    shards, slices, rows, slots, cap, place, x_far, cot_far, gain_far, router_far, col_ref, row_ref, *outs
):
    x_ref, cot_ref, gain_ref, router_ref, sems = outs[-5:]
    outs = outs[:-5]
    loads = [
        pltpu.make_async_copy(source, target, sems.at[index])
        for index, (source, target) in enumerate([(x_far, x_ref), (cot_far, cot_ref), (gain_far, gain_ref), (router_far, router_ref)])
    ]
    for load in loads:
        load.start()
    for load in loads:
        load.wait()
    h_outs, c_outs = outs[:shards], outs[shards : 2 * shards - 1]
    gather_ref, scatter_ref, own_ref = outs[2 * shards - 1 :]
    me = place[0]
    is_last = place[1] == place[2]
    total = x_ref.shape[0]
    experts = router_ref.shape[0]
    x = x_ref[...].astype(F32)
    h32 = (x * row_norm(x)) * gain_ref[...]
    h = h32.astype(BF16)
    logits = lax.dot_general(
        h.astype(F32), router_ref[...], (((1,), (1,)), ((), ())),
        preferred_element_type=F32, precision=lax.Precision.HIGHEST,
    )
    scores = 1.0 / (1.0 + jnp.exp(-logits))
    ids = iota((total, experts), 1)
    hits = jnp.logical_or(col_ref[:, 0:1] == ids, col_ref[:, 1:2] == ids).astype(F32)
    totals = jnp.sum(scores * hits, axis=-1, keepdims=True)
    weights = scores * hits / totals
    slopes = scores * (1.0 - scores) / totals
    first, second = iota((total, total), 0), iota((total, total), 1)
    same = (first // rows) == (second // rows)
    before = jnp.logical_and(same, second < first).astype(BF16)
    after = jnp.logical_and(same, first < second).astype(BF16)
    base_col = (iota((total, experts), 0) // rows * cap).astype(F32)
    slot_col = jnp.where(hits > 0.0, dot(before, hits.astype(BF16), (1, 0)) + base_col, -1.0)
    ids_row = iota((experts, total), 0)
    hits_row = jnp.logical_or(row_ref[0:1, :] == ids_row, row_ref[1:2, :] == ids_row).astype(F32)
    base_row = (iota((experts, total), 1) // rows * cap).astype(F32)
    slot_row = jnp.where(hits_row > 0.0, dot(hits_row.astype(BF16), after, (1, 0)) + base_row, -1.0)
    cot = cot_ref[...]
    own_ref[...] = jnp.where(is_last, cot.astype(F32), 0.0).astype(BF16)
    slot_lane = iota((total, slots), 1).astype(F32)
    slot_sub = iota((slots, total), 0).astype(F32)
    for step in range(shards):
        expert = lax.rem(me + step, shards) // slices
        mine = (ids == expert).astype(F32)
        slot_c = jnp.sum(slot_col * mine, axis=-1, keepdims=True)
        slot_r = jnp.sum(slot_row * (ids_row == expert).astype(F32), axis=0, keepdims=True)
        scatter = (slot_c == slot_lane).astype(F32)
        gather = (slot_r == slot_sub).astype(F32).astype(BF16)
        weight_c = jnp.sum(weights * mine, axis=-1, keepdims=True)
        rest = hits * (1.0 - mine)
        slope_c = jnp.sum(slopes * mine, axis=-1, keepdims=True)
        slope_o = jnp.sum(slopes * rest, axis=-1, keepdims=True)
        other_c = jnp.sum(ids.astype(F32) * rest, axis=-1, keepdims=True)
        sides = [weight_c, (1.0 - weight_c) * slope_c, 0.0 - weight_c * slope_o, other_c]
        aux = jnp.zeros((AUX, slots), F32)
        aux_id = iota((AUX, slots), 0)
        for index, side in enumerate(sides):
            side_r = jnp.sum(scatter * side, axis=0, keepdims=True)
            high = side_r.astype(BF16).astype(F32)
            aux = jnp.where(aux_id == 2 * index, high, jnp.where(aux_id == 2 * index + 1, side_r - high, aux))
        aux = aux.astype(BF16)
        picked = dot(gather, h, (1, 0)).astype(BF16)
        for target in [h_outs[step]] + ([c_outs[step - 1]] if step else []):
            target[0:slots, :] = picked
            target[slots : slots + AUX, :] = jnp.zeros((AUX, x.shape[1]), BF16)
            target[slots : slots + AUX, 0:slots] = aux
        if step:
            c_outs[step - 1][slots + AUX :, :] = dot(gather, cot, (1, 0)).astype(BF16)
        gather_ref[step] = gather
        scatter_ref[step] = scatter.astype(BF16)


def forward_rows(sources, slots, row0, up_ref, width, outs, ready):
    act_ref, slope_ref, rows_ref, side_ref = outs
    count = len(sources) * slots
    for index, source in enumerate(sources):
        span = slice(row0 + index * slots, row0 + (index + 1) * slots)
        value = source[0 : slots + AUX, :].astype(F32)
        rows_ref[span, :] = value[0:slots, :].astype(BF16)
        for column in range(SIDES):
            low = slots + 2 * column
            side_r = value[low : low + 1, 0:slots] + value[low + 1 : low + 2, 0:slots]
            side_ref[span, column : column + 1] = jnp.sum(eye(slots) * side_r, axis=-1, keepdims=True)
    rows = slice(row0, row0 + count)

    def block(index, carry):
        ready(index)
        span = pl.ds(pl.multiple_of(index * width, width), width)
        u = dot(rows_ref[rows, :], up_ref[:, span], (1, 0))
        square = u * u
        tanh_val = jnp.tanh(gelu_coef * (u + cubic_coef * square * u))
        half = 0.5 * (1.0 + tanh_val)
        act_ref[rows, span] = (u * half).astype(BF16)
        slope = half + 0.5 * u * (1.0 - tanh_val * tanh_val) * (gelu_coef * (1.0 + 3.0 * cubic_coef * square))
        slope_ref[rows, span] = (slope * side_ref[rows, 0:1]).astype(BF16)
        return carry

    lax.fori_loop(0, up_ref.shape[1] // width, block, 0)


def first_kernel(slots, width, parts, place, *refs):
    sources = refs[:parts]
    up_far, down_far = refs[parts : parts + 2]
    outs = refs[parts + 2 : parts + 6]
    up_ref, down_ref, sems = refs[parts + 6 :]
    blocks = up_ref.shape[1] // width
    last = place[1] == place[2]

    def column_load(index):
        span = pl.ds(pl.multiple_of(index * width, width), width)
        return pltpu.make_async_copy(up_far.at[:, span], up_ref.at[:, span], sems.at[index])

    down_load = pltpu.make_async_copy(down_far, down_ref, sems.at[blocks])
    for index in range(blocks):
        column_load(index).start()
    down_load.start()

    @pl.when(last)
    def _():
        forward_rows(sources, slots, 0, up_ref, width, outs, lambda index: column_load(index).wait())

    @pl.when(jnp.logical_not(last))
    def _():
        for index in range(blocks):
            column_load(index).wait()

    down_load.wait()


def second_kernel(slots, width, parts, place, *refs):
    sources = refs[:parts]
    refs = refs[:parts] + refs[parts + 1 :]
    before = refs[parts : parts + 4]
    up_ref = refs[parts + 4]
    outs = refs[parts + 5 :]

    @pl.when(place[1] == place[2])
    def _():
        count = before[0].shape[0]
        for old, new in zip(before, outs):
            new[0:count, :] = old[...]
        forward_rows(sources, slots, count, up_ref, width, outs, lambda index: None)


def third_kernel(slots, width, parts, place, *refs):
    sources = refs[:parts]
    before = refs[parts : parts + 4]
    up_ref = refs[parts + 4]
    outs = refs[parts + 5 :]

    @pl.when(place[1] == place[2])
    def _():
        for old, new in zip(before, outs):
            new[...] = old[...]

    @pl.when(place[1] != place[2])
    def _():
        forward_rows(sources, slots, 0, up_ref, width, outs, lambda index: None)


def back_kernel(shards, slices, slots, width, base, stage, keep, has_prev, place, after, *refs):
    refs = list(refs)
    take = lambda n: [refs.pop(0) for _ in range(n)]
    own_in = take(2 if has_prev else 1)
    gather_ref = take(1)[0]
    recv_in = take(shards - 1)
    prev_ref = take(1)[0] if has_prev else None
    up_ref, down_ref, act_ref, slope_ref, side_ref, router_ref = take(6)
    rows_ref, gain_ref = take(2) if keep else (None, None)
    own_out = None if keep else take(1)[0]
    cot_ref = take(1)[0]
    q_ref, acc_ref = take(2) if keep else (None, None)
    parts = [] if keep else take(shards)
    if not keep:
        q_ref = refs[0]
    own = own_in[0][...]
    if has_prev:
        own = (own.astype(F32) + own_in[1][...].astype(F32)).astype(BF16)
    if not keep:
        own_out[...] = own
    cot_ref[0:slots, :] = dot(gather_ref[0], own, (1, 0)).astype(BF16)
    for index in range(1, shards):
        rows = slice(index * slots, (index + 1) * slots)
        value = recv_in[index - 1][base : base + slots, :]
        if has_prev:
            value = (value.astype(F32) + prev_ref[rows, :].astype(F32)).astype(BF16)
        cot_ref[rows, :] = value

    @pl.when(place[1] + stage >= place[2])
    def _():
        hidden, feat = down_ref.shape
        lanes = 128
        every = cot_ref.shape[0]

        def block(index, comb):
            span = pl.ds(pl.multiple_of(index * width, width), width)
            t = dot(cot_ref[...], down_ref[span, :], (1, 1))
            prod = act_ref[:, span].astype(F32) * t
            for start in range(0, width, lanes):
                comb = comb + prod[:, start : start + lanes]
            q_ref[:, span] = (slope_ref[:, span].astype(F32) * t).astype(BF16)
            return comb

        comb = lax.fori_loop(0, hidden // width, block, jnp.zeros((every, lanes), F32))
        comb_c = jnp.sum(comb, axis=-1, keepdims=True)
        experts = router_ref.shape[0]
        ids = iota((every, experts), 1)
        pull = jnp.where(ids == place[0] // slices, comb_c * side_ref[:, 1:2], 0.0)
        pull = pull + jnp.where(ids.astype(F32) == side_ref[:, 3:4], comb_c * side_ref[:, 2:3], 0.0)
        if keep:
            acc_ref[...] = jnp.zeros_like(acc_ref)
            rest, routed = pull, jnp.zeros((experts, feat), F32)
            for _ in range(3):
                piece = rest.astype(BF16)
                rest = rest - piece.astype(F32)
                routed = routed + dot(piece, rows_ref[...], (0, 0))
            acc_ref[0:experts, :] = routed
        wide = min(FEAT_WIDTH, feat)
        for start in range(0, feat, wide):
            cols = slice(start, start + wide)
            term = dot(q_ref[...], up_ref[cols, :], (1, 1))
            for expert in range(experts):
                term = term + pull[:, expert : expert + 1] * router_ref[expert : expert + 1, cols]
            if keep:
                gained = jnp.sum(term * rows_ref[:, cols].astype(F32), axis=0, keepdims=True)
                acc_ref[experts : experts + 1, cols] = gained / gain_ref[:, cols]
            for index, part in enumerate(parts):
                part[:, cols] = term[index * slots : (index + 1) * slots, :].astype(BF16)


def owner_kernel(shards, stage, place, *refs):
    parts = refs[:shards]
    own_ref, x_ref, gain_ref, scatter_ref, gather_ref = refs[shards : shards + 5]
    own_out, sends = refs[shards + 5], refs[shards + 6 :]

    @pl.when(place[1] == place[2] - stage)
    def _():
        gh = dot(scatter_ref[0], parts[0][...], (1, 0))
        for step in range(1, shards):
            gh = gh + dot(scatter_ref[step], parts[step][...], (1, 0))
        x = x_ref[...].astype(F32)
        inverse = row_norm(x)
        normed = x * inverse
        scaled = gh * gain_ref[...]
        center = jnp.mean(scaled * normed, axis=-1, keepdims=True)
        gx = (own_ref[...].astype(F32) + inverse * (scaled - normed * center)).astype(BF16)
        own_out[...] = gx
        for step in range(1, shards):
            sends[step - 1][...] = dot(gather_ref[step], gx, (1, 0)).astype(BF16)


def weight_kernel(rows_ref, q_ref, cot_ref, side_ref, act_ref, up_ref, down_ref, turned, y_ref):
    @pl.when(pl.program_id(0) == 0)
    def _():
        turned[...] = rows_ref[...].astype(F32).T.astype(BF16)
        y_ref[...] = (side_ref[:, 0:1] * cot_ref[...].astype(F32)).astype(BF16)

    up_ref[...] = dot(turned[...], q_ref[...], (1, 0)).astype(BF16)
    down_ref[...] = dot(act_ref[...], y_ref[...], (0, 0)).astype(BF16)


def finish_kernel(shards, experts, *refs):
    total = refs[0][...]
    for ref in refs[1:shards]:
        total = total + ref[...]
    refs[shards][...] = total[0:experts, :]
    refs[shards + 1][...] = total[experts : experts + 1, :]


def body(
    layer_inputs, out_cotangent, expert_routes, norm_gain, router_weight, up_weight, down_weight
):
    sections = lax.axis_size("section")
    section_id = lax.axis_index("section")
    shards = lax.axis_size("expert")
    shard_id = lax.axis_index("expert")
    micro, rows, feat = layer_inputs.shape[1:]
    router = router_weight[0]
    experts = router.shape[0]
    up = up_weight[0]
    down = down_weight[0]
    hidden = up.shape[1]
    slices = shards // experts
    total = micro * rows
    cap = rows // BLOCK_ROWS * BLOCK_CAP if rows % BLOCK_ROWS == 0 else rows
    slots = micro * cap
    sent = slots + AUX
    last = sections - 1
    x = layer_inputs[0].reshape(total, feat)
    cot = out_cotangent.reshape(total, feat)
    chosen = lax.dynamic_slice_in_dim(expert_routes[0], shard_id * rows, rows, 1).reshape(total, 2)
    gain = norm_gain
    place = jnp.stack([shard_id, section_id, jnp.int32(last)]).astype(jnp.int32)
    steps = list(range(shards))
    split = max(1, shards // 2)
    width = min(1024, hidden)
    blocks = hidden // width

    def sds(shape, dtype=BF16):
        return jax.ShapeDtypeStruct(shape, dtype)

    def move(value, pairs):
        flat = [(sz * sections + ss, dz * sections + ds) for (ss, sz), (ds, dz) in pairs]
        return lax.ppermute(value, ("expert", "section"), flat)

    def spread(value, step, sources, drop):
        return move(
            value,
            [((s, z), (s - drop, (z + step) % shards)) for s in sources for z in range(shards) if s - drop >= 0],
        )

    def any_place():
        return pl.BlockSpec(memory_space=pl.ANY)

    everyone = list(range(sections))
    far = [pltpu.with_memory_space_constraint(array, pltpu.HBM) for array in (x, cot, gain, router, up, down)]
    hbm = pl.BlockSpec(memory_space=pltpu.HBM)
    prep = pl.pallas_call(
        functools.partial(prep_kernel, shards, slices, rows, slots, cap),
        out_shape=[sds((sent, feat))] * shards
        + [sds((sent + slots, feat))] * (shards - 1)
        + [sds((shards, slots, total)), sds((shards, total, slots)), sds((total, feat))],
        in_specs=[smem()] + [hbm] * 4 + [vmem()] * 2,
        out_specs=[vmem()] * (2 * shards + 2),
        scratch_shapes=[pltpu.VMEM((total, feat), BF16)] * 2
        + [pltpu.VMEM(gain.shape, F32), pltpu.VMEM(router.shape, F32), pltpu.SemaphoreType.DMA((4,))],
        compiler_params=params(),
        cost_estimate=cost(1e7, 4e6),
        name="prep",
    )(place, *far[:4], chosen, chosen.T)
    h_send, c_send = prep[:shards], [None] + list(prep[shards : 2 * shards - 1])
    gather, scatter, own = prep[2 * shards - 1 :]
    first_recv = [None] + [spread(c_send[step], step, [last], 0) for step in steps[1:]]
    gather_next = move(gather, [((s - 1, z), (s, z)) for s in everyone[1:] for z in range(shards)])
    every = shards * slots
    half = split * slots

    def forward(kernel, sources, extra, extra_specs, count, more, scratch):
        return list(
            pl.pallas_call(
                functools.partial(kernel, slots, width, len(sources)),
                out_shape=[sds((count, hidden))] * 2 + [sds((count, feat)), sds((count, SIDES), F32)] + more,
                in_specs=[smem()] + [vmem()] * len(sources) + extra_specs,
                out_specs=[vmem()] * (4 + len(more)),
                scratch_shapes=scratch,
                compiler_params=params(),
                cost_estimate=cost(2 * half * feat * hidden, 2 * feat * hidden),
            )(place, *sources, *extra)
        )

    outs = forward(
        first_kernel, [h_send[0]] + first_recv[1:split], far[4:], [hbm] * 2, half,
        [pltpu.VMEM(up.shape, BF16), pltpu.VMEM(down.shape, BF16)], [pltpu.SemaphoreType.DMA((blocks + 1,))],
    )
    near = [pltpu.with_memory_space_constraint(array, pltpu.VMEM) for array in outs[4:]]
    kept = outs[:4]
    flag_value = kept[3]
    if shards > split:
        extra = [gather_next] + kept + near[:1]
        kept = forward(second_kernel, first_recv[split:], extra, [any_place()] + [vmem()] * 5, every, [], [])

    def back(after, stage, recv, base, own_recv, own, prev):
        has_prev = prev is not None
        keep = stage == last
        args = [place, after] + ([own_recv, own] if has_prev else [own]) + [gather]
        args += [recv[step] for step in steps[1:]]
        args += [prev] * int(has_prev) + near + [kept[0], kept[1], kept[3], router]
        args += [kept[2], gain] * int(keep)
        outs = pl.pallas_call(
            functools.partial(back_kernel, shards, slices, slots, min(2 * width, hidden), base, stage, keep, has_prev),
            out_shape=([] if keep else [sds((total, feat))])
            + [sds((every, feat))]
            + ([sds((every, hidden)), sds((-(-(experts + 1) // 8) * 8, feat), F32)] if keep else [sds((slots, feat))] * shards),
            in_specs=[smem(), any_place()] + [vmem()] * (len(args) - 2),
            out_specs=[vmem()] * (3 if keep else 2 + shards),
            scratch_shapes=[] if keep else [pltpu.VMEM((every, hidden), BF16)],
            compiler_params=params(12 + every * feat * 8 // (1024 * 1024)),
            cost_estimate=cost(4 * every * feat * hidden, 4 * feat * hidden),
            name="back",
        )(*args)
        return list(outs)

    flag = move(flag_value, [((s, z), (s - 1, z)) for s in [last] for z in range(shards)])
    recv, base, own_recv, prev = first_recv, sent, None, None
    for stage in range(last):
        own, prev, *parts = back(flag, stage, recv, base, own_recv, own, prev)
        section = last - stage
        partial = [parts[0]]
        for step in steps[1:]:
            partial.append(spread(parts[step], -step, [section], 0))
        if stage == 0:
            later = lax.optimization_barrier((flag, *h_send[1:]))[1:]
            h_recv = [spread(value, step, everyone[:-1], 0) for step, value in zip(steps[1:], later)]
            kept = forward(third_kernel, [h_send[0]] + h_recv, kept + near[:1], [vmem()] * 5, every, [], [])
        outs = pl.pallas_call(
            functools.partial(owner_kernel, shards, stage),
            out_shape=[sds((total, feat))] + [sds((slots, feat))] * (shards - 1),
            in_specs=[smem()] + [vmem()] * (shards + 5),
            out_specs=[vmem()] * shards,
            compiler_params=params(),
            cost_estimate=cost(1e7, 4e6),
            name="owner",
        )(place, *partial, own, x, gain, scatter, gather_next)
        recv = [None]
        for step in steps[1:]:
            recv.append(spread(outs[step], step, [section], 1))
        own_recv = spread(outs[0], 0, [section], 1)
        base = 0
    cots, q, acc = back(flag, last, recv, base, own_recv, own, prev)
    sums = [acc] + [spread(acc, step, everyone, 0) for step in steps[1:]]
    whole = lambda array: pl.BlockSpec(array.shape, lambda i: (0,) * array.ndim)
    cut = min(GRAD_WIDTH, hidden)
    column = pl.BlockSpec((every, cut), lambda i: (0, i))
    up_grad, down_grad = pl.pallas_call(
        weight_kernel,
        grid=(hidden // cut,),
        out_shape=[sds((feat, hidden)), sds((hidden, feat))],
        in_specs=[whole(kept[2]), column, whole(cots), whole(kept[3]), column],
        out_specs=[pl.BlockSpec((feat, cut), lambda i: (0, i)), pl.BlockSpec((cut, feat), lambda i: (i, 0))],
        scratch_shapes=[pltpu.VMEM((feat, every), BF16), pltpu.VMEM((every, feat), BF16)],
        compiler_params=params(30),
        cost_estimate=cost(4 * every * feat * hidden, 4 * feat * hidden),
        name="weights",
    )(kept[2], q, cots, kept[3], kept[0])
    router_grad, gain_grad = pl.pallas_call(
        functools.partial(finish_kernel, shards, experts),
        out_shape=[sds((experts, feat), F32), sds((1, feat), F32)],
        in_specs=[vmem()] * shards,
        out_specs=[vmem()] * 2,
        compiler_params=params(),
        name="finish",
    )(*sums)
    return (up_grad[None], down_grad[None], router_grad[None], gain_grad)


def solution(mesh):
    in_specs = (
        P("section", None, ("groups", "expert"), None),
        P(None, ("groups", "expert"), None),
        P("section", None, "groups", None),
        P("section", None),
        P("section", None, None),
        P("section", None, "expert"),
        P("section", "expert", None),
    )
    out_specs = (
        P("section", "groups", "expert"),
        P("section", "expert", "groups"),
        P("section", "groups", None),
        P("section", "groups"),
    )
    return jax.shard_map(body, mesh=mesh, in_specs=in_specs, out_specs=out_specs, check_vma=False)
```

time: 172 us -> 162 us (0.942)
  waiting for transfers between devices: 92.9 us -> 78.9 us
  Pallas kernels: 39.8 us -> 42.1 us
  starting transfers between devices: 36.8 us -> 38.6 us
    ppermute x31 -> x32, waiting for transfers between devices: 92.9 us -> 78.9 us  [move(): return lax.ppermute(value, ('expert', 'section'), flat)]
    pallas_call x11, Pallas kernels: 36.3 us -> 38.5 us  [the longest x3 14.3 us: forward(): pl.pallas_call(functools.partial(kernel, slots, width, len(sources)), out...]
    ppermute x31 -> x32, starting transfers between devices: 36.8 us -> 38.6 us  [move(): return lax.ppermute(value, ('expert', 'section'), flat)]
  transfers between devices with their start and end apart: 31 -> 32, of which waited for: 4 -> 4; matrix products, arithmetic and copies ran while one was open for 0% -> 0% of each run, Pallas kernels for 12% -> 16%
where the time goes in v3:
time: 162 us
  waiting for transfers between devices  78.9 us (49%)
  Pallas kernels  42.1 us (26%)
  starting transfers between devices  38.6 us (24%)
    ppermute x32, waiting for transfers between devices, move(): return lax.ppermute(value, ('expert', 'section'), flat)  78.9 us
    ppermute x32, starting transfers between devices, move(): return lax.ppermute(value, ('expert', 'section'), flat)  38.6 us
    pallas_call x3, Pallas kernels, forward(): pl.pallas_call(functools.partial(kernel, slots, width, len(sources)), out...  14.3 us
    pallas_call x1, Pallas kernels, body(): pl.pallas_call(weight_kernel, grid=(hidden // cut,), out_shape=[sds((feat...  11.5 us
    pallas_call x4, Pallas kernels, back(): pl.pallas_call(functools.partial(back_kernel, shards, slices, slots, min(...  11 us
  transfers between devices with their start and end apart: 32, of which 4 were waited for; matrix products, arithmetic and copies ran while one was open for 0% of the time, Pallas kernels for 16%

profile of v3, /device:TPU:0, one launch (start us, length us, event | category | flops | bytes accessed | tf_op | source)
XLA Modules:
  0.0 161.8 jit_solution(9775886645169550893)
XLA Ops:
  0.6 0.0 copy-start
  0.7 0.7 copy-done
  1.3 0.1 constant_dynamic-slice_fusion
  1.4 0.1 reshape.17
  1.5 0.1 copy.12.col_ref
  1.6 0.1 pad_add_fusion.place
  1.7 3.0 %prep.1 = (bf16[88,1024]{1,0:T(8,128)(2,1)S(1)}, bf16[88,1024]{1,0:T(8,128)(2,1)S(1)}, bf16[88,1024]{1,0:T(8,128)(2,1)S(1)}, bf16[88,1024]{1,0:T(8,128)(2,1)S(1)...) custom-call(s32[3]{0:T(128)S(1)} %pad_add_fusion.place, ...), custom_call_target="tpu_custom_call" | custom-call | flops 10000000 | bytes 4000000 | tf_op jit(solution)/shard_map/prep/pallas_call | solution.py:379
  4.7 0.7 collective-permute-start
  5.4 0.7 collective-permute-start.5
  6.0 0.7 collective-permute-start.6
  6.7 2.4 %collective-permute-start.7 = (bf16[4,80,128]{2,1,0:T(8,128)(2,1)S(1)}, bf16[4,80,128]{2,1,0:T(8,128)(2,1)S(1)}, u32[]{:S(2)}, u32[]{:S(2)}) collective-permute-start(bf16[4,80,128]{2,1,0:T(8,128)(2,1)S(1)} %get-tuple-element.79.refs_1_.refs_2_), channel_id=1, source_target_pairs={{0,1},{4,5},{8,9},{12,13},{1,2},{5,6},{9,10},{13,14},{2,3},{6,7},{... | collective-permute-start | bytes 245768 | tf_op jit(solution)/shard_map/ppermute | solution.py:365
  9.1 0.0 collective-permute-done.refs_1_.refs_2_
  9.2 6.5 %shard_map.102 = (bf16[160,4096]{1,0:T(8,128)(2,1)S(1)}, bf16[160,4096]{1,0:T(8,128)(2,1)S(1)}, bf16[160,1024]{1,0:T(8,128)(2,1)S(1)}, f32[160,4]{1,0:T(8,128)S(...) custom-call(s32[3]{0:T(128)S(1)} %pad_add_fusion.place, ...), custom_call_target="tpu_custom_call" | custom-call | flops 1342177280 | bytes 8388608 | tf_op jit(solution)/shard_map/pallas_call | solution.py:401
  15.6 0.7 collective-permute-start.1
  16.3 0.0 collective-permute-done.5.refs_0_.refs_3_
  16.3 0.0 collective-permute-done.6.refs_1_.refs_4_
  16.3 0.0 copy-start.3
  16.4 0.6 shard_map.103
  16.9 0.0 collective-permute-done.1.after
  16.9 0.1 copy-done.3
  17.1 0.7 back.4
  17.8 0.7 collective-permute-start.8
  18.5 0.7 collective-permute-start.9
  19.2 0.7 collective-permute-start.10
  19.8 4.3 %collective-permute-start.2 = (bf16[88,1024]{1,0:T(8,128)(2,1)S(1)}, bf16[88,1024]{1,0:T(8,128)(2,1)S(1)}, u32[]{:S(2)}, u32[]{:S(2)}) collective-permute-start(bf16[88,1024]{1,0:T(8,128)(2,1)S(1)} %get-tuple-element.74), channel_id=1, source_target_pairs={{0,4},{4,8},{8,12},{12,0},{1,5},{5,9},{9,13},{13,1},{2,6},{6,10},{... | collective-permute-start | bytes 540680 | tf_op jit(solution)/shard_map/ppermute | solution.py:365
  24.1 4.5 %collective-permute-start.3 = (bf16[88,1024]{1,0:T(8,128)(2,1)S(1)}, bf16[88,1024]{1,0:T(8,128)(2,1)S(1)}, u32[]{:S(2)}, u32[]{:S(2)}) collective-permute-start(bf16[88,1024]{1,0:T(8,128)(2,1)S(1)} %get-tuple-element.75), channel_id=1, source_target_pairs={{0,8},{4,12},{8,0},{12,4},{1,9},{5,13},{9,1},{13,5},{2,10},{6,14},... | collective-permute-start | bytes 540680 | tf_op jit(solution)/shard_map/ppermute | solution.py:365
  28.7 3.3 %collective-permute-start.4 = (bf16[88,1024]{1,0:T(8,128)(2,1)S(1)}, bf16[88,1024]{1,0:T(8,128)(2,1)S(1)}, u32[]{:S(2)}, u32[]{:S(2)}) collective-permute-start(bf16[88,1024]{1,0:T(8,128)(2,1)S(1)} %get-tuple-element.76), channel_id=1, source_target_pairs={{0,12},{4,0},{8,4},{12,8},{1,13},{5,1},{9,5},{13,9},{2,14},{6,2},{... | collective-permute-start | bytes 540680 | tf_op jit(solution)/shard_map/ppermute | solution.py:365
  32.0 0.6 owner.3
  32.5 0.7 collective-permute-start.11
  33.2 0.7 collective-permute-start.12
  33.9 0.7 collective-permute-start.13
  34.6 4.8 %collective-permute-done.3.refs_2_ = bf16[88,1024]{1,0:T(8,128)(2,1)S(1)} collective-permute-done((bf16[88,1024]{1,0:T(8,128)(2,1)S(1)}, bf16[88,1024]{1,0:T(8,128)(2,1)S(1)}, u32[]{:S(2)}, u32[]{:S(2)}) %collective-permute-start.3) | collective-permute-done | bytes 180256 | tf_op jit(solution)/shard_map/ppermute | solution.py:365
  39.3 0.7 collective-permute-start.14
  40.0 1.5 collective-permute-done.4.refs_3_
  41.5 7.2 %shard_map.104 = (bf16[320,4096]{1,0:T(8,128)(2,1)S(1)}, bf16[320,4096]{1,0:T(8,128)(2,1)S(1)}, bf16[320,1024]{1,0:T(8,128)(2,1)S(1)}, f32[320,4]{1,0:T(8,128)S(1)}) custom-call(s32[3]{0:T(128)S(1)} %pad_add_fusion.place, bf16[88,1024]{1,0:T(8,128)(2,1)S(1)} %get-tuple-element.68.refs_0_, bf16[88,1024]{1,0:T(8,128)(2,1)S(1)} %collective-permute-done.2.refs_1_, ...), custom_call_target="tpu_custom_call" | custom-call | flops 1342177280 | bytes 8388608 | tf_op jit(solution)/shard_map/pallas_call | solution.py:401
  48.8 0.0 collective-permute-done.14.refs_5_
  48.8 0.0 collective-permute-done.11.refs_0_
  48.8 0.9 back.5
  49.7 0.7 collective-permute-start.15
  50.3 0.7 collective-permute-start.16
  51.0 0.7 collective-permute-start.17
  51.7 0.0 collective-permute-done.16.refs_2_
  51.7 0.6 owner.4
  52.3 0.7 collective-permute-start.18
  53.0 0.7 collective-permute-start.19
  53.7 0.7 collective-permute-start.20
  54.3 0.7 collective-permute-start.21
  55.1 0.9 back.6
  55.9 0.7 collective-permute-start.22
  56.6 0.7 collective-permute-start.23
  57.3 0.7 collective-permute-start.24
  58.0 0.6 owner.5
  58.6 1.3 collective-permute-start.25
  59.9 1.3 collective-permute-start.26
  61.2 1.3 collective-permute-start.27
  62.5 1.3 collective-permute-start.28
  63.8 69.2 %collective-permute-done.26.refs_3_ = bf16[80,1024]{1,0:T(8,128)(2,1)S(1)} collective-permute-done((bf16[80,1024]{1,0:T(8,128)(2,1)S(1)}, bf16[80,1024]{1,0:T(8,128)(2,1)S(1)}, u32[]{:S(2)}, u32[]{:S(2)}) %collective-permute-start.26) | collective-permute-done | bytes 163872 | tf_op jit(solution)/shard_map/ppermute | solution.py:365
  133.0 3.3 %collective-permute-done.27.refs_4_ = bf16[80,1024]{1,0:T(8,128)(2,1)S(1)} collective-permute-done((bf16[80,1024]{1,0:T(8,128)(2,1)S(1)}, bf16[80,1024]{1,0:T(8,128)(2,1)S(1)}, u32[]{:S(2)}, u32[]{:S(2)}) %collective-permute-start.27) | collective-permute-done | bytes 163872 | tf_op jit(solution)/shard_map/ppermute | solution.py:365
  136.3 8.6 %back.7 = (bf16[320,1024]{1,0:T(8,128)(2,1)S(1)}, bf16[320,4096]{1,0:T(8,128)(2,1)S(1)}, f32[8,1024]{1,0:T(8,128)S(1)}) custom-call(s32[3]{0:T(128)S(1)} %pad_add_fusion.place, f32[160,4]{1,0:T(8,128)S(1)} %collective-permute-done.1.after, bf16[128,1024]{1,0:T(8,128)(2,1)S(1)} %collective-permute-done.25.refs_0_, ...), custom_call_target="tpu_custom_call" | custom-call | flops 5368709120 | bytes 16777216 | tf_op jit(solution)/shard_map/back/pallas_call | solution.py:430
  144.9 2.4 %collective-permute-start.29 = (f32[8,1024]{1,0:T(8,128)S(1)}, f32[8,1024]{1,0:T(8,128)S(1)}, u32[]{:S(2)}, u32[]{:S(2)}) collective-permute-start(f32[8,1024]{1,0:T(8,128)S(1)} %get-tuple-element.129.refs_0_), channel_id=1, source_target_pairs={{0,4},{4,8},{8,12},{12,0},{1,5},{5,9},{9,13},{13,1},{2,6},{6,10},{... | collective-permute-start | bytes 98312 | tf_op jit(solution)/shard_map/ppermute | solution.py:365
  147.3 0.3 collective-permute-start.30
  147.6 2.1 %collective-permute-start.31 = (f32[8,1024]{1,0:T(8,128)S(1)}, f32[8,1024]{1,0:T(8,128)S(1)}, u32[]{:S(2)}, u32[]{:S(2)}) collective-permute-start(f32[8,1024]{1,0:T(8,128)S(1)} %get-tuple-element.129.refs_0_), channel_id=1, source_target_pairs={{0,12},{4,0},{8,4},{12,8},{1,13},{5,1},{9,5},{13,9},{2,14},{6,2},{... | collective-permute-start | bytes 98312 | tf_op jit(solution)/shard_map/ppermute | solution.py:365
  149.7 11.5 %weights.1 = (bf16[1024,4096]{1,0:T(8,128)(2,1)}, bf16[4096,1024]{1,0:T(8,128)(2,1)}) custom-call(bf16[320,1024]{1,0:T(8,128)(2,1)S(1)} %get-tuple-element.88.refs_13_.rows_ref, bf16[320,4096]{1,0:T(8,128)(2,1)S(1)} %get-tuple-element.125.q_ref, bf16[320,1024]{1,0:T(8,128)(2,1)S(1)} %get-tuple-element.126.cot_ref, ...), custom_call_target="tpu_custom_call" | custom-call | flops 5368709120 | bytes 16777216 | tf_op jit(solution)/shard_map/weights/pallas_call | solution.py:475
  161.2 0.6 finish.1
  (28 shorter events, 0.1 us)
Async XLA Ops:
  0.6 0.7 copy-start
  4.7 4.5 %collective-permute-start = (bf16[168,1024]{1,0:T(8,128)(2,1)S(1)}, bf16[168,1024]{1,0:T(8,128)(2,1)S(1)}, u32[]{:S(2)}, u32[]{:S(2)}) collective-permute-start(bf16[168,1024]{1,0:T(8,128)(2,1)S(1)} %get-tuple-element.69), channel_id=1, source_target_pairs={{3,7},{7,11},{11,15},{15,3},{19,23},{23,27},{27,31},{31,19}} | collective-permute-start | bytes 1032200 | tf_op jit(solution)/shard_map/ppermute | solution.py:365
  5.4 11.0 %collective-permute-start.5 = (bf16[168,1024]{1,0:T(8,128)(2,1)S(1)}, bf16[168,1024]{1,0:T(8,128)(2,1)S(1)}, u32[]{:S(2)}, u32[]{:S(2)}) collective-permute-start(bf16[168,1024]{1,0:T(8,128)(2,1)S(1)} %get-tuple-element.77), channel_id=1, source_target_pairs={{3,11},{7,15},{11,3},{15,7},{19,27},{23,31},{27,19},{31,23}} | collective-permute-start | bytes 1032200 | tf_op jit(solution)/shard_map/ppermute | solution.py:365
  6.0 10.3 %collective-permute-start.6 = (bf16[168,1024]{1,0:T(8,128)(2,1)S(1)}, bf16[168,1024]{1,0:T(8,128)(2,1)S(1)}, u32[]{:S(2)}, u32[]{:S(2)}) collective-permute-start(bf16[168,1024]{1,0:T(8,128)(2,1)S(1)} %get-tuple-element.78), channel_id=1, source_target_pairs={{3,15},{7,3},{11,7},{15,11},{19,31},{23,19},{27,23},{31,27}} | collective-permute-start | bytes 1032200 | tf_op jit(solution)/shard_map/ppermute | solution.py:365
  6.7 9.6 %collective-permute-start.7 = (bf16[4,80,128]{2,1,0:T(8,128)(2,1)S(1)}, bf16[4,80,128]{2,1,0:T(8,128)(2,1)S(1)}, u32[]{:S(2)}, u32[]{:S(2)}) collective-permute-start(bf16[4,80,128]{2,1,0:T(8,128)(2,1)S(1)} %get-tuple-element.79.refs_1_.refs_2_), channel_id=1, source_target_pairs={{0,1},{4,5},{8,9},{12,13},{1,2},{5,6},{9,10},{13,14},{2,3},{6,7},{... | collective-permute-start | bytes 245768 | tf_op jit(solution)/shard_map/ppermute | solution.py:365
  15.6 1.3 collective-permute-start.1
  16.3 0.7 copy-start.3
  17.1 14.9 %copy-start.2 = (bf16[1,2,64,1024]{3,2,1,0:T(8,128)(2,1)S(1)}, bf16[1,2,64,1024]{3,2,1,0:T(8,128)(2,1)}, u32[]{:S(2)}) copy-start(bf16[1,2,64,1024]{3,2,1,0:T(8,128)(2,1)} %param.7) | copy-start | bytes 786436
  17.1 14.9 %copy-start.4 = (f32[1,1024]{1,0:T(1,128)S(1)}, f32[1,1024]{1,0:T(1,128)}, u32[]{:S(2)}) copy-start(f32[1,1024]{1,0:T(1,128)} %refs_14_.1) | copy-start | bytes 12292
  17.8 10.9 %collective-permute-start.8 = (bf16[80,1024]{1,0:T(8,128)(2,1)S(1)}, bf16[80,1024]{1,0:T(8,128)(2,1)S(1)}, u32[]{:S(2)}, u32[]{:S(2)}) collective-permute-start(bf16[80,1024]{1,0:T(8,128)(2,1)S(1)} %get-tuple-element.92), channel_id=1, source_target_pairs={{3,15},{7,3},{11,7},{15,11},{19,31},{23,19},{27,23},{31,27}} | collective-permute-start | bytes 491528 | tf_op jit(solution)/shard_map/ppermute | solution.py:365
  18.5 13.5 %collective-permute-start.9 = (bf16[80,1024]{1,0:T(8,128)(2,1)S(1)}, bf16[80,1024]{1,0:T(8,128)(2,1)S(1)}, u32[]{:S(2)}, u32[]{:S(2)}) collective-permute-start(bf16[80,1024]{1,0:T(8,128)(2,1)S(1)} %get-tuple-element.93), channel_id=1, source_target_pairs={{3,11},{7,15},{11,3},{15,7},{19,27},{23,31},{27,19},{31,23}} | collective-permute-start | bytes 491528 | tf_op jit(solution)/shard_map/ppermute | solution.py:365
  19.2 12.8 %collective-permute-start.10 = (bf16[80,1024]{1,0:T(8,128)(2,1)S(1)}, bf16[80,1024]{1,0:T(8,128)(2,1)S(1)}, u32[]{:S(2)}, u32[]{:S(2)}) collective-permute-start(bf16[80,1024]{1,0:T(8,128)(2,1)S(1)} %get-tuple-element.94), channel_id=1, source_target_pairs={{3,7},{7,11},{11,15},{15,3},{19,23},{23,27},{27,31},{31,19}} | collective-permute-start | bytes 491528 | tf_op jit(solution)/shard_map/ppermute | solution.py:365
  19.8 14.1 %collective-permute-start.2 = (bf16[88,1024]{1,0:T(8,128)(2,1)S(1)}, bf16[88,1024]{1,0:T(8,128)(2,1)S(1)}, u32[]{:S(2)}, u32[]{:S(2)}) collective-permute-start(bf16[88,1024]{1,0:T(8,128)(2,1)S(1)} %get-tuple-element.74), channel_id=1, source_target_pairs={{0,4},{4,8},{8,12},{12,0},{1,5},{5,9},{9,13},{13,1},{2,6},{6,10},{... | collective-permute-start | bytes 540680 | tf_op jit(solution)/shard_map/ppermute | solution.py:365
  24.1 15.2 %collective-permute-start.3 = (bf16[88,1024]{1,0:T(8,128)(2,1)S(1)}, bf16[88,1024]{1,0:T(8,128)(2,1)S(1)}, u32[]{:S(2)}, u32[]{:S(2)}) collective-permute-start(bf16[88,1024]{1,0:T(8,128)(2,1)S(1)} %get-tuple-element.75), channel_id=1, source_target_pairs={{0,8},{4,12},{8,0},{12,4},{1,9},{5,13},{9,1},{13,5},{2,10},{6,14},... | collective-permute-start | bytes 540680 | tf_op jit(solution)/shard_map/ppermute | solution.py:365
  28.7 12.8 %collective-permute-start.4 = (bf16[88,1024]{1,0:T(8,128)(2,1)S(1)}, bf16[88,1024]{1,0:T(8,128)(2,1)S(1)}, u32[]{:S(2)}, u32[]{:S(2)}) collective-permute-start(bf16[88,1024]{1,0:T(8,128)(2,1)S(1)} %get-tuple-element.76), channel_id=1, source_target_pairs={{0,12},{4,0},{8,4},{12,8},{1,13},{5,1},{9,5},{13,9},{2,14},{6,2},{... | collective-permute-start | bytes 540680 | tf_op jit(solution)/shard_map/ppermute | solution.py:365
  32.5 16.3 %collective-permute-start.11 = (bf16[128,1024]{1,0:T(8,128)(2,1)S(1)}, bf16[128,1024]{1,0:T(8,128)(2,1)S(1)}, u32[]{:S(2)}, u32[]{:S(2)}) collective-permute-start(bf16[128,1024]{1,0:T(8,128)(2,1)S(1)} %get-tuple-element.97), channel_id=1, source_target_pairs={{3,2},{7,6},{11,10},{15,14},{19,18},{23,22},{27,26},{31,30}} | collective-permute-start | bytes 786440 | tf_op jit(solution)/shard_map/ppermute | solution.py:365
  33.2 15.5 %collective-permute-start.12 = (bf16[80,1024]{1,0:T(8,128)(2,1)S(1)}, bf16[80,1024]{1,0:T(8,128)(2,1)S(1)}, u32[]{:S(2)}, u32[]{:S(2)}) collective-permute-start(bf16[80,1024]{1,0:T(8,128)(2,1)S(1)} %get-tuple-element.98), channel_id=1, source_target_pairs={{3,6},{7,10},{11,14},{15,2},{19,22},{23,26},{27,30},{31,18}} | collective-permute-start | bytes 491528 | tf_op jit(solution)/shard_map/ppermute | solution.py:365
  33.9 14.9 %collective-permute-start.13 = (bf16[80,1024]{1,0:T(8,128)(2,1)S(1)}, bf16[80,1024]{1,0:T(8,128)(2,1)S(1)}, u32[]{:S(2)}, u32[]{:S(2)}) collective-permute-start(bf16[80,1024]{1,0:T(8,128)(2,1)S(1)} %get-tuple-element.99), channel_id=1, source_target_pairs={{3,10},{7,14},{11,2},{15,6},{19,26},{23,30},{27,18},{31,22}} | collective-permute-start | bytes 491528 | tf_op jit(solution)/shard_map/ppermute | solution.py:365
  39.3 9.4 %collective-permute-start.14 = (bf16[80,1024]{1,0:T(8,128)(2,1)S(1)}, bf16[80,1024]{1,0:T(8,128)(2,1)S(1)}, u32[]{:S(2)}, u32[]{:S(2)}) collective-permute-start(bf16[80,1024]{1,0:T(8,128)(2,1)S(1)} %get-tuple-element.100), channel_id=1, source_target_pairs={{3,14},{7,2},{11,6},{15,10},{19,30},{23,18},{27,22},{31,26}} | collective-permute-start | bytes 491528 | tf_op jit(solution)/shard_map/ppermute | solution.py:365
  49.7 2.0 %collective-permute-start.15 = (bf16[80,1024]{1,0:T(8,128)(2,1)S(1)}, bf16[80,1024]{1,0:T(8,128)(2,1)S(1)}, u32[]{:S(2)}, u32[]{:S(2)}) collective-permute-start(bf16[80,1024]{1,0:T(8,128)(2,1)S(1)} %get-tuple-element.106), channel_id=1, source_target_pairs={{2,14},{6,2},{10,6},{14,10},{18,30},{22,18},{26,22},{30,26}} | collective-permute-start | bytes 491528 | tf_op jit(solution)/shard_map/ppermute | solution.py:365
  50.3 1.4 collective-permute-start.16
  51.0 0.7 collective-permute-start.17
  52.3 2.8 %collective-permute-start.18 = (bf16[128,1024]{1,0:T(8,128)(2,1)S(1)}, bf16[128,1024]{1,0:T(8,128)(2,1)S(1)}, u32[]{:S(2)}, u32[]{:S(2)}) collective-permute-start(bf16[128,1024]{1,0:T(8,128)(2,1)S(1)} %get-tuple-element.110), channel_id=1, source_target_pairs={{2,1},{6,5},{10,9},{14,13},{18,17},{22,21},{26,25},{30,29}} | collective-permute-start | bytes 786440 | tf_op jit(solution)/shard_map/ppermute | solution.py:365
  53.0 2.0 %collective-permute-start.19 = (bf16[80,1024]{1,0:T(8,128)(2,1)S(1)}, bf16[80,1024]{1,0:T(8,128)(2,1)S(1)}, u32[]{:S(2)}, u32[]{:S(2)}) collective-permute-start(bf16[80,1024]{1,0:T(8,128)(2,1)S(1)} %get-tuple-element.111), channel_id=1, source_target_pairs={{2,5},{6,9},{10,13},{14,1},{18,21},{22,25},{26,29},{30,17}} | collective-permute-start | bytes 491528 | tf_op jit(solution)/shard_map/ppermute | solution.py:365
  53.7 1.4 collective-permute-start.20
  54.3 0.7 collective-permute-start.21
  55.9 2.0 %collective-permute-start.22 = (bf16[80,1024]{1,0:T(8,128)(2,1)S(1)}, bf16[80,1024]{1,0:T(8,128)(2,1)S(1)}, u32[]{:S(2)}, u32[]{:S(2)}) collective-permute-start(bf16[80,1024]{1,0:T(8,128)(2,1)S(1)} %get-tuple-element.116), channel_id=1, source_target_pairs={{1,13},{5,1},{9,5},{13,9},{17,29},{21,17},{25,21},{29,25}} | collective-permute-start | bytes 491528 | tf_op jit(solution)/shard_map/ppermute | solution.py:365
  56.6 1.4 collective-permute-start.23
  57.3 0.7 collective-permute-start.24
  58.6 77.7 %collective-permute-start.25 = (bf16[128,1024]{1,0:T(8,128)(2,1)S(1)}, bf16[128,1024]{1,0:T(8,128)(2,1)S(1)}, u32[]{:S(2)}, u32[]{:S(2)}) collective-permute-start(bf16[128,1024]{1,0:T(8,128)(2,1)S(1)} %get-tuple-element.120), channel_id=1, source_target_pairs={{1,0},{5,4},{9,8},{13,12},{17,16},{21,20},{25,24},{29,28}} | collective-permute-start | bytes 786440 | tf_op jit(solution)/shard_map/ppermute | solution.py:365
  59.9 73.1 %collective-permute-start.26 = (bf16[80,1024]{1,0:T(8,128)(2,1)S(1)}, bf16[80,1024]{1,0:T(8,128)(2,1)S(1)}, u32[]{:S(2)}, u32[]{:S(2)}) collective-permute-start(bf16[80,1024]{1,0:T(8,128)(2,1)S(1)} %get-tuple-element.121), channel_id=1, source_target_pairs={{1,4},{5,8},{9,12},{13,0},{17,20},{21,24},{25,28},{29,16}} | collective-permute-start | bytes 491528 | tf_op jit(solution)/shard_map/ppermute | solution.py:365
  61.2 75.1 %collective-permute-start.27 = (bf16[80,1024]{1,0:T(8,128)(2,1)S(1)}, bf16[80,1024]{1,0:T(8,128)(2,1)S(1)}, u32[]{:S(2)}, u32[]{:S(2)}) collective-permute-start(bf16[80,1024]{1,0:T(8,128)(2,1)S(1)} %get-tuple-element.122), channel_id=1, source_target_pairs={{1,8},{5,12},{9,0},{13,4},{17,24},{21,28},{25,16},{29,20}} | collective-permute-start | bytes 491528 | tf_op jit(solution)/shard_map/ppermute | solution.py:365
  62.5 73.8 %collective-permute-start.28 = (bf16[80,1024]{1,0:T(8,128)(2,1)S(1)}, bf16[80,1024]{1,0:T(8,128)(2,1)S(1)}, u32[]{:S(2)}, u32[]{:S(2)}) collective-permute-start(bf16[80,1024]{1,0:T(8,128)(2,1)S(1)} %get-tuple-element.123), channel_id=1, source_target_pairs={{1,12},{5,0},{9,4},{13,8},{17,28},{21,16},{25,20},{29,24}} | collective-permute-start | bytes 491528 | tf_op jit(solution)/shard_map/ppermute | solution.py:365
  144.9 16.3 %collective-permute-start.29 = (f32[8,1024]{1,0:T(8,128)S(1)}, f32[8,1024]{1,0:T(8,128)S(1)}, u32[]{:S(2)}, u32[]{:S(2)}) collective-permute-start(f32[8,1024]{1,0:T(8,128)S(1)} %get-tuple-element.129.refs_0_), channel_id=1, source_target_pairs={{0,4},{4,8},{8,12},{12,0},{1,5},{5,9},{9,13},{13,1},{2,6},{6,10},{... | collective-permute-start | bytes 98312 | tf_op jit(solution)/shard_map/ppermute | solution.py:365
  147.3 13.9 %collective-permute-start.30 = (f32[8,1024]{1,0:T(8,128)S(1)}, f32[8,1024]{1,0:T(8,128)S(1)}, u32[]{:S(2)}, u32[]{:S(2)}) collective-permute-start(f32[8,1024]{1,0:T(8,128)S(1)} %get-tuple-element.129.refs_0_), channel_id=1, source_target_pairs={{0,8},{4,12},{8,0},{12,4},{1,9},{5,13},{9,1},{13,5},{2,10},{6,14},... | collective-permute-start | bytes 98312 | tf_op jit(solution)/shard_map/ppermute | solution.py:365
  147.6 13.6 %collective-permute-start.31 = (f32[8,1024]{1,0:T(8,128)S(1)}, f32[8,1024]{1,0:T(8,128)S(1)}, u32[]{:S(2)}, u32[]{:S(2)}) collective-permute-start(f32[8,1024]{1,0:T(8,128)S(1)} %get-tuple-element.129.refs_0_), channel_id=1, source_target_pairs={{0,12},{4,0},{8,4},{12,8},{1,13},{5,1},{9,5},{13,9},{2,14},{6,2},{... | collective-permute-start | bytes 98312 | tf_op jit(solution)/shard_map/ppermute | solution.py:365
  149.7 12.1 %copy-start.1 = (s32[1,2,256,2]{2,3,1,0:T(2,128)S(1)}, s32[1,2,256,2]{2,3,1,0:T(2,128)}, u32[]{:S(2)}) copy-start(s32[1,2,256,2]{2,3,1,0:T(2,128)} %param.9) | copy-start | bytes 12292

commit v4 on v3

--- a/solution.py
+++ b/solution.py
@@ -17,7 +17,7 @@
 BF16 = jnp.bfloat16
 AUX = 8
 SIDES = 4
-FEAT_WIDTH = 512
+FEAT_WIDTH = 256
 GRAD_WIDTH = 1024
 
 
@@ -391,8 +391,9 @@
     )(place, *far[:4], chosen, chosen.T)
     h_send, c_send = prep[:shards], [None] + list(prep[shards : 2 * shards - 1])
     gather, scatter, own = prep[2 * shards - 1 :]
-    first_recv = [None] + [spread(c_send[step], step, [last], 0) for step in steps[1:]]
-    gather_next = move(gather, [((s - 1, z), (s, z)) for s in everyone[1:] for z in range(shards)])
+    first_recv = [None]
+    for step in steps[1:]:
+        first_recv.append(spread(c_send[step], step, [last], 0))
     every = shards * slots
     half = split * slots
 
@@ -416,6 +417,8 @@
     near = [pltpu.with_memory_space_constraint(array, pltpu.VMEM) for array in outs[4:]]
     kept = outs[:4]
     flag_value = kept[3]
+    gather_late = lax.optimization_barrier((gather, kept[3]))[0]
+    gather_next = move(gather_late, [((s - 1, z), (s, z)) for s in everyone[1:] for z in range(shards)])
     if shards > split:
         extra = [gather_next] + kept + near[:1]
         kept = forward(second_kernel, first_recv[split:], extra, [any_place()] + [vmem()] * 5, every, [], [])
@@ -451,7 +454,9 @@
             partial.append(spread(parts[step], -step, [section], 0))
         if stage == 0:
             later = lax.optimization_barrier((flag, *h_send[1:]))[1:]
-            h_recv = [spread(value, step, everyone[:-1], 0) for step, value in zip(steps[1:], later)]
+            h_recv = []
+            for step, value in zip(steps[1:], later):
+                h_recv.append(spread(value, step, everyone[:-1], 0))
             kept = forward(third_kernel, [h_send[0]] + h_recv, kept + near[:1], [vmem()] * 5, every, [], [])
         outs = pl.pallas_call(
             functools.partial(owner_kernel, shards, stage),

time: 162 us -> 163 us (level)
  transfers between devices with their start and end apart: 32 -> 32, of which waited for: 4 -> 5; matrix products, arithmetic and copies ran while one was open for 0% -> 0% of each run, Pallas kernels for 16% -> 16%
where the time goes in v4:
time: 163 us; the launch traced here: 162 us
  waiting for transfers between devices  79.2 us (49%)
  Pallas kernels  42.1 us (26%)
  starting transfers between devices  38.6 us (24%)
    ppermute x32, waiting for transfers between devices, move(): return lax.ppermute(value, ('expert', 'section'), flat)  79.2 us
    ppermute x32, starting transfers between devices, move(): return lax.ppermute(value, ('expert', 'section'), flat)  38.6 us
    pallas_call x3, Pallas kernels, forward(): pl.pallas_call(functools.partial(kernel, slots, width, len(sources)), out...  14.3 us
    pallas_call x1, Pallas kernels, body(): pl.pallas_call(weight_kernel, grid=(hidden // cut,), out_shape=[sds((feat...  11.5 us
    pallas_call x4, Pallas kernels, back(): pl.pallas_call(functools.partial(back_kernel, shards, slices, slots, min(...  11.1 us
  transfers between devices with their start and end apart: 32, of which 5 were waited for; matrix products, arithmetic and copies ran while one was open for 0% of the time, Pallas kernels for 16%

profile of v4, /device:TPU:0, one launch (start us, length us, event | category | flops | bytes accessed | tf_op | source)
XLA Modules:
  0.0 162.2 jit_solution(7189069250015372072)
XLA Ops:
  0.6 0.0 copy-start
  0.7 0.7 copy-done
  1.3 0.1 constant_dynamic-slice_fusion
  1.4 0.1 reshape.17
  1.5 0.1 copy.12.col_ref
  1.6 0.1 pad_add_fusion.place
  1.7 3.0 %prep.1 = (bf16[88,1024]{1,0:T(8,128)(2,1)S(1)}, bf16[88,1024]{1,0:T(8,128)(2,1)S(1)}, bf16[88,1024]{1,0:T(8,128)(2,1)S(1)}, bf16[88,1024]{1,0:T(8,128)(2,1)S(1)...) custom-call(s32[3]{0:T(128)S(1)} %pad_add_fusion.place, ...), custom_call_target="tpu_custom_call" | custom-call | flops 10000000 | bytes 4000000 | tf_op jit(solution)/shard_map/prep/pallas_call | solution.py:379
  4.7 0.7 collective-permute-start
  5.4 0.7 collective-permute-start.5
  6.0 0.7 collective-permute-start.6
  6.7 6.5 %shard_map.102 = (bf16[160,4096]{1,0:T(8,128)(2,1)S(1)}, bf16[160,4096]{1,0:T(8,128)(2,1)S(1)}, bf16[160,1024]{1,0:T(8,128)(2,1)S(1)}, f32[160,4]{1,0:T(8,128)S(...) custom-call(s32[3]{0:T(128)S(1)} %pad_add_fusion.place, ...), custom_call_target="tpu_custom_call" | custom-call | flops 1342177280 | bytes 8388608 | tf_op jit(solution)/shard_map/pallas_call | solution.py:402
  13.2 2.4 %collective-permute-start.7 = (bf16[4,80,128]{2,1,0:T(8,128)(2,1)S(1)}, bf16[4,80,128]{2,1,0:T(8,128)(2,1)S(1)}, u32[]{:S(2)}, u32[]{:S(2)}) collective-permute-start(bf16[4,80,128]{2,1,0:T(8,128)(2,1)S(1)} %get-tuple-element.81.refs_1_.refs_2_), channel_id=1, source_target_pairs={{0,1},{4,5},{8,9},{12,13},{1,2},{5,6},{9,10},{13,14},{2,3},{6,7},{... | collective-permute-start | bytes 245768 | tf_op jit(solution)/shard_map/ppermute | solution.py:365
  15.6 0.7 collective-permute-start.1
  16.3 0.0 collective-permute-done.6.refs_1_.refs_4_
  16.3 0.2 collective-permute-done.7.refs_2_.refs_8_
  16.5 0.5 shard_map.103
  17.1 0.0 collective-permute-done.1.after
  17.1 0.1 copy-done.3
  17.3 0.7 back.4
  18.0 0.7 collective-permute-start.8
  18.7 0.7 collective-permute-start.9
  19.3 0.7 collective-permute-start.10
  20.0 4.3 %collective-permute-start.2 = (bf16[88,1024]{1,0:T(8,128)(2,1)S(1)}, bf16[88,1024]{1,0:T(8,128)(2,1)S(1)}, u32[]{:S(2)}, u32[]{:S(2)}) collective-permute-start(bf16[88,1024]{1,0:T(8,128)(2,1)S(1)} %get-tuple-element.75), channel_id=1, source_target_pairs={{0,4},{4,8},{8,12},{12,0},{1,5},{5,9},{9,13},{13,1},{2,6},{6,10},{... | collective-permute-start | bytes 540680 | tf_op jit(solution)/shard_map/ppermute | solution.py:365
  24.3 4.5 %collective-permute-start.3 = (bf16[88,1024]{1,0:T(8,128)(2,1)S(1)}, bf16[88,1024]{1,0:T(8,128)(2,1)S(1)}, u32[]{:S(2)}, u32[]{:S(2)}) collective-permute-start(bf16[88,1024]{1,0:T(8,128)(2,1)S(1)} %get-tuple-element.76), channel_id=1, source_target_pairs={{0,8},{4,12},{8,0},{12,4},{1,9},{5,13},{9,1},{13,5},{2,10},{6,14},... | collective-permute-start | bytes 540680 | tf_op jit(solution)/shard_map/ppermute | solution.py:365
  28.9 3.3 %collective-permute-start.4 = (bf16[88,1024]{1,0:T(8,128)(2,1)S(1)}, bf16[88,1024]{1,0:T(8,128)(2,1)S(1)}, u32[]{:S(2)}, u32[]{:S(2)}) collective-permute-start(bf16[88,1024]{1,0:T(8,128)(2,1)S(1)} %get-tuple-element.77), channel_id=1, source_target_pairs={{0,12},{4,0},{8,4},{12,8},{1,13},{5,1},{9,5},{13,9},{2,14},{6,2},{... | collective-permute-start | bytes 540680 | tf_op jit(solution)/shard_map/ppermute | solution.py:365
  32.1 0.0 collective-permute-done.9.refs_2_
  32.2 0.6 owner.3
  32.7 0.7 collective-permute-start.11
  33.4 0.7 collective-permute-start.12
  34.1 0.7 collective-permute-start.13
  34.8 4.7 %collective-permute-done.3.refs_2_ = bf16[88,1024]{1,0:T(8,128)(2,1)S(1)} collective-permute-done((bf16[88,1024]{1,0:T(8,128)(2,1)S(1)}, bf16[88,1024]{1,0:T(8,128)(2,1)S(1)}, u32[]{:S(2)}, u32[]{:S(2)}) %collective-permute-start.3) | collective-permute-done | bytes 180256 | tf_op jit(solution)/shard_map/ppermute | solution.py:365
  39.5 0.7 collective-permute-start.14
  40.1 1.2 collective-permute-done.4.refs_3_
  41.3 7.2 %shard_map.104 = (bf16[320,4096]{1,0:T(8,128)(2,1)S(1)}, bf16[320,4096]{1,0:T(8,128)(2,1)S(1)}, bf16[320,1024]{1,0:T(8,128)(2,1)S(1)}, f32[320,4]{1,0:T(8,128)S(1)}) custom-call(s32[3]{0:T(128)S(1)} %pad_add_fusion.place, bf16[88,1024]{1,0:T(8,128)(2,1)S(1)} %get-tuple-element.69.refs_0_, bf16[88,1024]{1,0:T(8,128)(2,1)S(1)} %collective-permute-done.2.refs_1_, ...), custom_call_target="tpu_custom_call" | custom-call | flops 1342177280 | bytes 8388608 | tf_op jit(solution)/shard_map/pallas_call | solution.py:402
  48.6 0.0 collective-permute-done.14.refs_5_
  48.6 0.9 back.5
  49.5 0.7 collective-permute-start.15
  50.1 0.7 collective-permute-start.16
  50.8 0.7 collective-permute-start.17
  51.5 0.0 collective-permute-done.16.refs_2_
  51.5 0.6 owner.4
  52.1 0.7 collective-permute-start.18
  52.8 0.7 collective-permute-start.19
  53.5 0.7 collective-permute-start.20
  54.1 0.7 collective-permute-start.21
  54.8 0.0 collective-permute-done.19.refs_3_
  54.8 0.0 collective-permute-done.21.refs_5_
  54.9 0.9 back.6
  55.7 0.7 collective-permute-start.22
  56.4 0.7 collective-permute-start.23
  57.1 0.7 collective-permute-start.24
  57.8 0.6 owner.5
  58.4 1.3 collective-permute-start.25
  59.7 1.3 collective-permute-start.26
  61.0 1.3 collective-permute-start.27
  62.3 1.3 collective-permute-start.28
  63.6 69.7 %collective-permute-done.26.refs_3_ = bf16[80,1024]{1,0:T(8,128)(2,1)S(1)} collective-permute-done((bf16[80,1024]{1,0:T(8,128)(2,1)S(1)}, bf16[80,1024]{1,0:T(8,128)(2,1)S(1)}, u32[]{:S(2)}, u32[]{:S(2)}) %collective-permute-start.26) | collective-permute-done | bytes 163872 | tf_op jit(solution)/shard_map/ppermute | solution.py:365
  133.3 3.3 %collective-permute-done.27.refs_4_ = bf16[80,1024]{1,0:T(8,128)(2,1)S(1)} collective-permute-done((bf16[80,1024]{1,0:T(8,128)(2,1)S(1)}, bf16[80,1024]{1,0:T(8,128)(2,1)S(1)}, u32[]{:S(2)}, u32[]{:S(2)}) %collective-permute-start.27) | collective-permute-done | bytes 163872 | tf_op jit(solution)/shard_map/ppermute | solution.py:365
  136.7 8.6 %back.7 = (bf16[320,1024]{1,0:T(8,128)(2,1)S(1)}, bf16[320,4096]{1,0:T(8,128)(2,1)S(1)}, f32[8,1024]{1,0:T(8,128)S(1)}) custom-call(s32[3]{0:T(128)S(1)} %pad_add_fusion.place, f32[160,4]{1,0:T(8,128)S(1)} %collective-permute-done.1.after, bf16[128,1024]{1,0:T(8,128)(2,1)S(1)} %collective-permute-done.25.refs_0_, ...), custom_call_target="tpu_custom_call" | custom-call | flops 5368709120 | bytes 16777216 | tf_op jit(solution)/shard_map/back/pallas_call | solution.py:433
  145.3 2.4 %collective-permute-start.29 = (f32[8,1024]{1,0:T(8,128)S(1)}, f32[8,1024]{1,0:T(8,128)S(1)}, u32[]{:S(2)}, u32[]{:S(2)}) collective-permute-start(f32[8,1024]{1,0:T(8,128)S(1)} %get-tuple-element.131.refs_0_), channel_id=1, source_target_pairs={{0,4},{4,8},{8,12},{12,0},{1,5},{5,9},{9,13},{13,1},{2,6},{6,10},{... | collective-permute-start | bytes 98312 | tf_op jit(solution)/shard_map/ppermute | solution.py:365
  147.6 0.3 collective-permute-start.30
  148.0 2.1 %collective-permute-start.31 = (f32[8,1024]{1,0:T(8,128)S(1)}, f32[8,1024]{1,0:T(8,128)S(1)}, u32[]{:S(2)}, u32[]{:S(2)}) collective-permute-start(f32[8,1024]{1,0:T(8,128)S(1)} %get-tuple-element.131.refs_0_), channel_id=1, source_target_pairs={{0,12},{4,0},{8,4},{12,8},{1,13},{5,1},{9,5},{13,9},{2,14},{6,2},{... | collective-permute-start | bytes 98312 | tf_op jit(solution)/shard_map/ppermute | solution.py:365
  150.1 11.5 %weights.1 = (bf16[1024,4096]{1,0:T(8,128)(2,1)}, bf16[4096,1024]{1,0:T(8,128)(2,1)}) custom-call(bf16[320,1024]{1,0:T(8,128)(2,1)S(1)} %get-tuple-element.90.refs_13_.rows_ref, bf16[320,4096]{1,0:T(8,128)(2,1)S(1)} %get-tuple-element.127.q_ref, bf16[320,1024]{1,0:T(8,128)(2,1)S(1)} %get-tuple-element.128.cot_ref, ...), custom_call_target="tpu_custom_call" | custom-call | flops 5368709120 | bytes 16777216 | tf_op jit(solution)/shard_map/weights/pallas_call | solution.py:480
  161.6 0.6 finish.1
  (28 shorter events, 0.1 us)
Async XLA Ops:
  0.6 0.7 copy-start
  4.7 2.1 %collective-permute-start = (bf16[168,1024]{1,0:T(8,128)(2,1)S(1)}, bf16[168,1024]{1,0:T(8,128)(2,1)S(1)}, u32[]{:S(2)}, u32[]{:S(2)}) collective-permute-start(bf16[168,1024]{1,0:T(8,128)(2,1)S(1)} %get-tuple-element.70), channel_id=1, source_target_pairs={{3,7},{7,11},{11,15},{15,3},{19,23},{23,27},{27,31},{31,19}} | collective-permute-start | bytes 1032200 | tf_op jit(solution)/shard_map/ppermute | solution.py:365
  5.4 11.0 %collective-permute-start.5 = (bf16[168,1024]{1,0:T(8,128)(2,1)S(1)}, bf16[168,1024]{1,0:T(8,128)(2,1)S(1)}, u32[]{:S(2)}, u32[]{:S(2)}) collective-permute-start(bf16[168,1024]{1,0:T(8,128)(2,1)S(1)} %get-tuple-element.78), channel_id=1, source_target_pairs={{3,11},{7,15},{11,3},{15,7},{19,27},{23,31},{27,19},{31,23}} | collective-permute-start | bytes 1032200 | tf_op jit(solution)/shard_map/ppermute | solution.py:365
  6.0 10.3 %collective-permute-start.6 = (bf16[168,1024]{1,0:T(8,128)(2,1)S(1)}, bf16[168,1024]{1,0:T(8,128)(2,1)S(1)}, u32[]{:S(2)}, u32[]{:S(2)}) collective-permute-start(bf16[168,1024]{1,0:T(8,128)(2,1)S(1)} %get-tuple-element.79), channel_id=1, source_target_pairs={{3,15},{7,3},{11,7},{15,11},{19,31},{23,19},{27,23},{31,27}} | collective-permute-start | bytes 1032200 | tf_op jit(solution)/shard_map/ppermute | solution.py:365
  13.2 3.3 %collective-permute-start.7 = (bf16[4,80,128]{2,1,0:T(8,128)(2,1)S(1)}, bf16[4,80,128]{2,1,0:T(8,128)(2,1)S(1)}, u32[]{:S(2)}, u32[]{:S(2)}) collective-permute-start(bf16[4,80,128]{2,1,0:T(8,128)(2,1)S(1)} %get-tuple-element.81.refs_1_.refs_2_), channel_id=1, source_target_pairs={{0,1},{4,5},{8,9},{12,13},{1,2},{5,6},{9,10},{13,14},{2,3},{6,7},{... | collective-permute-start | bytes 245768 | tf_op jit(solution)/shard_map/ppermute | solution.py:365
  15.6 1.5 collective-permute-start.1
  16.5 0.7 copy-start.3
  17.3 14.9 %copy-start.2 = (bf16[1,2,64,1024]{3,2,1,0:T(8,128)(2,1)S(1)}, bf16[1,2,64,1024]{3,2,1,0:T(8,128)(2,1)}, u32[]{:S(2)}) copy-start(bf16[1,2,64,1024]{3,2,1,0:T(8,128)(2,1)} %param.7) | copy-start | bytes 786436
  17.3 14.9 %copy-start.4 = (f32[1,1024]{1,0:T(1,128)S(1)}, f32[1,1024]{1,0:T(1,128)}, u32[]{:S(2)}) copy-start(f32[1,1024]{1,0:T(1,128)} %refs_14_.1) | copy-start | bytes 12292
  18.0 10.9 %collective-permute-start.8 = (bf16[80,1024]{1,0:T(8,128)(2,1)S(1)}, bf16[80,1024]{1,0:T(8,128)(2,1)S(1)}, u32[]{:S(2)}, u32[]{:S(2)}) collective-permute-start(bf16[80,1024]{1,0:T(8,128)(2,1)S(1)} %get-tuple-element.94), channel_id=1, source_target_pairs={{3,15},{7,3},{11,7},{15,11},{19,31},{23,19},{27,23},{31,27}} | collective-permute-start | bytes 491528 | tf_op jit(solution)/shard_map/ppermute | solution.py:365
  18.7 13.5 %collective-permute-start.9 = (bf16[80,1024]{1,0:T(8,128)(2,1)S(1)}, bf16[80,1024]{1,0:T(8,128)(2,1)S(1)}, u32[]{:S(2)}, u32[]{:S(2)}) collective-permute-start(bf16[80,1024]{1,0:T(8,128)(2,1)S(1)} %get-tuple-element.95), channel_id=1, source_target_pairs={{3,11},{7,15},{11,3},{15,7},{19,27},{23,31},{27,19},{31,23}} | collective-permute-start | bytes 491528 | tf_op jit(solution)/shard_map/ppermute | solution.py:365
  19.3 12.8 %collective-permute-start.10 = (bf16[80,1024]{1,0:T(8,128)(2,1)S(1)}, bf16[80,1024]{1,0:T(8,128)(2,1)S(1)}, u32[]{:S(2)}, u32[]{:S(2)}) collective-permute-start(bf16[80,1024]{1,0:T(8,128)(2,1)S(1)} %get-tuple-element.96), channel_id=1, source_target_pairs={{3,7},{7,11},{11,15},{15,3},{19,23},{23,27},{27,31},{31,19}} | collective-permute-start | bytes 491528 | tf_op jit(solution)/shard_map/ppermute | solution.py:365
  20.0 14.1 %collective-permute-start.2 = (bf16[88,1024]{1,0:T(8,128)(2,1)S(1)}, bf16[88,1024]{1,0:T(8,128)(2,1)S(1)}, u32[]{:S(2)}, u32[]{:S(2)}) collective-permute-start(bf16[88,1024]{1,0:T(8,128)(2,1)S(1)} %get-tuple-element.75), channel_id=1, source_target_pairs={{0,4},{4,8},{8,12},{12,0},{1,5},{5,9},{9,13},{13,1},{2,6},{6,10},{... | collective-permute-start | bytes 540680 | tf_op jit(solution)/shard_map/ppermute | solution.py:365
  24.3 15.1 %collective-permute-start.3 = (bf16[88,1024]{1,0:T(8,128)(2,1)S(1)}, bf16[88,1024]{1,0:T(8,128)(2,1)S(1)}, u32[]{:S(2)}, u32[]{:S(2)}) collective-permute-start(bf16[88,1024]{1,0:T(8,128)(2,1)S(1)} %get-tuple-element.76), channel_id=1, source_target_pairs={{0,8},{4,12},{8,0},{12,4},{1,9},{5,13},{9,1},{13,5},{2,10},{6,14},... | collective-permute-start | bytes 540680 | tf_op jit(solution)/shard_map/ppermute | solution.py:365
  28.9 12.4 %collective-permute-start.4 = (bf16[88,1024]{1,0:T(8,128)(2,1)S(1)}, bf16[88,1024]{1,0:T(8,128)(2,1)S(1)}, u32[]{:S(2)}, u32[]{:S(2)}) collective-permute-start(bf16[88,1024]{1,0:T(8,128)(2,1)S(1)} %get-tuple-element.77), channel_id=1, source_target_pairs={{0,12},{4,0},{8,4},{12,8},{1,13},{5,1},{9,5},{13,9},{2,14},{6,2},{... | collective-permute-start | bytes 540680 | tf_op jit(solution)/shard_map/ppermute | solution.py:365
  32.7 15.9 %collective-permute-start.11 = (bf16[128,1024]{1,0:T(8,128)(2,1)S(1)}, bf16[128,1024]{1,0:T(8,128)(2,1)S(1)}, u32[]{:S(2)}, u32[]{:S(2)}) collective-permute-start(bf16[128,1024]{1,0:T(8,128)(2,1)S(1)} %get-tuple-element.99), channel_id=1, source_target_pairs={{3,2},{7,6},{11,10},{15,14},{19,18},{23,22},{27,26},{31,30}} | collective-permute-start | bytes 786440 | tf_op jit(solution)/shard_map/ppermute | solution.py:365
  33.4 15.1 %collective-permute-start.12 = (bf16[80,1024]{1,0:T(8,128)(2,1)S(1)}, bf16[80,1024]{1,0:T(8,128)(2,1)S(1)}, u32[]{:S(2)}, u32[]{:S(2)}) collective-permute-start(bf16[80,1024]{1,0:T(8,128)(2,1)S(1)} %get-tuple-element.100), channel_id=1, source_target_pairs={{3,6},{7,10},{11,14},{15,2},{19,22},{23,26},{27,30},{31,18}} | collective-permute-start | bytes 491528 | tf_op jit(solution)/shard_map/ppermute | solution.py:365
  34.1 14.5 %collective-permute-start.13 = (bf16[80,1024]{1,0:T(8,128)(2,1)S(1)}, bf16[80,1024]{1,0:T(8,128)(2,1)S(1)}, u32[]{:S(2)}, u32[]{:S(2)}) collective-permute-start(bf16[80,1024]{1,0:T(8,128)(2,1)S(1)} %get-tuple-element.101), channel_id=1, source_target_pairs={{3,10},{7,14},{11,2},{15,6},{19,26},{23,30},{27,18},{31,22}} | collective-permute-start | bytes 491528 | tf_op jit(solution)/shard_map/ppermute | solution.py:365
  39.5 9.1 %collective-permute-start.14 = (bf16[80,1024]{1,0:T(8,128)(2,1)S(1)}, bf16[80,1024]{1,0:T(8,128)(2,1)S(1)}, u32[]{:S(2)}, u32[]{:S(2)}) collective-permute-start(bf16[80,1024]{1,0:T(8,128)(2,1)S(1)} %get-tuple-element.102), channel_id=1, source_target_pairs={{3,14},{7,2},{11,6},{15,10},{19,30},{23,18},{27,22},{31,26}} | collective-permute-start | bytes 491528 | tf_op jit(solution)/shard_map/ppermute | solution.py:365
  49.5 2.0 %collective-permute-start.15 = (bf16[80,1024]{1,0:T(8,128)(2,1)S(1)}, bf16[80,1024]{1,0:T(8,128)(2,1)S(1)}, u32[]{:S(2)}, u32[]{:S(2)}) collective-permute-start(bf16[80,1024]{1,0:T(8,128)(2,1)S(1)} %get-tuple-element.108), channel_id=1, source_target_pairs={{2,14},{6,2},{10,6},{14,10},{18,30},{22,18},{26,22},{30,26}} | collective-permute-start | bytes 491528 | tf_op jit(solution)/shard_map/ppermute | solution.py:365
  50.1 1.4 collective-permute-start.16
  50.8 0.7 collective-permute-start.17
  52.1 2.8 %collective-permute-start.18 = (bf16[128,1024]{1,0:T(8,128)(2,1)S(1)}, bf16[128,1024]{1,0:T(8,128)(2,1)S(1)}, u32[]{:S(2)}, u32[]{:S(2)}) collective-permute-start(bf16[128,1024]{1,0:T(8,128)(2,1)S(1)} %get-tuple-element.112), channel_id=1, source_target_pairs={{2,1},{6,5},{10,9},{14,13},{18,17},{22,21},{26,25},{30,29}} | collective-permute-start | bytes 786440 | tf_op jit(solution)/shard_map/ppermute | solution.py:365
  52.8 2.0 %collective-permute-start.19 = (bf16[80,1024]{1,0:T(8,128)(2,1)S(1)}, bf16[80,1024]{1,0:T(8,128)(2,1)S(1)}, u32[]{:S(2)}, u32[]{:S(2)}) collective-permute-start(bf16[80,1024]{1,0:T(8,128)(2,1)S(1)} %get-tuple-element.113), channel_id=1, source_target_pairs={{2,5},{6,9},{10,13},{14,1},{18,21},{22,25},{26,29},{30,17}} | collective-permute-start | bytes 491528 | tf_op jit(solution)/shard_map/ppermute | solution.py:365
  53.5 1.4 collective-permute-start.20
  54.1 0.7 collective-permute-start.21
  55.7 2.0 %collective-permute-start.22 = (bf16[80,1024]{1,0:T(8,128)(2,1)S(1)}, bf16[80,1024]{1,0:T(8,128)(2,1)S(1)}, u32[]{:S(2)}, u32[]{:S(2)}) collective-permute-start(bf16[80,1024]{1,0:T(8,128)(2,1)S(1)} %get-tuple-element.118), channel_id=1, source_target_pairs={{1,13},{5,1},{9,5},{13,9},{17,29},{21,17},{25,21},{29,25}} | collective-permute-start | bytes 491528 | tf_op jit(solution)/shard_map/ppermute | solution.py:365
  56.4 1.4 collective-permute-start.23
  57.1 0.7 collective-permute-start.24
  58.4 78.3 %collective-permute-start.25 = (bf16[128,1024]{1,0:T(8,128)(2,1)S(1)}, bf16[128,1024]{1,0:T(8,128)(2,1)S(1)}, u32[]{:S(2)}, u32[]{:S(2)}) collective-permute-start(bf16[128,1024]{1,0:T(8,128)(2,1)S(1)} %get-tuple-element.122), channel_id=1, source_target_pairs={{1,0},{5,4},{9,8},{13,12},{17,16},{21,20},{25,24},{29,28}} | collective-permute-start | bytes 786440 | tf_op jit(solution)/shard_map/ppermute | solution.py:365
  59.7 73.6 %collective-permute-start.26 = (bf16[80,1024]{1,0:T(8,128)(2,1)S(1)}, bf16[80,1024]{1,0:T(8,128)(2,1)S(1)}, u32[]{:S(2)}, u32[]{:S(2)}) collective-permute-start(bf16[80,1024]{1,0:T(8,128)(2,1)S(1)} %get-tuple-element.123), channel_id=1, source_target_pairs={{1,4},{5,8},{9,12},{13,0},{17,20},{21,24},{25,28},{29,16}} | collective-permute-start | bytes 491528 | tf_op jit(solution)/shard_map/ppermute | solution.py:365
  61.0 75.7 %collective-permute-start.27 = (bf16[80,1024]{1,0:T(8,128)(2,1)S(1)}, bf16[80,1024]{1,0:T(8,128)(2,1)S(1)}, u32[]{:S(2)}, u32[]{:S(2)}) collective-permute-start(bf16[80,1024]{1,0:T(8,128)(2,1)S(1)} %get-tuple-element.124), channel_id=1, source_target_pairs={{1,8},{5,12},{9,0},{13,4},{17,24},{21,28},{25,16},{29,20}} | collective-permute-start | bytes 491528 | tf_op jit(solution)/shard_map/ppermute | solution.py:365
  62.3 74.4 %collective-permute-start.28 = (bf16[80,1024]{1,0:T(8,128)(2,1)S(1)}, bf16[80,1024]{1,0:T(8,128)(2,1)S(1)}, u32[]{:S(2)}, u32[]{:S(2)}) collective-permute-start(bf16[80,1024]{1,0:T(8,128)(2,1)S(1)} %get-tuple-element.125), channel_id=1, source_target_pairs={{1,12},{5,0},{9,4},{13,8},{17,28},{21,16},{25,20},{29,24}} | collective-permute-start | bytes 491528 | tf_op jit(solution)/shard_map/ppermute | solution.py:365
  145.3 16.3 %collective-permute-start.29 = (f32[8,1024]{1,0:T(8,128)S(1)}, f32[8,1024]{1,0:T(8,128)S(1)}, u32[]{:S(2)}, u32[]{:S(2)}) collective-permute-start(f32[8,1024]{1,0:T(8,128)S(1)} %get-tuple-element.131.refs_0_), channel_id=1, source_target_pairs={{0,4},{4,8},{8,12},{12,0},{1,5},{5,9},{9,13},{13,1},{2,6},{6,10},{... | collective-permute-start | bytes 98312 | tf_op jit(solution)/shard_map/ppermute | solution.py:365
  147.6 13.9 %collective-permute-start.30 = (f32[8,1024]{1,0:T(8,128)S(1)}, f32[8,1024]{1,0:T(8,128)S(1)}, u32[]{:S(2)}, u32[]{:S(2)}) collective-permute-start(f32[8,1024]{1,0:T(8,128)S(1)} %get-tuple-element.131.refs_0_), channel_id=1, source_target_pairs={{0,8},{4,12},{8,0},{12,4},{1,9},{5,13},{9,1},{13,5},{2,10},{6,14},... | collective-permute-start | bytes 98312 | tf_op jit(solution)/shard_map/ppermute | solution.py:365
  148.0 13.6 %collective-permute-start.31 = (f32[8,1024]{1,0:T(8,128)S(1)}, f32[8,1024]{1,0:T(8,128)S(1)}, u32[]{:S(2)}, u32[]{:S(2)}) collective-permute-start(f32[8,1024]{1,0:T(8,128)S(1)} %get-tuple-element.131.refs_0_), channel_id=1, source_target_pairs={{0,12},{4,0},{8,4},{12,8},{1,13},{5,1},{9,5},{13,9},{2,14},{6,2},{... | collective-permute-start | bytes 98312 | tf_op jit(solution)/shard_map/ppermute | solution.py:365
  150.1 12.1 %copy-start.1 = (s32[1,2,256,2]{2,3,1,0:T(2,128)S(1)}, s32[1,2,256,2]{2,3,1,0:T(2,128)}, u32[]{:S(2)}) copy-start(s32[1,2,256,2]{2,3,1,0:T(2,128)} %param.9) | copy-start | bytes 12292
